TPU v7x, 32 devices: a whole 2x2x4 slice. The times are simulated.
32 devices in a mesh: dp: 4 (over y, x), context: 2 (over core), expert: 4 (over z).
Axes of the slice: x: 2, y: 2, z: 4, core: 2. Of those that a mesh axis runs over, the one named last changes fastest.
Arguments:
- tokens: bfloat16 [16, 1024, 1536], P(('dp', 'expert'), 'context'), may hold values from -6 to 6
- cotangent: bfloat16 [16, 1024, 1536], P(('dp', 'expert'), 'context'), may hold values from -6 to 6
- segment_ids: int32 [16, 1024], P(('dp', 'expert')), may hold values from 0 to 5, never falling along the last dimension, each value on 1 to 512 neighbouring positions
- routes: int32 [16, 1024, 4], P(('dp', 'expert'), 'context'), may hold values from 0 to 7, all different within a row
- fill_rank: int32 [16, 2, 2048], P(('dp', 'expert'), 'context'), may hold values from 0 to 2047, each once within a row
- query_weight: bfloat16 [1536, 1536], P('context'), may hold values from -0.3125 to 0.3125
- key_projection_weight: bfloat16 [1536, 256], P('context'), may hold values from -0.15625 to 0.15625
- value_projection_weight: bfloat16 [1536, 256], P('context'), may hold values from -0.15625 to 0.15625
- output_weight: bfloat16 [1536, 1536], P('context'), may hold values from -0.625 to 0.625
- router_weight: bfloat16 [1536, 8], P('context'), may hold values from -0.078125 to 0.078125
- gain_attention: bfloat16 [1536], P('context'), may hold values from 0.5 to 1.5
- gain_experts: bfloat16 [1536], P('context'), may hold values from 0.5 to 1.5
- gate_weight: bfloat16 [8, 1536, 768], P('expert'), may hold values from -0.15625 to 0.15625
- up_weight: bfloat16 [8, 1536, 768], P('expert'), may hold values from -0.15625 to 0.15625
- down_weight: bfloat16 [8, 1536, 768], P('expert'), may hold values from -0.4375 to 0.4375
Outputs:
- layer_out: bfloat16 [16, 1024, 1536], P(('dp', 'expert'), 'context')
- grad_tokens: bfloat16 [16, 1024, 1536], P(('dp', 'expert'), 'context')
- query_grad: float32 [1536, 1536], P('context')
- key_grad: float32 [1536, 256], P('context')
- value_grad: float32 [1536, 256], P('context')
- output_grad: float32 [1536, 1536], P('context')
- router_grad: float32 [1536, 8], P('context')
- gain_attention_grad: float32 [1536], P('context')
- gain_experts_grad: float32 [1536], P('context')
- gate_grad: float32 [8, 1536, 768], P('expert', ('dp', 'context'))
- up_grad: float32 [8, 1536, 768], P('expert', ('dp', 'context'))
- down_grad: float32 [8, 1536, 768], P('expert', ('dp', 'context'))
Inputs may be any that keep to these rules, and one draw needn't show every extreme that they name: `segment_ids`: segment ids never fall along a sequence; each id covers 1 to 512 positions and some id covers exactly 512. `routes`: each token names 4 different experts. `fill_rank`: each device's row is a permutation of its 2048 pairs.
All inputs are finite; a program needn't handle non-finite values.
Results may differ from a plain program's by a relative error of at most 0.022.
Values may be sent and summed in bfloat16 or wider, within the bound.
A program may use at most 384 MiB of HBM per device.

v0:
```python
import math

import jax
import jax.numpy as jnp
from jax import lax
from jax.sharding import PartitionSpec as P

MODEL_WIDTH = 1536
QUERY_HEADS = 12
KEY_VALUE_HEADS = 2
HEAD_SIZE = 128
TOP = 4


norm_eps = 1e-06
rope_base = 10000.0
masked_fill_value = -1e30


def matmul(first_operand, second_operand):
    return jnp.dot(first_operand, second_operand, preferred_element_type=jnp.float32)


def matmul_nt(first_operand, second_operand):
    return lax.dot_general(
        first_operand, second_operand, (((1,), (1,)), ((), ())), preferred_element_type=jnp.float32
    )


def matmul_tn(first_operand, second_operand):
    return lax.dot_general(
        first_operand, second_operand, (((0,), (0,)), ((), ())), preferred_element_type=jnp.float32
    )


def precise_dims(first_operand, second_operand, contract_dims):
    return lax.dot_general(
        first_operand,
        second_operand,
        (contract_dims, ((), ())),
        precision=lax.Precision.HIGHEST,
        preferred_element_type=jnp.float32,
    )


def inverse_root(value_tensor):
    return lax.rsqrt(jnp.mean(value_tensor * value_tensor, axis=-1, keepdims=True) + norm_eps)


def norm_back(value_tensor, root_scale, gain_vector, upstream):
    scaled = upstream * gain_vector
    cubed = root_scale * root_scale * root_scale
    return root_scale * scaled - value_tensor * cubed * jnp.mean(
        value_tensor * scaled, axis=-1, keepdims=True
    )


def rope_tables(positions, head_width):
    half_width = head_width // 2
    frequency = jnp.exp(
        -(jnp.arange(half_width, dtype=jnp.float32) * (2.0 / head_width)) * math.log(rope_base)
    )
    angle = positions.astype(jnp.float32)[:, None] * frequency[None, :]
    return (jnp.cos(angle)[:, None, :], jnp.sin(angle)[:, None, :])


def apply_rotary(value_tensor, cosine_lookup, sine_lookup, direction):
    half_width = value_tensor.shape[-1] // 2
    first_half = value_tensor[..., :half_width]
    second_half = value_tensor[..., half_width:]
    return jnp.concatenate(
        [
            first_half * cosine_lookup - direction * second_half * sine_lookup,
            second_half * cosine_lookup + direction * first_half * sine_lookup,
        ],
        axis=-1,
    )


def block_slots(route_pairs, rank_pairs, expert_count):
    pair_count = route_pairs.shape[0]
    ordering = (
        jnp.zeros((pair_count,), jnp.int32)
        .at[rank_pairs]
        .set(jnp.arange(pair_count, dtype=jnp.int32))
    )
    ordered = route_pairs[ordering]
    onehot = (ordered[:, None] == jnp.arange(expert_count, dtype=jnp.int32)[None, :]).astype(
        jnp.int32
    )
    before = jnp.cumsum(onehot, axis=0) - onehot
    slot_ordered = jnp.sum(before * onehot, axis=1)
    return slot_ordered[rank_pairs]


def visible(query_pos, query_seg, key_pos, key_seg):
    return (key_pos[None, :] <= query_pos[:, None]) & (key_seg[None, :] == query_seg[:, None])


def heads_to_rows(value_tensor, token_rows, query_group_size):
    return (
        value_tensor.reshape(token_rows, KEY_VALUE_HEADS, query_group_size, HEAD_SIZE)
        .transpose(1, 2, 0, 3)
        .reshape(KEY_VALUE_HEADS, query_group_size * token_rows, HEAD_SIZE)
    )


def rows_to_heads(value_tensor, token_rows, query_group_size):
    return (
        value_tensor.reshape(KEY_VALUE_HEADS, query_group_size, token_rows, HEAD_SIZE)
        .transpose(2, 0, 1, 3)
        .reshape(token_rows, QUERY_HEADS, HEAD_SIZE)
    )


def body(
    tokens,
    cotangent,
    segment_ids,
    routes,
    fill_rank,
    query_weight,
    key_projection_weight,
    value_projection_weight,
    output_weight,
    router_weight,
    gain_attention,
    gain_experts,
    gate_weight,
    up_weight,
    down_weight,
):
    context_size = lax.axis_size("context")
    context_index = lax.axis_index("context")
    expert_size = lax.axis_size("expert")
    token_rows = tokens.shape[1]
    seq_length = segment_ids.shape[1]
    query_group_size = QUERY_HEADS // KEY_VALUE_HEADS
    count_of_rows = query_group_size * token_rows
    key_value_width = KEY_VALUE_HEADS * HEAD_SIZE
    score_scale = 1.0 / math.sqrt(HEAD_SIZE)
    query_full, key_full, value_full, output_full, router_full, gain_first, gain_second = (
        lax.all_gather(query_weight, "context", axis=0, tiled=True),
        lax.all_gather(key_projection_weight, "context", axis=0, tiled=True),
        lax.all_gather(value_projection_weight, "context", axis=0, tiled=True),
        lax.all_gather(output_weight, "context", axis=0, tiled=True),
        lax.all_gather(router_weight, "context", axis=0, tiled=True),
        lax.all_gather(gain_attention, "context", axis=0, tiled=True),
        lax.all_gather(gain_experts, "context", axis=0, tiled=True),
    )
    router_float = router_full.astype(jnp.float32)
    gain_first = gain_first.astype(jnp.float32)
    gain_second = gain_second.astype(jnp.float32)
    residual = tokens[0].astype(jnp.float32)
    root_first = inverse_root(residual)
    attn_input = (residual * root_first * gain_first).astype(jnp.bfloat16)
    query_unrotated = matmul(attn_input, query_full)
    key_unrotated = matmul(attn_input, key_full)
    value_rounded = matmul(attn_input, value_full).astype(jnp.bfloat16)
    positions = context_index * token_rows + jnp.arange(token_rows, dtype=jnp.int32)
    cosine_lookup, sine_lookup = rope_tables(positions, HEAD_SIZE)
    query_rotated = apply_rotary(
        query_unrotated.reshape(token_rows, QUERY_HEADS, HEAD_SIZE), cosine_lookup, sine_lookup, 1.0
    ).astype(jnp.bfloat16)
    key_rounded = (
        apply_rotary(
            key_unrotated.reshape(token_rows, KEY_VALUE_HEADS, HEAD_SIZE),
            cosine_lookup,
            sine_lookup,
            1.0,
        )
        .astype(jnp.bfloat16)
        .reshape(token_rows, key_value_width)
    )
    query_rows = heads_to_rows(query_rotated, token_rows, query_group_size)
    segments = segment_ids[0]
    query_pos = jnp.tile(positions, query_group_size)
    query_seg = jnp.tile(
        lax.dynamic_slice_in_dim(segments, context_index * token_rows, token_rows), query_group_size
    )
    per_block = 1
    limit_shards = max(1, 1024 // token_rows)
    while per_block * 2 <= limit_shards and context_size % (per_block * 2) == 0:
        per_block = per_block * 2
    rows_per_block = per_block * token_rows
    block_count = context_size // per_block
    block_starts = jnp.arange(block_count, dtype=jnp.int32) * rows_per_block

    def key_mask(piece_start, count_of_keys):
        key_pos = piece_start + jnp.arange(count_of_keys, dtype=jnp.int32)
        key_seg = lax.dynamic_slice_in_dim(segments, piece_start, count_of_keys)
        return visible(query_pos, query_seg, key_pos, key_seg)

    def score_block(key_section):
        count_of_keys = key_section.shape[0]
        key_row_matrix = key_section.reshape(count_of_keys, KEY_VALUE_HEADS, HEAD_SIZE)
        return (
            jnp.einsum(
                "hrd,nhd->hrn", query_rows, key_row_matrix, preferred_element_type=jnp.float32
            )
            * score_scale
        )

    key_section = lax.all_gather(key_rounded, "context", axis=0, tiled=True)
    allowed = key_mask(jnp.int32(0), key_section.shape[0])
    running_maximum_score = jnp.full(
        (KEY_VALUE_HEADS, count_of_rows), masked_fill_value, jnp.float32
    )
    scores = jnp.where(allowed[None], score_block(key_section), masked_fill_value)
    next_max = jnp.maximum(running_maximum_score, jnp.max(scores, axis=-1))
    weight_bundle = jnp.where(allowed[None], jnp.exp(scores - next_max[..., None]), 0.0)
    final_state = (next_max, jnp.sum(weight_bundle, axis=-1))
    key_whole, value_whole = (
        lax.all_gather(key_rounded, "context", axis=0, tiled=True),
        lax.all_gather(value_rounded, "context", axis=0, tiled=True),
    )
    running_maximum_score, running_sum = final_state
    logsum = running_maximum_score + jnp.log(running_sum)
    key_blocks = key_whole.reshape(block_count, rows_per_block, key_value_width)
    value_blocks = value_whole.reshape(block_count, rows_per_block, key_value_width)

    def value_step(values_acc, block_item):
        key_section, value_section, piece_start = block_item
        allowed = key_mask(piece_start, rows_per_block)
        normalized = jnp.where(
            allowed[None], jnp.exp(score_block(key_section) - logsum[..., None]), 0.0
        )
        value_row_matrix = value_section.reshape(rows_per_block, KEY_VALUE_HEADS, HEAD_SIZE)
        return (
            values_acc
            + jnp.einsum(
                "hrn,nhd->hrd",
                normalized.astype(jnp.bfloat16),
                value_row_matrix,
                preferred_element_type=jnp.float32,
            ),
            None,
        )

    mixed_rows, unused_values = lax.scan(
        value_step,
        jnp.zeros((KEY_VALUE_HEADS, count_of_rows, HEAD_SIZE), jnp.float32),
        (key_blocks, value_blocks, block_starts),
    )
    mixed_low = (
        rows_to_heads(mixed_rows, token_rows, query_group_size)
        .reshape(token_rows, QUERY_HEADS * HEAD_SIZE)
        .astype(jnp.bfloat16)
    )
    hidden = residual + matmul(mixed_low, output_full)
    root_second = inverse_root(hidden)
    normed_second = hidden * root_second * gain_second
    expert_input = normed_second.astype(jnp.bfloat16)
    logits = precise_dims(normed_second, router_float, ((1,), (0,)))
    expert_count = router_full.shape[1]
    local_experts = gate_weight.shape[0]
    route_rows = routes[0]
    route_onehot = (
        route_rows[:, :, None] == jnp.arange(expert_count, dtype=jnp.int32)[None, None, :]
    ).astype(jnp.float32)
    chosen_logits = jnp.sum(route_onehot * logits[:, None, :], axis=-1)
    gate_probs = jax.nn.softmax(chosen_logits, axis=-1)
    pair_count = token_rows * TOP
    capacity = 5 * token_rows * TOP // (4 * expert_count)
    route_pairs = route_rows.reshape(pair_count)
    slot_number = block_slots(route_pairs, fill_rank[0, 0], expert_count)
    pair_kept = slot_number < capacity
    flat_slot = jnp.where(pair_kept, route_pairs * capacity + slot_number, expert_count * capacity)
    slot_pair = (
        jnp.full((expert_count * capacity,), pair_count, jnp.int32)
        .at[flat_slot]
        .set(jnp.arange(pair_count, dtype=jnp.int32), mode="drop")
    )
    slot_valid = slot_pair < pair_count
    slot_clip = jnp.minimum(slot_pair, pair_count - 1)
    slot_token = slot_clip // TOP
    pair_slot = jnp.where(pair_kept, flat_slot, 0)
    kept_float = pair_kept.reshape(token_rows, TOP).astype(jnp.float32)
    kept_weight = gate_probs * kept_float
    send_rows = jnp.where(
        slot_valid[:, None], expert_input[slot_token], jnp.zeros((), jnp.bfloat16)
    )
    send_rows = send_rows.reshape(expert_size, local_experts, capacity, MODEL_WIDTH)
    received = lax.all_to_all(send_rows, "expert", split_axis=0, concat_axis=0, tiled=True)
    gate_pre = jnp.einsum(
        "secd,edf->secf", received, gate_weight, preferred_element_type=jnp.float32
    )
    up_pre = jnp.einsum("secd,edf->secf", received, up_weight, preferred_element_type=jnp.float32)
    hidden_low = (jax.nn.silu(gate_pre) * up_pre).astype(jnp.bfloat16)
    expert_out = jnp.einsum(
        "secf,edf->secd", hidden_low, down_weight, preferred_element_type=jnp.float32
    ).astype(jnp.bfloat16)
    returned = lax.all_to_all(expert_out, "expert", split_axis=0, concat_axis=0, tiled=True)
    returned, received, gate_pre, up_pre, hidden_low = (
        returned,
        received,
        gate_pre,
        up_pre,
        hidden_low,
    )
    returned_flat = returned.reshape(expert_count * capacity, MODEL_WIDTH)
    picked = returned_flat[pair_slot].reshape(token_rows, TOP, MODEL_WIDTH).astype(jnp.float32)
    mixture = jnp.sum(kept_weight[:, :, None] * picked, axis=1)
    layer_out = (hidden + mixture).astype(jnp.bfloat16)
    upstream = cotangent[0].astype(jnp.float32)
    slot_weight = jnp.where(slot_valid, kept_weight.reshape(pair_count)[slot_clip], 0.0)
    grad_send = (slot_weight[:, None] * upstream[slot_token]).astype(jnp.bfloat16)
    grad_send = grad_send.reshape(expert_size, local_experts, capacity, MODEL_WIDTH)
    grad_received = lax.all_to_all(grad_send, "expert", split_axis=0, concat_axis=0, tiled=True)
    hidden_grad = jnp.einsum(
        "secd,edf->secf", grad_received, down_weight, preferred_element_type=jnp.float32
    )
    sigmoid_gate = jax.nn.sigmoid(gate_pre)
    gate_grad_low = (
        hidden_grad * up_pre * sigmoid_gate * (1.0 + gate_pre * (1.0 - sigmoid_gate))
    ).astype(jnp.bfloat16)
    up_grad_low = (hidden_grad * gate_pre * sigmoid_gate).astype(jnp.bfloat16)
    input_grad = jnp.einsum(
        "secf,edf->secd", gate_grad_low, gate_weight, preferred_element_type=jnp.float32
    )
    input_grad = input_grad + jnp.einsum(
        "secf,edf->secd", up_grad_low, up_weight, preferred_element_type=jnp.float32
    )
    input_back = lax.all_to_all(
        input_grad.astype(jnp.bfloat16), "expert", split_axis=0, concat_axis=0, tiled=True
    )
    gate_sum = jnp.einsum(
        "secd,secf->edf", received, gate_grad_low, preferred_element_type=jnp.float32
    )
    up_sum = jnp.einsum("secd,secf->edf", received, up_grad_low, preferred_element_type=jnp.float32)
    down_sum = jnp.einsum(
        "secd,secf->edf", grad_received, hidden_low, preferred_element_type=jnp.float32
    )
    gate_grad, up_grad, down_grad = (
        lax.psum_scatter(gate_sum, ("dp", "context"), scatter_dimension=1, tiled=True),
        lax.psum_scatter(up_sum, ("dp", "context"), scatter_dimension=1, tiled=True),
        lax.psum_scatter(down_sum, ("dp", "context"), scatter_dimension=1, tiled=True),
    )
    gate_dot = jnp.sum(upstream[:, None, :] * picked, axis=-1) * kept_float
    chosen_grad = gate_probs * (gate_dot - jnp.sum(gate_probs * gate_dot, axis=-1, keepdims=True))
    logit_grad = jnp.sum(chosen_grad[:, :, None] * route_onehot, axis=1)
    back_flat = input_back.reshape(expert_count * capacity, MODEL_WIDTH)
    pair_back = back_flat[pair_slot].reshape(token_rows, TOP, MODEL_WIDTH).astype(jnp.float32)
    normed_grad = jnp.sum(kept_float[:, :, None] * pair_back, axis=1) + precise_dims(
        logit_grad, router_float, ((1,), (1,))
    )
    router_local = precise_dims(normed_second, logit_grad, ((0,), (0,)))
    hidden_total = upstream + norm_back(hidden, root_second, gain_second, normed_grad)
    gain_second_grad = jnp.sum(normed_grad * hidden * root_second, axis=0)
    attn_grad_low = hidden_total.astype(jnp.bfloat16)
    output_local = matmul_tn(mixed_low, attn_grad_low)
    mixed_grad_low = matmul_nt(attn_grad_low, output_full).astype(jnp.bfloat16)
    grad_rows = heads_to_rows(mixed_grad_low, token_rows, query_group_size)
    row_delta = jnp.sum(grad_rows.astype(jnp.float32) * mixed_rows, axis=-1)

    def backward_step(query_grad_acc, block_item):
        key_section, value_section, piece_start = block_item
        allowed = key_mask(piece_start, rows_per_block)
        key_row_matrix = key_section.reshape(rows_per_block, KEY_VALUE_HEADS, HEAD_SIZE)
        value_row_matrix = value_section.reshape(rows_per_block, KEY_VALUE_HEADS, HEAD_SIZE)
        normalized = jnp.where(
            allowed[None], jnp.exp(score_block(key_section) - logsum[..., None]), 0.0
        )
        value_block = jnp.einsum(
            "hrn,hrd->nhd",
            normalized.astype(jnp.bfloat16),
            grad_rows,
            preferred_element_type=jnp.float32,
        )
        prob_grad = jnp.einsum(
            "hrd,nhd->hrn", grad_rows, value_row_matrix, preferred_element_type=jnp.float32
        )
        score_grad = (normalized * (prob_grad - row_delta[..., None])).astype(jnp.bfloat16)
        grad_next = (
            query_grad_acc
            + jnp.einsum(
                "hrn,nhd->hrd", score_grad, key_row_matrix, preferred_element_type=jnp.float32
            )
            * score_scale
        )
        key_block = (
            jnp.einsum("hrn,hrd->nhd", score_grad, query_rows, preferred_element_type=jnp.float32)
            * score_scale
        )
        return (
            grad_next,
            (
                key_block.reshape(rows_per_block, key_value_width),
                value_block.reshape(rows_per_block, key_value_width),
            ),
        )

    query_grad_rows, block_grads = lax.scan(
        backward_step,
        jnp.zeros((KEY_VALUE_HEADS, count_of_rows, HEAD_SIZE), jnp.float32),
        (key_blocks, value_blocks, block_starts),
    )
    key_grad_all = block_grads[0].reshape(seq_length, key_value_width)
    value_grad_all = block_grads[1].reshape(seq_length, key_value_width)
    key_gradient_local, value_grad_own = (
        lax.psum_scatter(
            key_grad_all.astype(jnp.bfloat16), "context", scatter_dimension=0, tiled=True
        ).astype(jnp.float32),
        lax.psum_scatter(
            value_grad_all.astype(jnp.bfloat16), "context", scatter_dimension=0, tiled=True
        ).astype(jnp.float32),
    )
    query_grad_heads = rows_to_heads(query_grad_rows, token_rows, query_group_size)
    query_grad_low = (
        apply_rotary(query_grad_heads, cosine_lookup, sine_lookup, -1.0)
        .reshape(token_rows, QUERY_HEADS * HEAD_SIZE)
        .astype(jnp.bfloat16)
    )
    key_grad_low = (
        apply_rotary(
            key_gradient_local.reshape(token_rows, KEY_VALUE_HEADS, HEAD_SIZE),
            cosine_lookup,
            sine_lookup,
            -1.0,
        )
        .reshape(token_rows, key_value_width)
        .astype(jnp.bfloat16)
    )
    value_grad_low = value_grad_own.astype(jnp.bfloat16)
    input_total = (
        matmul_nt(query_grad_low, query_full)
        + matmul_nt(key_grad_low, key_full)
        + matmul_nt(value_grad_low, value_full)
    )
    query_local = matmul_tn(attn_input, query_grad_low)
    key_local = matmul_tn(attn_input, key_grad_low)
    value_local = matmul_tn(attn_input, value_grad_low)
    grad_tokens = (hidden_total + norm_back(residual, root_first, gain_first, input_total)).astype(
        jnp.bfloat16
    )
    gain_first_grad = jnp.sum(input_total * residual * root_first, axis=0)
    (
        query_part,
        key_part,
        value_part,
        output_part,
        router_part,
        gain_first_part,
        gain_second_part,
    ) = (
        lax.psum_scatter(
            query_local.astype(jnp.bfloat16), "context", scatter_dimension=0, tiled=True
        ).astype(jnp.float32),
        lax.psum_scatter(
            key_local.astype(jnp.bfloat16), "context", scatter_dimension=0, tiled=True
        ).astype(jnp.float32),
        lax.psum_scatter(
            value_local.astype(jnp.bfloat16), "context", scatter_dimension=0, tiled=True
        ).astype(jnp.float32),
        lax.psum_scatter(
            output_local.astype(jnp.bfloat16), "context", scatter_dimension=0, tiled=True
        ).astype(jnp.float32),
        lax.psum_scatter(
            router_local.astype(jnp.bfloat16), "context", scatter_dimension=0, tiled=True
        ).astype(jnp.float32),
        lax.psum_scatter(
            gain_first_grad.astype(jnp.bfloat16), "context", scatter_dimension=0, tiled=True
        ).astype(jnp.float32),
        lax.psum_scatter(
            gain_second_grad.astype(jnp.bfloat16), "context", scatter_dimension=0, tiled=True
        ).astype(jnp.float32),
    )
    (
        query_grad,
        key_grad,
        value_grad,
        output_grad,
        router_grad,
        gain_attention_grad,
        gain_experts_grad,
    ) = (
        lax.psum(query_part.astype(jnp.bfloat16), ("dp", "expert")).astype(jnp.float32),
        lax.psum(key_part.astype(jnp.bfloat16), ("dp", "expert")).astype(jnp.float32),
        lax.psum(value_part.astype(jnp.bfloat16), ("dp", "expert")).astype(jnp.float32),
        lax.psum(output_part.astype(jnp.bfloat16), ("dp", "expert")).astype(jnp.float32),
        lax.psum(router_part.astype(jnp.bfloat16), ("dp", "expert")).astype(jnp.float32),
        lax.psum(gain_first_part.astype(jnp.bfloat16), ("dp", "expert")).astype(jnp.float32),
        lax.psum(gain_second_part.astype(jnp.bfloat16), ("dp", "expert")).astype(jnp.float32),
    )
    return (
        layer_out[None],
        grad_tokens[None],
        query_grad,
        key_grad,
        value_grad,
        output_grad,
        router_grad,
        gain_attention_grad,
        gain_experts_grad,
        gate_grad,
        up_grad,
        down_grad,
    )


def solution(mesh):
    return jax.shard_map(
        body,
        mesh=mesh,
        in_specs=(
            P(("dp", "expert"), "context", None),
            P(("dp", "expert"), "context", None),
            P(("dp", "expert"), None),
            P(("dp", "expert"), "context", None),
            P(("dp", "expert"), "context", None),
            P("context", None),
            P("context", None),
            P("context", None),
            P("context", None),
            P("context", None),
            P("context"),
            P("context"),
            P("expert", None, None),
            P("expert", None, None),
            P("expert", None, None),
        ),
        out_specs=(
            P(("dp", "expert"), "context", None),
            P(("dp", "expert"), "context", None),
            P("context", None),
            P("context", None),
            P("context", None),
            P("context", None),
            P("context", None),
            P("context"),
            P("context"),
            P("expert", ("dp", "context"), None),
            P("expert", ("dp", "context"), None),
            P("expert", ("dp", "context"), None),
        ),
        check_vma=False,
    )
```

profile of v0, /device:TPU:0, one launch (start us, length us, event | category | flops | bytes accessed | tf_op | source)
XLA Modules:
  0.0 1579.7 jit_solution(3359882682857113302)
XLA Ops:
  15.5 8.0 scatter_custom_fusion
  27.2 11.8 gather_fusion
  41.9 11.8 gather_fusion.1
  54.4 8.1 scatter_custom_fusion.1
  78.5 4.2 fusion.1
  82.7 6.6 copy.133
  89.3 4.7 fusion.55
  97.8 13.3 select_reduce_fusion.1
  111.2 11.7 select_reduce_fusion
  122.9 15.4 fusion.93
  140.1 5.3 multiply_reduce_fusion.6
  150.4 13.6 gather_fusion.4
  164.2 9.6 gather_fusion.2
  173.8 6.9 broadcast_select_fusion
  180.7 6.2 all-to-all-start
  188.7 10.3 gather_fusion.5
  199.0 8.6 multiply_convert_fusion.1
  207.6 152.4 %all-to-all-done = bf16[4,2,320,1536]{3,2,1,0:T(8,128)(2,1)} async-done(((bf16[4,2,320,1536]{3,2,1,0:T(8,128)(2,1)}), bf16[4,2,320,1536]{3,2,1,0:T(8,128)(2,1)}, u32[]{:S(2)}, u32[]{:S(2)}) %all-to-all-start) | async-done | bytes 7864352 | tf_op jit(solution)/shard_map/all_to_all | solution.py:284
  360.0 5.9 all-to-all-start.2
  366.0 11.9 fusion.15
  377.8 11.8 fusion.17
  389.7 148.3 %all-to-all-done.2 = bf16[4,2,320,1536]{3,2,1,0:T(8,128)(2,1)} async-done(((bf16[4,2,320,1536]{3,2,1,0:T(8,128)(2,1)}), bf16[4,2,320,1536]{3,2,1,0:T(8,128)(2,1)}, u32[]{:S(2)}, u32[]{:S(2)}) %all-to-all-start.2) | async-done | bytes 7864352 | tf_op jit(solution)/shard_map/all_to_all | solution.py:309
  537.9 16.7 %fusion.7 = (bf16[4,2,320,768]{3,2,0,1:T(8,128)(2,1)}, bf16[4,2,320,768]{3,2,0,1:T(8,128)(2,1)}, bf16[4,2,320,768]{3,2,0,1:T(8,128)(2,1)S(1)}) fusion(f32[2,4,320,768]{3,2,1,0:T(8,128)} %fusion.17, f32[2,4,320,768]{3,2,1,0:T(8,128)} %fusion.15, bf16[2,1536,768]{2,1,0:T(8,128)(2,1)} %param.29, bf16[4,2,320,1536]{3,2,1,0:T(8,128)(2,1)} %all-to-all-done.2), kind=kOutput, calls=%fused_computation.28 | convolution fusion | flops 6071255040 | bytes 40108032 | tf_op jit(solution)/shard_map/secd,edf->secf/dot_general | solution.py:310
  554.7 12.2 convert_bitcast_fusion
  566.8 7.0 copy.146
  573.8 5.7 all-to-all-start.1
  579.5 12.6 fusion.21
  592.1 13.7 fusion.2
  605.8 6.9 copy.149
  612.7 138.2 %all-to-all-done.1 = bf16[4,2,320,1536]{3,2,1,0:T(8,128)(2,1)} async-done(((bf16[4,2,320,1536]{3,2,1,0:T(8,128)(2,1)}), bf16[4,2,320,1536]{3,2,1,0:T(8,128)(2,1)}, u32[]{:S(2)}, u32[]{:S(2)}) %all-to-all-start.1) | async-done | bytes 7864352 | tf_op jit(solution)/shard_map/all_to_all | solution.py:293
  750.9 5.5 all-to-all-start.3
  757.8 17.8 %gather_fusion.3 = bf16[2048,1536]{1,0:T(8,128)(2,1)} fusion(bf16[2560,1536]{1,0:T(8,128)(2,1)} %bitcast.35, s32[2048]{0:T(1024)S(1)} %broadcast_clamp_fusion), kind=kCustom, calls=%fused_computation.3 | custom fusion | bytes 12591104 | tf_op jit(solution)/shard_map/gather | solution.py:302
  775.6 12.2 reshape.656
  787.8 17.2 %multiply_reduce_fusion = (f32[512,4]{1,0:T(8,128)}, f32[512,1536]{1,0:T(8,128)}) fusion(f32[512,4,1536]{2,1,0:T(4,128)} %reshape.656, f32[512,1536]{1,0:T(8,128)S(1)} %bitcast_convert_fusion, f32[512,4]{1,0:T(8,128)} %copy.142), kind=kLoop, calls=%fused_computation.16 | loop fusion | flops 11794432 | bytes 18890752 | tf_op jit(solution)/shard_map/reduce_sum | solution.py:339
  806.1 121.6 %all-to-all-done.3 = bf16[4,2,320,1536]{3,2,1,0:T(8,128)(2,1)} async-done(((bf16[4,2,320,1536]{3,2,1,0:T(8,128)(2,1)}), bf16[4,2,320,1536]{3,2,1,0:T(8,128)(2,1)}, u32[]{:S(2)}, u32[]{:S(2)}) %all-to-all-start.3) | async-done | bytes 7864352 | tf_op jit(solution)/shard_map/all_to_all | solution.py:324
  927.7 17.5 %gather_fusion.6 = bf16[2048,1536]{1,0:T(8,128)(2,1)} fusion(bf16[2560,1536]{1,0:T(8,128)(2,1)} %bitcast.46, s32[2048]{0:T(1024)S(1)} %broadcast_clamp_fusion), kind=kCustom, calls=%fused_computation.6 | custom fusion | bytes 12591104 | tf_op jit(solution)/shard_map/gather | solution.py:343
  945.3 12.2 reshape.658
  957.5 32.8 %multiply_reduce_fusion.1 = f32[512,1536]{1,0:T(8,128)S(1)} fusion(f32[512,4,1536]{2,1,0:T(4,128)} %reshape.658, f32[512,4]{1,0:T(8,128)S(1)} %convert_element_type.283), kind=kLoop, calls=%fused_computation.17 | loop fusion | flops 5505024 | bytes 15736832 | tf_op jit(solution)/shard_map/reduce_sum | solution.py:344
  990.3 2.8 multiply_reduce_fusion.3
  997.0 3.7 convolution_convert_fusion.2
  1006.0 3.3 multiply_reduce_fusion.4
  1009.2 13.7 convolution_convert_fusion.5
  1023.0 18.7 %multiply_convert_fusion = bf16[2,3072,1024]{1,2,0:T(8,128)(2,1)} fusion(f32[2,3072,1024]{1,2,0:T(8,128)} %get-tuple-element.122, f32[2,3072]{1,0:T(2,128)S(1)} %multiply_reduce_fusion.4, f32[2,3072]{1,0:T(2,128)S(1)} %copy-done.55, pred[3072,1024]{0,1:T(8,128)(4,1)} %fusion.1, bf16[2,3072,128]{2,1,0:T(8,128)(2,1)} %bitcast.258, ...), kind=kOutput, calls=%fused_computation.9 | convolution fusion | flops 1648361472 | bytes 43040768 | tf_op jit(solution)/shard_map/while/body/eval_jaxpr/hrd,nhd->hrn/dot_general | solution.py:370
  1041.8 9.7 fusion.63
  1051.6 3.1 convolution_convert_fusion.3
  1054.8 3.5 reduce-scatter.11.cloned.1.call-done
  1060.2 3.1 convolution_convert_fusion.4
  1063.3 7.2 convolution_convert_fusion
  1070.8 11.3 convolution_multiply_fusion
  1082.1 3.6 copy.158
  1089.4 4.7 convolution_convert_fusion.1
  1099.3 16.8 %reduce-scatter.15.cloned.1.call-done = bf16[768,1536]{1,0:T(8,128)(2,1)} async-done(((bf16[1536,1536]{1,0:T(8,128)(2,1)}), bf16[768,1536]{1,0:T(8,128)(2,1)}) %reduce-scatter.15.cloned.1.call-update) | async-done | bytes 2359312 | tf_op jit(solution)/shard_map/reduce_scatter | solution.py:446
  1116.4 12.2 convolution_bitcast_fusion
  1128.7 12.2 convolution_bitcast_fusion.1
  1141.2 12.2 convolution_bitcast_fusion.2
  1155.3 4.7 fusion.94
  1161.8 2.9 fusion.44
  1167.3 78.6 %all-reduce.2 = (bf16[768,8]{0,1:T(8,128)(2,1)S(1)}, bf16[768]{0:T(1024)(128)(2,1)S(1)}, bf16[768]{0:T(1024)(128)(2,1)S(1)}) all-reduce(bf16[768,8]{0,1:T(8,128)(2,1)} %reduce-scatter.23.cloned.1.call-done, bf16[768]{0:T(1024)(128)(2,1)S(1)} %dynamic-slice.4, ...), channel_id=1, replica_groups=mesh['dp'=4,'context'=2,'expert'=4] {'dp','expert'}, use_global_device_ids=true, to_apply=%region_31.32 | all-reduce | flops 7680 | bytes 30720 | tf_op jit(solution)/shard_map/psum | solution.py:481
  1247.7 4.8 fusion.52
  1252.5 79.4 %all-reduce.7.cloned.1.call-done = (bf16[768,1536]{1,0:T(8,128)(2,1)}, bf16[768,256]{1,0:T(8,128)(2,1)}, bf16[768,256]{1,0:T(8,128)(2,1)}, bf16[768,1536]{1,0:T(8,128)(2,1)}) async-done(((bf16[768,1536]{1,0:T(8,128)(2,1)}, bf16[768,256]{1,0:T(8,128)(2,1)}, bf16[768,256]{1,0:T(8,128)(2,1)}, bf16[768,1536]{1,0:T(8,128)(2,1)}), (bf16[768,1536]{1,0:T(8,128)(2,1)}, bf16[768,256]{1,0:T(8,128)(2,1)}, ...) | async-done | bytes 5505040 | tf_op jit(solution)/shard_map/psum | solution.py:477
  1338.8 3.0 convert_element_type.313
  1341.8 69.8 %reduce-scatter.29.cloned.1.call-done = f32[2,192,768]{2,1,0:T(8,128)} async-done(((f32[2,1536,768]{2,1,0:T(8,128)}), f32[2,192,768]{2,1,0:T(8,128)}) %reduce-scatter.29.cloned.1.call-update) | async-done | bytes 1179664 | tf_op jit(solution)/shard_map/reduce_scatter | solution.py:337
  1411.6 80.4 %reduce-scatter.27.cloned.1.call-done = f32[2,192,768]{2,1,0:T(8,128)} async-done(((f32[2,1536,768]{2,1,0:T(8,128)}), f32[2,192,768]{2,1,0:T(8,128)}) %reduce-scatter.27.cloned.1.call-update) | async-done | bytes 1179664 | tf_op jit(solution)/shard_map/reduce_scatter | solution.py:336
  1492.0 80.6 %reduce-scatter.25.cloned.1.call-done = f32[2,192,768]{2,1,0:T(8,128)} async-done(((f32[2,1536,768]{2,1,0:T(8,128)}), f32[2,192,768]{2,1,0:T(8,128)}) %reduce-scatter.25.cloned.1.call-update) | async-done | bytes 1179664 | tf_op jit(solution)/shard_map/reduce_scatter | solution.py:335
  (281 shorter events, 81.4 us)
Async XLA Ops:
  7.2 3.8 copy-start.67
  7.2 6.4 copy-start.68
  7.2 8.2 copy-start.64
  7.2 16.9 %copy-start.60 = (s32[1,1024]{1,0:T(1,128)S(1)}, s32[1,1024]{1,0:T(1,128)}, u32[]{:S(2)}) copy-start(s32[1,1024]{1,0:T(1,128)} %param.17) | copy-start | bytes 12292
  7.2 17.5 %copy-start.59 = (bf16[768,8]{0,1:T(8,128)(2,1)S(1)}, bf16[768,8]{0,1:T(8,128)(2,1)}, u32[]{:S(2)}) copy-start(bf16[768,8]{0,1:T(8,128)(2,1)} %param.24) | copy-start | bytes 36868
  7.3 75.4 %all-gather.5.cloned.1.call-start = ((), (), s32[]{:S(2)}) async-start(), calls=%async_computation.14 | async-start | bytes 7077888 | tf_op jit(solution)/shard_map/all_gather | solution.py:143
  8.0 132.1 %all-gather.7.cloned.1.call-start = ((), (), s32[]{:S(2)}) async-start(), calls=%async_computation.15 | async-start | bytes 7077888 | tf_op jit(solution)/shard_map/all_gather | solution.py:146
  15.4 131.0 %copy-start.30 = (f32[1536]{0:T(1024)}, f32[1536]{0:T(1024)S(1)}, u32[]{:S(2)}) copy-start(f32[1536]{0:T(1024)S(1)} %reshape.742) | copy-start | bytes 18436
  41.9 21.1 %copy-start.28 = (bf16[768,256]{1,0:T(8,128)(2,1)S(1)}, bf16[768,256]{1,0:T(8,128)(2,1)}, u32[]{:S(2)}) copy-start(bf16[768,256]{1,0:T(8,128)(2,1)} %param.21) | copy-start | bytes 1179652
  41.9 23.5 %copy-start.29 = (bf16[768,256]{1,0:T(8,128)(2,1)S(1)}, bf16[768,256]{1,0:T(8,128)(2,1)}, u32[]{:S(2)}) copy-start(bf16[768,256]{1,0:T(8,128)(2,1)} %param.22) | copy-start | bytes 1179652
  65.4 6.2 copy-start.10
  67.8 5.0 copy-start.15
  67.8 5.0 copy-start.43
  67.8 5.0 copy-start.56
  72.8 5.7 copy-start.51
  72.8 5.7 copy-start.52
  72.8 5.7 copy-start.49
  72.8 5.7 copy-start.50
  72.8 5.7 copy-start.61
  75.9 18.1 %copy-start.13 = (f32[512,64]{0,1:T(8,128)}, f32[512,64]{0,1:T(8,128)S(1)}, u32[]{:S(2)}) copy-start(f32[512,64]{0,1:T(8,128)S(1)} %get-tuple-element.116) | copy-start | bytes 393220
  97.8 13.4 copy-start.2
  97.8 13.4 copy-start.9
  111.2 11.7 copy-start.25
  122.9 15.5 copy-start.54
  140.1 5.4 copy-start.19
  150.4 13.6 copy-start.38
  180.7 179.3 %all-to-all-start = ((bf16[4,2,320,1536]{3,2,1,0:T(8,128)(2,1)}), bf16[4,2,320,1536]{3,2,1,0:T(8,128)(2,1)}, u32[]{:S(2)}, u32[]{:S(2)}) async-start(bf16[4,2,320,1536]{3,2,1,0:T(8,128)(2,1)} %broadcast_select_fusion), calls=%async_computation | async-start | bytes 15728640 | tf_op jit(solution)/shard_map/all_to_all | solution.py:284
  360.0 177.9 %all-to-all-start.2 = ((bf16[4,2,320,1536]{3,2,1,0:T(8,128)(2,1)}), bf16[4,2,320,1536]{3,2,1,0:T(8,128)(2,1)}, u32[]{:S(2)}, u32[]{:S(2)}) async-start(bf16[4,2,320,1536]{3,2,1,0:T(8,128)(2,1)} %multiply_convert_fusion.1), calls=%async_computation.2 | async-start | bytes 15728640 | tf_op jit(solution)/shard_map/all_to_all | solution.py:309
  554.7 12.2 copy-start.71
  573.8 177.1 %all-to-all-start.1 = ((bf16[4,2,320,1536]{3,2,1,0:T(8,128)(2,1)}), bf16[4,2,320,1536]{3,2,1,0:T(8,128)(2,1)}, u32[]{:S(2)}, u32[]{:S(2)}) async-start(bf16[4,2,320,1536]{3,2,1,0:T(8,128)(2,1)} %copy.146), calls=%async_computation.1 | async-start | bytes 15728640 | tf_op jit(solution)/shard_map/all_to_all | solution.py:293
  612.7 143.7 %copy-start.53 = (s32[2048,1]{0,1:T(1,128)S(1)}, s32[2048,1]{0,1:T(1,128)}, u32[]{:S(2)}) copy-start(s32[2048,1]{0,1:T(1,128)} %get-tuple-element.110) | copy-start | bytes 24580
  612.7 143.8 %copy-start.65 = (pred[2048]{0:T(1024)(128)(4,1)S(1)}, pred[2048]{0:T(1024)(128)(4,1)}, u32[]{:S(2)}) copy-start(pred[2048]{0:T(1024)(128)(4,1)} %get-tuple-element.96) | copy-start | bytes 6148
  612.7 144.2 %copy-start.27 = (f32[512,4]{0,1:T(4,128)S(1)}, f32[512,4]{0,1:T(4,128)}, u32[]{:S(2)}) copy-start(f32[512,4]{0,1:T(4,128)} %copy-done.26) | copy-start | bytes 24580
  612.7 144.2 %copy-start.40 = (f32[512]{0:T(512)S(1)}, f32[512]{0:T(512)}, u32[]{:S(2)}) copy-start(f32[512]{0:T(512)} %copy-done.39) | copy-start | bytes 6148
  612.7 144.2 %copy-start.48 = (f32[512]{0:T(512)S(1)}, f32[512]{0:T(512)}, u32[]{:S(2)}) copy-start(f32[512]{0:T(512)} %copy-done.47) | copy-start | bytes 6148
  750.9 176.9 %all-to-all-start.3 = ((bf16[4,2,320,1536]{3,2,1,0:T(8,128)(2,1)}), bf16[4,2,320,1536]{3,2,1,0:T(8,128)(2,1)}, u32[]{:S(2)}, u32[]{:S(2)}) async-start(bf16[4,2,320,1536]{3,2,1,0:T(8,128)(2,1)} %copy.149), calls=%async_computation.3 | async-start | bytes 15728640 | tf_op jit(solution)/shard_map/all_to_all | solution.py:324
  756.4 295.2 %reduce-scatter.13.cloned.1.call-start = ((), (), s32[]{:S(2)}) async-start(), calls=%async_computation.17 | async-start | bytes 786432 | tf_op jit(solution)/shard_map/reduce_scatter | solution.py:404
  787.8 18.3 %copy-start.36 = (s32[1,512,4]{1,2,0:T(4,128)S(1)}, s32[1,512,4]{1,2,0:T(4,128)}, u32[]{:S(2)}) copy-start(s32[1,512,4]{1,2,0:T(4,128)} %param.18) | copy-start | bytes 24580
  957.4 32.8 %copy-start.1 = (f32[512,1536]{1,0:T(8,128)S(1)}, f32[512,1536]{1,0:T(8,128)}, u32[]{:S(2)}) copy-start(f32[512,1536]{1,0:T(8,128)} %copy-done) | copy-start | bytes 9437188
  957.4 32.8 %copy-start.31 = (f32[1536]{0:T(1024)S(1)}, f32[1536]{0:T(1024)}, u32[]{:S(2)}) copy-start(f32[1536]{0:T(1024)} %copy-done.30) | copy-start | bytes 18436
  957.4 32.8 %copy-start.34 = (bf16[1536,8]{0,1:T(8,128)(2,1)S(1)}, bf16[1536,8]{0,1:T(8,128)(2,1)}, u32[]{:S(2)}) copy-start(bf16[1536,8]{0,1:T(8,128)(2,1)} %all_gather.36) | copy-start | bytes 73732
  957.4 32.9 %copy-start.46 = (f32[512]{0:T(512)S(1)}, f32[512]{0:T(512)}, u32[]{:S(2)}) copy-start(f32[512]{0:T(512)} %copy-done.45) | copy-start | bytes 6148
  990.3 6.7 slice-start
  993.2 3.8 slice-start.1
  1023.0 35.3 %reduce-scatter.11.cloned.1.call-start = ((), (), s32[]{:S(2)}) async-start(), calls=%async_computation.16 | async-start | bytes 786432 | tf_op jit(solution)/shard_map/reduce_scatter | solution.py:401
  1023.0 18.8 %copy-start.3 = (bf16[2,6,512,128]{3,2,1,0:T(8,128)(2,1)S(1)}, bf16[2,6,512,128]{3,2,1,0:T(8,128)(2,1)}, u32[]{:S(2)}) copy-start(bf16[2,6,512,128]{3,2,1,0:T(8,128)(2,1)} %copy-done.2) | copy-start | bytes 4718596
  1041.8 9.8 copy-start.44
  1041.8 9.8 copy-start.57
  1051.5 7.8 copy-start.14
  1051.5 7.9 copy-start.22
  1051.5 45.3 %reduce-scatter.19.cloned.1.call-start = ((), (), s32[]{:S(2)}) async-start(), calls=%async_computation.20 | async-start | bytes 1179648 | tf_op jit(solution)/shard_map/reduce_scatter | solution.py:452
  1054.7 42.2 %reduce-scatter.17.cloned.1.call-start = ((), (), s32[]{:S(2)}) async-start(), calls=%async_computation.19 | async-start | bytes 1179648 | tf_op jit(solution)/shard_map/reduce_scatter | solution.py:449
  1063.3 36.0 %reduce-scatter.21.cloned.1.call-start = ((), (), s32[]{:S(2)}) async-start(), calls=%async_computation.21 | async-start | bytes 7077888 | tf_op jit(solution)/shard_map/reduce_scatter | solution.py:455
  1070.5 45.6 %reduce-scatter.15.cloned.1.call-start = ((), (), s32[]{:S(2)}) async-start(), calls=%async_computation.18 | async-start | bytes 7077888 | tf_op jit(solution)/shard_map/reduce_scatter | solution.py:446
  1085.7 3.8 copy-start.5
  1094.1 73.2 %reduce-scatter.23.cloned.1.call-start = ((), (), s32[]{:S(2)}) async-start(), calls=%async_computation.22 | async-start | bytes 36864 | tf_op jit(solution)/shard_map/reduce_scatter | solution.py:458
  1096.8 235.1 %all-reduce.7.cloned.1.call-start = ((), (), s32[]{:S(2)}) async-start(), calls=%async_computation.26 | async-start | bytes 11010048 | tf_op jit(solution)/shard_map/psum | solution.py:477
  1116.1 295.5 %reduce-scatter.29.cloned.1.call-start = ((), (), s32[]{:S(2)}) async-start(), calls=%async_computation.25 | async-start | bytes 10616832 | tf_op jit(solution)/shard_map/reduce_scatter | solution.py:337
  1128.6 363.4 %reduce-scatter.27.cloned.1.call-start = ((), (), s32[]{:S(2)}) async-start(), calls=%async_computation.24 | async-start | bytes 10616832 | tf_op jit(solution)/shard_map/reduce_scatter | solution.py:336
  1140.9 431.7 %reduce-scatter.25.cloned.1.call-start = ((), (), s32[]{:S(2)}) async-start(), calls=%async_computation.23 | async-start | bytes 10616832 | tf_op jit(solution)/shard_map/reduce_scatter | solution.py:335
  1155.3 4.8 copy-start.11
  1155.3 4.8 copy-start.24
  1161.8 85.9 %copy-start.66 = (f32[512]{0:T(512)S(1)}, f32[512]{0:T(512)}, u32[]{:S(2)}) copy-start(f32[512]{0:T(512)} %get-tuple-element.117) | copy-start | bytes 6148
  1331.9 4.0 copy-start.18
  (27 other events, 51.9 us)
Sparse Core Ops, SparseCore 0:
  9.6 17.1 all-gather.4
  28.4 15.6 all-gather.6
  1023.1 6.6 reduce-scatter.12
  1051.6 6.6 reduce-scatter.10
  1061.0 9.3 reduce-scatter.18
  1073.2 9.3 reduce-scatter.16
  1085.5 13.7 reduce-scatter.20
  1102.3 13.7 reduce-scatter.14
  1118.9 8.5 reduce-scatter.22
  1133.7 198.1 all-reduce.6
  1336.0 75.5 reduce-scatter.28
  1415.5 76.4 reduce-scatter.26
  1496.1 76.4 reduce-scatter.24
where the time goes:
time: 1590 us; the launch traced here: 1580 us
  waiting for transfers between devices  895 us (56%)
  matrix products  248 us (16%)
  local copies, waits for them, and re-layouts  180 us (11%)
  other arithmetic  120 us (8%)
  blocking collectives  96.2 us (6%)
  starting transfers between devices  24.6 us (2%)
  between operations  16.2 us (1%)
    all_to_all x1, waiting for transfers between devices, body(): lax.all_to_all(send_rows, 'expert', split_axis=0, concat_axis=0, tiled=True)  152 us
    all_to_all x1, waiting for transfers between devices, body(): lax.all_to_all(grad_send, 'expert', split_axis=0, concat_axis=0, tiled=True)  148 us
    all_to_all x1, waiting for transfers between devices, body(): lax.all_to_all(expert_out, 'expert', split_axis=0, concat_axis=0, tiled=T...  138 us
    all_to_all x1, waiting for transfers between devices, body(): lax.all_to_all(input_grad.astype(jnp.bfloat16), 'expert', split_axis=0, c...  122 us
    reduce_scatter x1, waiting for transfers between devices, body(): lax.psum_scatter(gate_sum, ('dp', 'context'), scatter_dimension=1, tiled=...  80.6 us
    reduce_scatter x1, waiting for transfers between devices, body(): lax.psum_scatter(up_sum, ('dp', 'context'), scatter_dimension=1, tiled=True)  80.4 us
    psum x1, waiting for transfers between devices, body(): lax.psum(query_part.astype(jnp.bfloat16), ('dp', 'expert'))  79.4 us
    psum x1, blocking collectives, body(): lax.psum(router_part.astype(jnp.bfloat16), ('dp', 'expert'))  78.6 us
  transfers between devices with their start and end apart: 17, of which 11 were waited for; matrix products, arithmetic and copies ran while one was open for 24% of the time, Pallas kernels for 0%

commit v1 on v0

v1 whole, which is shorter than its diff:
```python
import functools
import math

import jax
import jax.numpy as jnp
from jax import lax
from jax.experimental import pallas as pl
from jax.experimental.pallas import tpu as pltpu
from jax.sharding import PartitionSpec as P

MODEL_WIDTH = 1536
QUERY_HEADS = 12
KEY_VALUE_HEADS = 2
HEAD_SIZE = 128
TOP = 4
GROUP = QUERY_HEADS // KEY_VALUE_HEADS
norm_eps = 1e-06
rope_base = 10000.0
NEG = -1e30
SCALE = 1.0 / math.sqrt(HEAD_SIZE)
BF = jnp.bfloat16
F32 = jnp.float32
VMEM_LIMIT = 60 * 1024 * 1024


def mm(a, b):
    return jnp.dot(a, b, preferred_element_type=F32)


def mm_nt(a, b):
    return lax.dot_general(a, b, (((1,), (1,)), ((), ())), preferred_element_type=F32)


def mm_tn(a, b):
    return lax.dot_general(a, b, (((0,), (0,)), ((), ())), preferred_element_type=F32)


def precise_dims(a, b, dims):
    return lax.dot_general(
        a, b, (dims, ((), ())), precision=lax.Precision.HIGHEST, preferred_element_type=F32
    )


def inverse_root(v):
    return lax.rsqrt(jnp.mean(v * v, axis=-1, keepdims=True) + norm_eps)


def norm_back(v, root, gain, upstream):
    scaled = upstream * gain
    cubed = root * root * root
    return root * scaled - v * cubed * jnp.mean(v * scaled, axis=-1, keepdims=True)


def rope_tables(positions):
    half = HEAD_SIZE // 2
    frequency = jnp.exp(
        -(jnp.arange(half, dtype=F32) * (2.0 / HEAD_SIZE)) * math.log(rope_base)
    )
    angle = positions.astype(F32)[:, None] * frequency[None, :]
    return jnp.cos(angle), jnp.sin(angle)


def apply_rotary(v, cosine, sine, direction):
    half = HEAD_SIZE // 2
    a, b = v[..., :half], v[..., half:]
    c, s = cosine[:, None, :], sine[:, None, :]
    return jnp.concatenate([a * c - direction * b * s, b * c + direction * a * s], axis=-1)


def fold_rows(v, op):
    rows, cols = v.shape
    return op(v.reshape(rows // 8, 8, cols), axis=0)


def make_bias(ctx, tokens, segk_ref, segq_ref, bias_ref):
    length = segk_ref.shape[0]
    key_pos = lax.broadcasted_iota(jnp.int32, (length, tokens), 0)
    query_pos = lax.broadcasted_iota(jnp.int32, (length, tokens), 1) + ctx * tokens
    same = segk_ref[...] == segq_ref[...]
    bias_ref[...] = jnp.where(same & (key_pos <= query_pos), 0.0, NEG)


def attn_fwd_kernel(kb, tq, meta, q_ref, k_ref, v_ref, segk_ref, segq_ref, o_ref, lse_ref,
                    bias_ref, s_ref, vt_ref):
    head = pl.program_id(0)
    tokens = q_ref.shape[0]

    @pl.when(head == 0)
    def _():
        make_bias(meta[0], tokens, segk_ref, segq_ref, bias_ref)

    @pl.when(lax.rem(head, GROUP) == 0)
    def _():
        vt_ref[...] = v_ref[...].astype(F32).T.astype(BF)

    for part in range(tokens // tq):
        cols = pl.ds(part * tq, tq)
        q = q_ref[cols, :]
        low, high = meta[1 + 2 * part], meta[2 + 2 * part]

        def score(i, top):
            rows = pl.ds(pl.multiple_of(i * kb, kb), kb)
            s = mm_nt(k_ref[rows, :], q) * SCALE + bias_ref[rows, cols]
            s_ref[rows, :] = s
            return jnp.maximum(top, fold_rows(s, jnp.max))

        top = lax.fori_loop(low, high, score, jnp.full((8, tq), NEG, F32))
        top = jnp.max(top, axis=0, keepdims=True)

        def value(i, carry):
            total, out = carry
            rows = pl.ds(pl.multiple_of(i * kb, kb), kb)
            p = jnp.exp(s_ref[rows, :] - top)
            total = total + fold_rows(p, jnp.sum)
            return total, out + mm(vt_ref[:, rows], p.astype(BF))

        total, out = lax.fori_loop(
            low, high, value, (jnp.zeros((8, tq), F32), jnp.zeros((HEAD_SIZE, tq), F32))
        )
        total = jnp.sum(total, axis=0, keepdims=True)
        o_ref[cols, :] = (out / total).T.astype(BF)
        lse_ref[0, :, cols] = top + jnp.log(total)


def attn_bwd_kernel(kb, tq, meta, q_ref, k_ref, v_ref, do_ref, lse_ref, cos_ref, sin_ref,
                    segk_ref, segq_ref, dq_ref, dk_ref, dv_ref,
                    bias_ref, p_ref, dp_ref, kt_ref, dk_acc, dv_acc):
    head = pl.program_id(0)
    tokens = q_ref.shape[0]

    @pl.when(head == 0)
    def _():
        make_bias(meta[0], tokens, segk_ref, segq_ref, bias_ref)

    @pl.when(lax.rem(head, GROUP) == 0)
    def _():
        kt_ref[...] = k_ref[...].astype(F32).T.astype(BF)
        dk_acc[...] = jnp.zeros_like(dk_acc)
        dv_acc[...] = jnp.zeros_like(dv_acc)

    for part in range(tokens // tq):
        cols = pl.ds(part * tq, tq)
        q = q_ref[cols, :]
        do = do_ref[cols, :]
        lse = lse_ref[0, :, cols]
        low, high = meta[1 + 2 * part], meta[2 + 2 * part]

        def score(i, delta):
            rows = pl.ds(pl.multiple_of(i * kb, kb), kb)
            s = mm_nt(k_ref[rows, :], q) * SCALE + bias_ref[rows, cols]
            p = jnp.exp(s - lse)
            dp = mm_nt(v_ref[rows, :], do)
            p_ref[rows, :] = p
            dp_ref[rows, :] = dp
            return delta + fold_rows(p * dp, jnp.sum)

        delta = lax.fori_loop(low, high, score, jnp.zeros((8, tq), F32))
        delta = jnp.sum(delta, axis=0, keepdims=True)

        def grads(i, dq):
            rows = pl.ds(pl.multiple_of(i * kb, kb), kb)
            p = p_ref[rows, :]
            ds = (p * (dp_ref[rows, :] - delta)).astype(BF)
            dv_acc[rows, :] += mm(p.astype(BF), do)
            dk_acc[rows, :] += mm(ds, q)
            return dq + mm(kt_ref[:, rows], ds)

        dq = lax.fori_loop(low, high, grads, jnp.zeros((HEAD_SIZE, tq), F32))
        dq = dq.T * SCALE
        turned = pltpu.roll(dq, HEAD_SIZE // 2, 1)
        dq_ref[cols, :] = (dq * cos_ref[cols, :] - turned * sin_ref[cols, :]).astype(BF)

    @pl.when(lax.rem(head, GROUP) == GROUP - 1)
    def _():
        dk_ref[...] = (dk_acc[...] * SCALE).astype(BF)
        dv_ref[...] = dv_acc[...].astype(BF)


def attention_sizes(tokens, length):
    tq = 256 if tokens % 256 == 0 else tokens
    kb = 256 if length % 256 == 0 else 128
    return tq, kb


def attention_meta(ctx, tokens, segments, tq, kb):
    entries = [ctx]
    for part in range(tokens // tq):
        first = ctx * tokens + part * tq
        own = lax.dynamic_slice_in_dim(segments, first, 1)
        start = jnp.sum((segments < own).astype(jnp.int32))
        entries += [start // kb, (first + tq + kb - 1) // kb]
    return jnp.stack(entries).astype(jnp.int32)


def attention_forward(q, k, v, meta, segk, segq):
    tokens, length = q.shape[0], k.shape[0]
    tq, kb = attention_sizes(tokens, length)
    const = lambda h, m: (0, 0)
    return pl.pallas_call(
        functools.partial(attn_fwd_kernel, kb, tq),
        out_shape=(
            jax.ShapeDtypeStruct(q.shape, BF),
            jax.ShapeDtypeStruct((QUERY_HEADS, 1, tokens), F32),
        ),
        grid_spec=pltpu.PrefetchScalarGridSpec(
            num_scalar_prefetch=1,
            grid=(QUERY_HEADS,),
            in_specs=[
                pl.BlockSpec((tokens, HEAD_SIZE), lambda h, m: (0, h)),
                pl.BlockSpec((length, HEAD_SIZE), lambda h, m: (0, h // GROUP)),
                pl.BlockSpec((length, HEAD_SIZE), lambda h, m: (0, h // GROUP)),
                pl.BlockSpec((length, 1), const),
                pl.BlockSpec((1, tokens), const),
            ],
            out_specs=[
                pl.BlockSpec((tokens, HEAD_SIZE), lambda h, m: (0, h)),
                pl.BlockSpec((1, 1, tokens), lambda h, m: (h, 0, 0)),
            ],
            scratch_shapes=[
                pltpu.VMEM((length, tokens), F32),
                pltpu.VMEM((length, tq), F32),
                pltpu.VMEM((HEAD_SIZE, length), BF),
            ],
        ),
        compiler_params=pltpu.CompilerParams(vmem_limit_bytes=VMEM_LIMIT),
        cost_estimate=pl.CostEstimate(
            flops=3 * QUERY_HEADS * tokens * length * HEAD_SIZE,
            transcendentals=QUERY_HEADS * tokens * length,
            bytes_accessed=4 * tokens * MODEL_WIDTH,
        ),
        name="attn_fwd",
    )(meta, q, k, v, segk, segq)


def attention_backward(q, k, v, do, lse, cos, sin, meta, segk, segq):
    tokens, length = q.shape[0], k.shape[0]
    tq, kb = attention_sizes(tokens, length)
    const = lambda h, m: (0, 0)
    by_head = lambda h, m: (0, h)
    by_group = lambda h, m: (0, h // GROUP)
    return pl.pallas_call(
        functools.partial(attn_bwd_kernel, kb, tq),
        out_shape=(
            jax.ShapeDtypeStruct(q.shape, BF),
            jax.ShapeDtypeStruct(k.shape, BF),
            jax.ShapeDtypeStruct(v.shape, BF),
        ),
        grid_spec=pltpu.PrefetchScalarGridSpec(
            num_scalar_prefetch=1,
            grid=(QUERY_HEADS,),
            in_specs=[
                pl.BlockSpec((tokens, HEAD_SIZE), by_head),
                pl.BlockSpec((length, HEAD_SIZE), by_group),
                pl.BlockSpec((length, HEAD_SIZE), by_group),
                pl.BlockSpec((tokens, HEAD_SIZE), by_head),
                pl.BlockSpec((1, 1, tokens), lambda h, m: (h, 0, 0)),
                pl.BlockSpec((tokens, HEAD_SIZE), const),
                pl.BlockSpec((tokens, HEAD_SIZE), const),
                pl.BlockSpec((length, 1), const),
                pl.BlockSpec((1, tokens), const),
            ],
            out_specs=[
                pl.BlockSpec((tokens, HEAD_SIZE), by_head),
                pl.BlockSpec((length, HEAD_SIZE), by_group),
                pl.BlockSpec((length, HEAD_SIZE), by_group),
            ],
            scratch_shapes=[
                pltpu.VMEM((length, tokens), F32),
                pltpu.VMEM((length, tq), F32),
                pltpu.VMEM((length, tq), F32),
                pltpu.VMEM((HEAD_SIZE, length), BF),
                pltpu.VMEM((length, HEAD_SIZE), F32),
                pltpu.VMEM((length, HEAD_SIZE), F32),
            ],
        ),
        compiler_params=pltpu.CompilerParams(vmem_limit_bytes=VMEM_LIMIT),
        cost_estimate=pl.CostEstimate(
            flops=8 * QUERY_HEADS * tokens * length * HEAD_SIZE,
            transcendentals=QUERY_HEADS * tokens * length,
            bytes_accessed=8 * tokens * MODEL_WIDTH,
        ),
        name="attn_bwd",
    )(meta, q, k, v, do, lse, cos, sin, segk, segq)


def expert_kernel(cap, tile, x_ref, cot_ref, srow_ref, scol_ref, grow_ref,
                  gate_ref, up_ref, down_ref,
                  py_ref, pdn_ref, dw_ref, xs_ref, dy_ref, hb_ref, dg_ref, du_ref,
                  pick_ref, put_ref, cg_ref, ys_ref, acc_ref):
    local = gate_ref.shape[0]
    tokens, width = x_ref.shape[1], x_ref.shape[2]
    hidden = gate_ref.shape[2]
    weights = []
    spread = lax.broadcasted_iota(jnp.int32, (tokens, local * cap), 1)
    put = None
    for e in range(local):
        slot = lax.broadcasted_iota(jnp.int32, (cap, tokens), 0)
        hit = slot == srow_ref[0, e : e + 1, :]
        pick_ref[pl.ds(e * cap, cap), :] = jnp.where(hit, 1.0, 0.0).astype(BF)
        weights.append(
            jnp.sum(jnp.where(hit, grow_ref[0, e : e + 1, :], 0.0), axis=1, keepdims=True)
        )
        own = scol_ref[0, :, e : e + 1]
        here = spread == jnp.where(own < 0, -1, own + e * cap)
        put = here if put is None else put | here
    put_ref[...] = jnp.where(put, 1.0, 0.0).astype(BF)

    def gather(j, _):
        cols = pl.ds(pl.multiple_of(j * tile, tile), tile)
        xs = mm(pick_ref[...], x_ref[0, :, cols]).astype(BF)
        cg = mm(pick_ref[...], cot_ref[0, :, cols])
        cg_ref[:, cols] = cg.astype(BF)
        for e in range(local):
            rows = slice(e * cap, (e + 1) * cap)
            xs_ref[0, e, :, cols] = xs[rows]
            dy_ref[0, e, :, cols] = (weights[e] * cg[rows]).astype(BF)
        return 0

    lax.fori_loop(0, width // tile, gather, 0)

    def middle(j, _):
        cols = pl.ds(pl.multiple_of(j * tile, tile), tile)
        for e in range(local):
            g = mm(xs_ref[0, e], gate_ref[e, :, cols])
            u = mm(xs_ref[0, e], up_ref[e, :, cols])
            dh = mm(dy_ref[0, e], down_ref[e, :, cols])
            s = 1.0 / (1.0 + jnp.exp(-g))
            act = g * s
            hb_ref[0, e, :, cols] = (act * u).astype(BF)
            dg_ref[0, e, :, cols] = (dh * u * (s * (1.0 + g * (1.0 - s)))).astype(BF)
            du_ref[0, e, :, cols] = (dh * act).astype(BF)
        return 0

    lax.fori_loop(0, hidden // tile, middle, 0)

    acc_ref[...] = jnp.zeros_like(acc_ref)

    def finish(j, _):
        cols = pl.ds(pl.multiple_of(j * tile, tile), tile)
        for e in range(local):
            rows = pl.ds(e * cap, cap)
            y = mm_nt(hb_ref[0, e], down_ref[e, cols, :])
            acc_ref[rows, :] += cg_ref[rows, cols].astype(F32) * y
            ys_ref[rows, :] = (weights[e] * y).astype(BF)
        py_ref[0, :, cols] = mm(put_ref[...], ys_ref[...]).astype(BF)
        for e in range(local):
            rows = pl.ds(e * cap, cap)
            dxs = mm_nt(dg_ref[0, e], gate_ref[e, cols, :])
            dxs = dxs + mm_nt(du_ref[0, e], up_ref[e, cols, :])
            ys_ref[rows, :] = dxs.astype(BF)
        pdn_ref[0, :, cols] = mm(put_ref[...], ys_ref[...]).astype(BF)
        return 0

    lax.fori_loop(0, width // tile, finish, 0)
    for e in range(local):
        dot = jnp.sum(acc_ref[pl.ds(e * cap, cap), :], axis=1, keepdims=True)
        slot = lax.broadcasted_iota(jnp.int32, (cap, tokens), 0)
        hit = slot == srow_ref[0, e : e + 1, :]
        dw_ref[0, e : e + 1, :] = jnp.sum(jnp.where(hit, dot, 0.0), axis=0, keepdims=True)


def expert_block(x, cot, srow, scol, grow, gate, up, down, cap):
    n, tokens, width = x.shape
    local, _, hidden = gate.shape
    tile = 256
    by_source = lambda s: (s, 0, 0)
    by_source4 = lambda s: (s, 0, 0, 0)
    const3 = lambda s: (0, 0, 0)
    weight_spec = pl.BlockSpec((local, width, hidden), const3, pipeline_mode=pl.Buffered(1))
    slot_in = lambda d: jax.ShapeDtypeStruct((n, local, cap, d), BF)
    slot_spec = lambda d: pl.BlockSpec((1, local, cap, d), by_source4)
    return pl.pallas_call(
        functools.partial(expert_kernel, cap, tile),
        out_shape=(
            jax.ShapeDtypeStruct((n, tokens, width), BF),
            jax.ShapeDtypeStruct((n, tokens, width), BF),
            jax.ShapeDtypeStruct((n, local, tokens), F32),
            slot_in(width), slot_in(width), slot_in(hidden), slot_in(hidden), slot_in(hidden),
        ),
        grid=(n,),
        in_specs=[
            pl.BlockSpec((1, tokens, width), by_source),
            pl.BlockSpec((1, tokens, width), by_source),
            pl.BlockSpec((1, local, tokens), by_source),
            pl.BlockSpec((1, tokens, local), by_source),
            pl.BlockSpec((1, local, tokens), by_source),
            weight_spec, weight_spec, weight_spec,
        ],
        out_specs=[
            pl.BlockSpec((1, tokens, width), by_source),
            pl.BlockSpec((1, tokens, width), by_source),
            pl.BlockSpec((1, local, tokens), by_source),
            slot_spec(width), slot_spec(width), slot_spec(hidden), slot_spec(hidden),
            slot_spec(hidden),
        ],
        scratch_shapes=[
            pltpu.VMEM((local * cap, tokens), BF),
            pltpu.VMEM((tokens, local * cap), BF),
            pltpu.VMEM((local * cap, width), BF),
            pltpu.VMEM((local * cap, tile), BF),
            pltpu.VMEM((local * cap, tile), F32),
        ],
        compiler_params=pltpu.CompilerParams(vmem_limit_bytes=VMEM_LIMIT),
        cost_estimate=pl.CostEstimate(
            flops=2 * n * local * cap * width * (6 * hidden + 4 * tokens),
            transcendentals=n * local * cap * hidden,
            bytes_accessed=2 * (4 * n * tokens * width + 3 * local * width * hidden),
        ),
        name="experts",
    )(x, cot, srow, scol, grow, gate, up, down)


def expert_grad_kernel(xs_ref, dy_ref, hb_ref, dg_ref, du_ref, out_ref):
    n, _, cap, tile = xs_ref.shape
    hidden = hb_ref.shape[3]
    flat = lambda ref: ref[...].reshape(n * cap, ref.shape[3])
    xs = flat(xs_ref)
    out_ref[0, :, 0:hidden] = mm_tn(xs, flat(dg_ref)).astype(BF)
    out_ref[0, :, hidden : 2 * hidden] = mm_tn(xs, flat(du_ref)).astype(BF)
    out_ref[0, :, 2 * hidden : 3 * hidden] = mm_tn(flat(dy_ref), flat(hb_ref)).astype(BF)


def expert_grads(xs, dy, hb, dg, du):
    n, local, cap, width = xs.shape
    hidden = hb.shape[3]
    tile = 256
    wide = pl.BlockSpec((n, 1, cap, tile), lambda e, j: (0, e, 0, j))
    deep = pl.BlockSpec((n, 1, cap, hidden), lambda e, j: (0, e, 0, 0))
    return pl.pallas_call(
        expert_grad_kernel,
        out_shape=jax.ShapeDtypeStruct((local, width, 3 * hidden), BF),
        grid=(local, width // tile),
        in_specs=[wide, wide, deep, deep, deep],
        out_specs=pl.BlockSpec((1, tile, 3 * hidden), lambda e, j: (e, j, 0)),
        compiler_params=pltpu.CompilerParams(vmem_limit_bytes=VMEM_LIMIT),
        cost_estimate=pl.CostEstimate(
            flops=6 * n * local * cap * width * hidden,
            transcendentals=0,
            bytes_accessed=2 * n * local * cap * (2 * width + 3 * hidden),
        ),
        name="expert_grads",
    )(xs, dy, hb, dg, du)


def body(
    tokens, cotangent, segment_ids, routes, fill_rank, query_weight, key_projection_weight,
    value_projection_weight, output_weight, router_weight, gain_attention, gain_experts,
    gate_weight, up_weight, down_weight,
):
    context_index = lax.axis_index("context")
    expert_size = lax.axis_size("expert")
    expert_index = lax.axis_index("expert")
    rows = tokens.shape[1]
    length = segment_ids.shape[1]
    kv_width = KEY_VALUE_HEADS * HEAD_SIZE
    gather = lambda w: lax.all_gather(w, "context", axis=0, tiled=True)

    upstream_low = cotangent[0]
    cot_all = lax.all_gather(upstream_low, "expert", axis=0)

    expert_count = router_weight.shape[1]
    local = gate_weight.shape[0]
    capacity = 5 * rows * TOP // (4 * expert_count)
    cap = -(-capacity // 64) * 64
    names = jnp.arange(expert_count, dtype=jnp.int32)
    route_hit = routes[0][:, :, None] == names[None, None, :]
    routed = jnp.any(route_hit, axis=1)
    ranks = fill_rank[0, 0].reshape(rows, TOP)
    order = jnp.sum(jnp.where(route_hit, ranks[:, :, None], 0), axis=1)
    order = jnp.where(routed, order, rows * TOP).T
    slots = jnp.sum((order[:, :, None] < order[:, None, :]).astype(jnp.int32), axis=1)
    kept = routed.T & (slots < capacity)
    slots = jnp.where(kept, slots, -1)
    slots_all = lax.all_gather(slots, "expert", axis=0)
    slots_mine = lax.dynamic_slice_in_dim(slots_all, expert_index * local, local, axis=1)
    kept_float = kept.T.astype(F32)

    query_full, key_full, value_full, output_full, router_full, gain_first, gain_second = (
        gather(query_weight), gather(key_projection_weight), gather(value_projection_weight),
        gather(output_weight), gather(router_weight), gather(gain_attention), gather(gain_experts),
    )
    router_float = router_full.astype(F32)
    gain_first = gain_first.astype(F32)
    gain_second = gain_second.astype(F32)
    residual = tokens[0].astype(F32)
    root_first = inverse_root(residual)
    attn_input = (residual * root_first * gain_first).astype(BF)
    positions = context_index * rows + jnp.arange(rows, dtype=jnp.int32)
    cosine, sine = rope_tables(positions)
    cos_full = jnp.concatenate([cosine, cosine], axis=-1)
    sin_full = jnp.concatenate([-sine, sine], axis=-1)
    turn = lambda v, heads, d: apply_rotary(
        v.reshape(rows, heads, HEAD_SIZE), cosine, sine, d
    ).reshape(rows, heads * HEAD_SIZE)
    q = turn(mm(attn_input, query_full), QUERY_HEADS, 1.0).astype(BF)
    k_own = turn(mm(attn_input, key_full), KEY_VALUE_HEADS, 1.0).astype(BF)
    v_own = mm(attn_input, value_full).astype(BF)
    kv = gather(jnp.concatenate([k_own, v_own], axis=1))
    k_all, v_all = kv[:, :kv_width], kv[:, kv_width:]
    segments = segment_ids[0]
    tq, kb = attention_sizes(rows, length)
    meta = attention_meta(context_index, rows, segments, tq, kb)
    segk = segments[:, None]
    segq = lax.dynamic_slice_in_dim(segments, context_index * rows, rows)[None, :]
    mixed, lse = attention_forward(q, k_all, v_all, meta, segk, segq)

    hidden = residual + mm(mixed, output_full)
    root_second = inverse_root(hidden)
    normed = hidden * root_second * gain_second
    expert_input = normed.astype(BF)
    logits = precise_dims(normed, router_float, ((1,), (0,)))
    gates = jax.nn.softmax(jnp.where(routed, logits, -jnp.inf), axis=-1)
    kept_gates = gates * kept_float

    x_all = lax.all_gather(expert_input, "expert", axis=0)
    gates_all = lax.all_gather(kept_gates.T, "expert", axis=0)
    gates_mine = lax.dynamic_slice_in_dim(gates_all, expert_index * local, local, axis=1)
    part_y, part_dn, dw, xs, dy, hb, dg, du = expert_block(
        x_all, cot_all, slots_mine, slots_mine.transpose(0, 2, 1), gates_mine,
        gate_weight, up_weight, down_weight, cap,
    )
    scatter = lambda v: lax.psum_scatter(v, "expert", scatter_dimension=0, tiled=False)
    dn_low = scatter(part_dn)
    dw_back = lax.all_to_all(dw, "expert", split_axis=0, concat_axis=0, tiled=True)
    gate_dot = dw_back.reshape(expert_count, rows).T * kept_float
    grads_low = expert_grads(xs, dy, hb, dg, du)
    grads_shard = lax.psum_scatter(
        grads_low, ("dp", "context"), scatter_dimension=1, tiled=True
    ).astype(F32)
    ff = gate_weight.shape[2]
    gate_grad, up_grad, down_grad = (grads_shard[:, :, i * ff : (i + 1) * ff] for i in range(3))
    mixture = scatter(part_y)
    layer_out = (hidden + mixture.astype(F32)).astype(BF)

    upstream = upstream_low.astype(F32)
    logit_grad = gates * (gate_dot - jnp.sum(gates * gate_dot, axis=-1, keepdims=True))
    normed_grad = dn_low.astype(F32) + precise_dims(logit_grad, router_float, ((1,), (1,)))
    router_local = precise_dims(normed, logit_grad, ((0,), (0,)))
    hidden_total = upstream + norm_back(hidden, root_second, gain_second, normed_grad)
    gain_second_grad = jnp.sum(normed_grad * hidden * root_second, axis=0)
    attn_grad_low = hidden_total.astype(BF)
    output_local = mm_tn(mixed, attn_grad_low)
    mixed_grad_low = mm_nt(attn_grad_low, output_full).astype(BF)

    dq_low, dk_part, dv_part = attention_backward(
        q, k_all, v_all, mixed_grad_low, lse, cos_full, sin_full, meta, segk, segq
    )
    dkv = lax.psum_scatter(
        jnp.concatenate([dk_part, dv_part], axis=1), "context", scatter_dimension=0, tiled=True
    )
    dk_low = turn(dkv[:, :kv_width].astype(F32), KEY_VALUE_HEADS, -1.0).astype(BF)
    dv_low = dkv[:, kv_width:]
    input_total = mm_nt(dq_low, query_full) + mm_nt(dk_low, key_full) + mm_nt(dv_low, value_full)
    query_local = mm_tn(attn_input, dq_low)
    key_local = mm_tn(attn_input, dk_low)
    value_local = mm_tn(attn_input, dv_low)
    grad_tokens = (hidden_total + norm_back(residual, root_first, gain_first, input_total)).astype(BF)
    gain_first_grad = jnp.sum(input_total * residual * root_first, axis=0)

    reduce_rows = lambda v: lax.psum(
        lax.psum_scatter(v.astype(BF), "context", scatter_dimension=0, tiled=True), ("dp", "expert")
    ).astype(F32)
    return (
        layer_out[None], grad_tokens[None],
        reduce_rows(query_local), reduce_rows(key_local), reduce_rows(value_local),
        reduce_rows(output_local), reduce_rows(router_local),
        reduce_rows(gain_first_grad), reduce_rows(gain_second_grad),
        gate_grad, up_grad, down_grad,
    )


def solution(mesh):
    both = ("dp", "expert")
    token_spec = P(both, "context", None)
    row_spec = P("context", None)
    expert_out = P("expert", ("dp", "context"), None)
    return jax.shard_map(
        body,
        mesh=mesh,
        in_specs=(
            token_spec, token_spec, P(both, None), token_spec, token_spec,
            row_spec, row_spec, row_spec, row_spec, row_spec, P("context"), P("context"),
            P("expert", None, None), P("expert", None, None), P("expert", None, None),
        ),
        out_specs=(
            token_spec, token_spec, row_spec, row_spec, row_spec, row_spec, row_spec,
            P("context"), P("context"), expert_out, expert_out, expert_out,
        ),
        check_vma=False,
    )
```

time: 1590 us -> 1090 us (0.69)
  waiting for transfers between devices: 895 us -> 619 us
  matrix products: 248 us -> 60.3 us
  Pallas kernels: 0 us -> 168 us
  local copies, waits for them, and re-layouts: 180 us -> 32 us
  other arithmetic: 120 us -> 45.1 us
  blocking collectives: 96.2 us -> 132 us
  starting transfers between devices: 24.6 us -> 4.94 us
    all_to_all x4 -> x1, waiting for transfers between devices: 560 us -> 5.99 us  [body(): lax.all_to_all(dw, 'expert', split_axis=0, concat_axis=0, tiled=True)]
    dot_general x30 -> x15, matrix products: 248 us -> 60.3 us  [the longest x4 20.4 us: mm_tn(): lax.dot_general(a, b, (((0,), (0,)), ((), ())), preferred_element_type=F32)]
    all_gather x2 -> x5, waiting for transfers between devices: 0.02 us -> 169 us  [the longest x1 116 us: body(): x_all = lax.all_gather(expert_input, 'expert', axis=0)]
    pallas_call x0 -> x4, Pallas kernels: none -> 168 us  [the longest x1 91.2 us: expert_block(): pl.pallas_call(functools.partial(expert_kernel, cap, tile), out_shape=(ja...]
    psum x1, waiting for transfers between devices: 79.4 us -> 200 us  [body(): lax.psum(lax.psum_scatter(v.astype(BF), 'context', scatter_dimension=0, t...]
    gather x7 -> x0, local copies, waits for them, and re-layouts: 92.3 us -> none  [the longest x1 17.8 us: body(): returned_flat[pair_slot].reshape(token_rows, TOP, MODEL_WIDTH)]
    reduce_sum x10 -> x6, other arithmetic: 65.5 us -> 5.61 us  [the longest x1 1.94 us: attention_meta(): start = jnp.sum((segments < own).astype(jnp.int32))]
    convert_element_type x8 -> x4, local copies, waits for them, and re-layouts: 43.2 us -> 1.73 us  [the longest x1 1.57 us: body(): q = turn(mm(attn_input, query_full), QUERY_HEADS, 1.0).astype(BF)]
  transfers between devices with their start and end apart: 17 -> 16, of which waited for: 11 -> 9; matrix products, arithmetic and copies ran while one was open for 24% -> 9% of each run, Pallas kernels for 0% -> 5%
where the time goes in v1:
time: 1090 us; the launch traced here: 1080 us
  waiting for transfers between devices  619 us (57%)
  Pallas kernels  168 us (15%)
  blocking collectives  132 us (12%)
  matrix products  60.3 us (6%)
  other arithmetic  45.1 us (4%)
  local copies, waits for them, and re-layouts  32 us (3%)
  between operations  20.8 us (2%)
    reduce_scatter x2, waiting for transfers between devices, body(): lax.psum_scatter(v, 'expert', scatter_dimension=0, tiled=False)  203 us
    psum x1, waiting for transfers between devices, body(): lax.psum(lax.psum_scatter(v.astype(BF), 'context', scatter_dimension=0, t...  200 us
    all_gather x1, waiting for transfers between devices, body(): x_all = lax.all_gather(expert_input, 'expert', axis=0)  116 us
    pallas_call x1, Pallas kernels, expert_block(): pl.pallas_call(functools.partial(expert_kernel, cap, tile), out_shape=(ja...  91.2 us
    psum x1, blocking collectives, body(): lax.psum(lax.psum_scatter(v.astype(BF), 'context', scatter_dimension=0, t...  78.1 us
    all_gather x1, waiting for transfers between devices, body(): cot_all = lax.all_gather(upstream_low, 'expert', axis=0)  40.3 us
    pallas_call x1, Pallas kernels, expert_grads(): pl.pallas_call(expert_grad_kernel, out_shape=jax.ShapeDtypeStruct((local,...  28.5 us
    pallas_call x1, Pallas kernels, attention_backward(): pl.pallas_call(functools.partial(attn_bwd_kernel, kb, tq), out_shape=(jax...  27.2 us
  transfers between devices with their start and end apart: 16, of which 9 were waited for; matrix products, arithmetic and copies ran while one was open for 9% of the time, Pallas kernels for 5%

profile of v1, /device:TPU:0, one launch (start us, length us, event | category | flops | bytes accessed | tf_op | source)
XLA Modules:
  0.0 1081.0 jit_solution(7441388871436150903)
XLA Ops:
  7.3 1.9 fusion.6
  10.4 1.9 all-gather.3
  12.4 2.6 all_gather.47
  15.0 2.6 all_gather.48
  17.6 1.2 copy.99
  18.8 1.3 convolution_convert_fusion.5
  20.1 1.5 fusion.25
  21.6 1.8 fusion.39
  23.7 1.1 subtract_convert_fusion.1
  25.0 1.8 pad_maximum_fusion.2
  29.5 1.9 fusion.50
  36.7 1.8 all-gather.4
  38.5 1.0 copy.105.segk_ref
  40.8 2.2 fusion.58
  43.0 12.7 %all-gather.11.cloned.1.call-done = bf16[1536,1536]{1,0:T(8,128)(2,1)} async-done(((bf16[768,1536]{1,0:T(8,128)(2,1)}), bf16[1536,1536]{1,0:T(8,128)(2,1)}) %all-gather.11.cloned.1.call-update) | async-done | bytes 4718608 | tf_op jit(solution)/shard_map/all_gather | solution.py:456
  55.7 6.6 copy.95
  62.3 4.7 fusion.27
  67.8 1.6 copy.104.q_ref
  69.3 20.8 %attn_fwd.1 = (bf16[512,1536]{1,0:T(8,128)(2,1)}, f32[12,1,512]{2,1,0:T(1,128)}) custom-call(s32[5]{0:T(128)} %stack.23.meta, bf16[512,1536]{1,0:T(8,128)(2,1)} %copy.104.q_ref, bf16[1024,256]{1,0:T(8,128)(2,1)} %get-tuple-element.63.k_ref, bf16[1024,256]{1,0:T(8,128)(2,1)} %get-tuple-element.62.v_ref, s32[1024,1]{1,0:T(8,128)} %copy.105.segk_ref, ...), custom_call_target="tpu_custom_call" | custom-call | flops 2415919104 | bytes 3145728 | tf_op jit(solution)/shard_map/attn_fwd/pallas_call | solution.py:199
  90.1 6.0 multiply_reduce_fusion.2
  97.3 1.5 fusion.21
  99.3 1.4 reduce.9
  101.7 1.1 copy.106
  102.7 11.1 %all_gather.57 = bf16[1536,8]{0,1:T(8,128)(2,1)S(1)} all-gather(bf16[768,8]{0,1:T(8,128)(2,1)} %param.24), channel_id=1, replica_groups=mesh['dp'=4,'context'=2,'expert'=4] {'context'}, dimensions={0}, use_global_device_ids=true | all-gather | bytes 36864 | tf_op jit(solution)/shard_map/all_gather | solution.py:456
  113.9 1.0 convert_reduce_fusion
  114.9 2.5 fusion.48
  118.1 16.0 %all-gather.1 = s32[32,512]{1,0:T(8,128)S(1)} all-gather(s32[8,512]{1,0:T(8,128)S(1)} %fusion.47), channel_id=3, replica_groups=mesh['dp'=4,'context'=2,'expert'=4] {'expert'}, dimensions={0}, use_global_device_ids=true | all-gather | bytes 81920 | tf_op jit(solution)/shard_map/all_gather | solution.py:474
  134.7 2.1 copy.117
  136.8 15.3 %all-gather.2 = f32[32,512]{1,0:T(8,128)S(1)} all-gather(f32[8,512]{1,0:T(8,128)} %get-tuple-element.53), channel_id=4, replica_groups=mesh['dp'=4,'context'=2,'expert'=4] {'expert'}, dimensions={0}, use_global_device_ids=true | all-gather | bytes 81920 | tf_op jit(solution)/shard_map/all_gather | solution.py:516
  152.7 40.3 %all-gather.17.cloned.1.call-done.cot_ref = bf16[4,512,1536]{2,1,0:T(8,128)(2,1)} async-done(((bf16[1,512,1536]{2,1,0:T(8,128)(2,1)}), bf16[4,512,1536]{2,1,0:T(8,128)(2,1)}) %all-gather.17.cloned.1.call-update) | async-done | bytes 6291472 | tf_op jit(solution)/shard_map/all_gather | solution.py:459
  193.0 115.6 %all-gather.19.cloned.1.call-done = bf16[2048,1536]{1,0:T(8,128)(2,1)} async-done(((bf16[512,1536]{1,0:T(8,128)(2,1)}), bf16[2048,1536]{1,0:T(8,128)(2,1)}) %all-gather.19.cloned.1.call-update) | async-done | bytes 6291472 | tf_op jit(solution)/shard_map/all_gather | solution.py:515
  308.6 91.2 %experts.1 = (bf16[4,512,1536]{2,1,0:T(8,128)(2,1)}, bf16[4,512,1536]{2,1,0:T(8,128)(2,1)}, f32[4,2,512]{2,1,0:T(2,128)}, bf16[4,2,320,1536]{3,2,1,0:T(8,128)(2,...) custom-call(bf16[4,512,1536]{2,1,0:T(8,128)(2,1)} %bitcast.155, ...), custom_call_target="tpu_custom_call" | custom-call | flops 52344913920 | bytes 39321600 | tf_op jit(solution)/shard_map/experts/pallas_call | solution.py:372
  400.5 3.9 all-to-all-start
  404.5 2.3 pad_maximum_fusion.4
  406.8 6.0 all-to-all-done
  414.3 95.0 %reduce-scatter.12.cloned.1.call-done = bf16[1,512,1536]{2,1,0:T(8,128)(2,1)} async-done(((bf16[4,512,1536]{2,1,0:T(8,128)(2,1)}), bf16[1,512,1536]{2,1,0:T(8,128)(2,1)}) %reduce-scatter.12.cloned.1.call-update) | async-done | bytes 1572880 | tf_op jit(solution)/shard_map/reduce_scatter | solution.py:522
  509.2 5.9 multiply_reduce_fusion
  515.2 107.7 %reduce-scatter.10.cloned.1.call-done = bf16[1,512,1536]{2,1,0:T(8,128)(2,1)} async-done(((bf16[4,512,1536]{2,1,0:T(8,128)(2,1)}), bf16[1,512,1536]{2,1,0:T(8,128)(2,1)}) %reduce-scatter.10.cloned.1.call-update) | async-done | bytes 1572880 | tf_op jit(solution)/shard_map/reduce_scatter | solution.py:522
  622.8 5.0 convert_add_fusion
  627.8 7.2 convolution_convert_fusion.2.do_ref
  635.0 27.2 %attn_bwd.1 = (bf16[512,1536]{1,0:T(8,128)(2,1)}, bf16[1024,256]{1,0:T(8,128)(2,1)}, bf16[1024,256]{1,0:T(8,128)(2,1)}) custom-call(s32[5]{0:T(128)} %stack.23.meta, bf16[512,1536]{1,0:T(8,128)(2,1)} %copy.104.q_ref, bf16[1024,256]{1,0:T(8,128)(2,1)} %get-tuple-element.63.k_ref, bf16[1024,256]{1,0:T(8,128)(2,1)} %get-tuple-element.62.v_ref, ...), custom_call_target="tpu_custom_call" | custom-call | flops 6442450944 | bytes 6291456 | tf_op jit(solution)/shard_map/attn_bwd/pallas_call | solution.py:241
  662.2 2.2 pad_maximum_fusion.1
  664.5 20.3 %reduce-scatter.14.cloned.1.call-done = bf16[512,512]{1,0:T(8,128)(2,1)} async-done(((bf16[1024,512]{1,0:T(8,128)(2,1)}), bf16[512,512]{1,0:T(8,128)(2,1)}) %reduce-scatter.14.cloned.1.call-update) | async-done | bytes 524304 | tf_op jit(solution)/shard_map/reduce_scatter | solution.py:548
  684.8 3.1 convolution_convert_fusion.3
  689.0 1.8 slice_convert_fusion
  690.7 2.0 copy.116
  692.8 1.2 multiply_subtract_fusion
  694.0 3.3 convolution_convert_fusion.4
  697.3 7.2 convolution_convert_fusion
  705.2 6.8 convolution_convert_fusion.1
  712.8 2.6 fusion.22
  715.6 28.5 %expert_grads.1 = bf16[2,1536,2304]{2,1,0:T(8,128)(2,1)} custom-call(bf16[4,2,320,1536]{3,2,1,0:T(8,128)(2,1)} %get-tuple-element.33.xs_ref, bf16[4,2,320,1536]{3,2,1,0:T(8,128)(2,1)} %get-tuple-element.34.dy_ref, bf16[4,2,320,768]{3,2,1,0:T(8,128)(2,1)} %get-tuple-element.35.hb_ref, bf16[4,2,320,768]{3,2,1,0:T(8,128)(2,1)} %get-tuple-element.36.dg_ref, ...), custom_call_target="tpu_custom_call" | custom-call | flops 18119393280 | bytes 27525120 | tf_op jit(solution)/shard_map/expert_grads/pallas_call | solution.py:429
  746.0 4.6 fusion.59
  752.3 2.8 fusion.15
  755.2 2.5 all-reduce.4
  757.8 78.1 %all-reduce.2 = (bf16[768,8]{0,1:T(8,128)(2,1)S(1)}, bf16[768]{0:T(1024)(128)(2,1)S(1)}, bf16[768]{0:T(1024)(128)(2,1)S(1)}) all-reduce(bf16[768,8]{0,1:T(8,128)(2,1)} %reduce-scatter.24.cloned.1.call-done, bf16[768]{0:T(1024)(128)(2,1)S(1)} %dynamic-slice.4, ...), channel_id=1, replica_groups=mesh['dp'=4,'context'=2,'expert'=4] {'dp','expert'}, use_global_device_ids=true, to_apply=%region_24.25 | all-reduce | flops 7680 | bytes 30720 | tf_op jit(solution)/shard_map/psum | solution.py:560
  837.7 5.3 fusion.24
  843.0 17.8 %reduce-scatter.26.cloned.1.call-done = bf16[2,192,2304]{2,1,0:T(8,128)(2,1)} async-done(((bf16[2,1536,2304]{2,1,0:T(8,128)(2,1)}), bf16[2,192,2304]{2,1,0:T(8,128)(2,1)}) %reduce-scatter.26.cloned.1.call-update) | async-done | bytes 1769488 | tf_op jit(solution)/shard_map/reduce_scatter | solution.py:527
  860.8 3.3 fusion.57
  864.1 200.2 %all-reduce.7.cloned.1.call-done = (bf16[768,1536]{1,0:T(8,128)(2,1)}, bf16[768,256]{1,0:T(8,128)(2,1)}, bf16[768,256]{1,0:T(8,128)(2,1)}, bf16[768,1536]{1,0:T(8,128)(2,1)}) async-done(((bf16[768,1536]{1,0:T(8,128)(2,1)}, bf16[768,256]{1,0:T(8,128)(2,1)}, bf16[768,256]{1,0:T(8,128)(2,1)}, bf16[768,1536]{1,0:T(8,128)(2,1)}), (bf16[768,1536]{1,0:T(8,128)(2,1)}, bf16[768,256]{1,0:T(8,128)(2,1)}, ...) | async-done | bytes 5505040 | tf_op jit(solution)/shard_map/psum | solution.py:560
  1064.4 2.1 convert_element_type.180
  1066.5 1.9 convert_element_type.182
  1068.4 2.8 convert_element_type.178
  1071.2 2.8 convert_element_type.184
  (169 shorter events, 20.9 us)
Async XLA Ops:
  7.2 11.6 %copy-start = (bf16[1,512,1536]{2,1,0:T(8,128)(2,1)S(1)}, bf16[1,512,1536]{2,1,0:T(8,128)(2,1)}, u32[]{:S(2)}) copy-start(bf16[1,512,1536]{2,1,0:T(8,128)(2,1)} %param.15) | copy-start | bytes 4718596
  7.2 33.6 %all-gather.13.cloned.1.call-start = ((), (), s32[]{:S(2)}) async-start(), calls=%async_computation.11 | async-start | bytes 1572864 | tf_op jit(solution)/shard_map/all_gather | solution.py:456
  9.8 10.4 copy-start.34
  12.4 49.9 %copy-start.23 = (f32[1536]{0:T(1024)}, f32[1536]{0:T(1024)S(1)}, u32[]{:S(2)}) copy-start(f32[1536]{0:T(1024)S(1)} %reshape.230) | copy-start | bytes 18436
  15.0 5.1 copy-start.3
  17.6 4.0 copy-start.5
  18.8 1.3 copy-start.11
  23.4 4.1 copy-start.9
  26.8 2.2 copy-start.33
  26.8 9.9 copy-start.42
  26.8 28.9 %all-gather.11.cloned.1.call-start = ((), (), s32[]{:S(2)}) async-start(), calls=%async_computation.10 | async-start | bytes 7077888 | tf_op jit(solution)/shard_map/all_gather | solution.py:456
  27.6 62.5 %all-gather.15.cloned.1.call-start = ((), (), s32[]{:S(2)}) async-start(), calls=%async_computation.12 | async-start | bytes 7077888 | tf_op jit(solution)/shard_map/all_gather | solution.py:456
  28.3 164.7 %all-gather.17.cloned.1.call-start = ((), (), s32[]{:S(2)}) async-start(), calls=%async_computation.13 | async-start | bytes 7864320 | tf_op jit(solution)/shard_map/all_gather | solution.py:459
  28.9 279.7 %all-gather.19.cloned.1.call-start = ((), (), s32[]{:S(2)}) async-start(), calls=%async_computation.23 | async-start | bytes 7864320 | tf_op jit(solution)/shard_map/all_gather | solution.py:515
  38.5 58.2 %copy-start.15 = (f32[1536]{0:T(1024)}, f32[1536]{0:T(1024)S(1)}, u32[]{:S(2)}) copy-start(f32[1536]{0:T(1024)S(1)} %reshape.231) | copy-start | bytes 18436
  55.7 6.6 copy-start.35
  96.7 0.6 copy-start.27
  97.3 16.5 %copy-start.32 = (s32[1,512,4]{1,2,0:T(4,128)S(1)}, s32[1,512,4]{1,2,0:T(4,128)}, u32[]{:S(2)}) copy-start(s32[1,512,4]{1,2,0:T(4,128)} %param.18) | copy-start | bytes 24580
  98.8 410.5 %reduce-scatter.12.cloned.1.call-start = ((), (), s32[]{:S(2)}) async-start(), calls=%async_computation.15 | async-start | bytes 7864320 | tf_op jit(solution)/shard_map/reduce_scatter | solution.py:522
  113.8 4.3 copy-start.20
  113.8 4.2 copy-start.13
  117.4 16.7 %copy-start.25 = (f32[512]{0:T(512)}, f32[512]{0:T(512)S(1)}, u32[]{:S(2)}) copy-start(f32[512]{0:T(512)S(1)} %get-tuple-element.80) | copy-start | bytes 6148
  117.4 0.6 copy-start.30
  118.1 16.1 %copy-start.21 = (pred[8,512]{1,0:T(8,128)(4,1)}, pred[8,512]{1,0:T(8,128)(4,1)S(1)}, u32[]{:S(2)}) copy-start(pred[8,512]{1,0:T(8,128)(4,1)S(1)} %get-tuple-element.54) | copy-start | bytes 12292
  399.8 223.0 %reduce-scatter.10.cloned.1.call-start = ((), (), s32[]{:S(2)}) async-start(), calls=%async_computation.14 | async-start | bytes 7864320 | tf_op jit(solution)/shard_map/reduce_scatter | solution.py:522
  400.5 12.2 %all-to-all-start = ((f32[4,2,512]{2,1,0:T(2,128)}), f32[4,2,512]{2,1,0:T(2,128)}, u32[]{:S(2)}, u32[]{:S(2)}) async-start(f32[4,2,512]{2,1,0:T(2,128)} %get-tuple-element.28), calls=%async_computation.2 | async-start | bytes 32768 | tf_op jit(solution)/shard_map/all_to_all | solution.py:524
  404.4 280.4 %reduce-scatter.14.cloned.1.call-start = ((), (), s32[]{:S(2)}) async-start(), calls=%async_computation.16 | async-start | bytes 1572864 | tf_op jit(solution)/shard_map/reduce_scatter | solution.py:548
  413.5 101.7 %copy-start.18 = (f32[8,512]{1,0:T(8,128)}, f32[8,512]{1,0:T(8,128)S(1)}, u32[]{:S(2)}) copy-start(f32[8,512]{1,0:T(8,128)S(1)} %reshape.214) | copy-start | bytes 49156
  414.2 100.9 %copy-start.37 = (f32[512]{0:T(512)}, f32[512]{0:T(512)S(1)}, u32[]{:S(2)}) copy-start(f32[512]{0:T(512)S(1)} %multiply_reduce_fusion.3) | copy-start | bytes 6148
  414.3 208.6 %copy-start.16 = (f32[1536]{0:T(1024)S(1)}, f32[1536]{0:T(1024)}, u32[]{:S(2)}) copy-start(f32[1536]{0:T(1024)} %copy-done.15) | copy-start | bytes 18436
  414.3 208.6 %copy-start.28 = (f32[512]{0:T(512)S(1)}, f32[512]{0:T(512)}, u32[]{:S(2)}) copy-start(f32[512]{0:T(512)} %copy-done.27) | copy-start | bytes 6148
  414.3 208.6 %copy-start.41 = (f32[512]{0:T(512)S(1)}, f32[512]{0:T(512)}, u32[]{:S(2)}) copy-start(f32[512]{0:T(512)} %get-tuple-element.76) | copy-start | bytes 6148
  627.8 7.2 copy-start.2
  664.4 23.7 %copy-start.10 = (f32[512,64]{1,0:T(8,128)S(1)}, f32[512,64]{1,0:T(8,128)}, u32[]{:S(2)}) copy-start(f32[512,64]{1,0:T(8,128)} %get-tuple-element.70) | copy-start | bytes 393220
  664.5 79.9 %reduce-scatter.20.cloned.1.call-start = ((), (), s32[]{:S(2)}) async-start(), calls=%async_computation.19 | async-start | bytes 1179648 | tf_op jit(solution)/shard_map/reduce_scatter | solution.py:561
  687.9 56.5 %reduce-scatter.18.cloned.1.call-start = ((), (), s32[]{:S(2)}) async-start(), calls=%async_computation.18 | async-start | bytes 1179648 | tf_op jit(solution)/shard_map/reduce_scatter | solution.py:561
  697.3 47.2 %reduce-scatter.22.cloned.1.call-start = ((), (), s32[]{:S(2)}) async-start(), calls=%async_computation.20 | async-start | bytes 7077888 | tf_op jit(solution)/shard_map/reduce_scatter | solution.py:561
  704.5 0.7 copy-start.24
  704.5 0.7 copy-start.36
  704.6 39.9 %reduce-scatter.16.cloned.1.call-start = ((), (), s32[]{:S(2)}) async-start(), calls=%async_computation.17 | async-start | bytes 7077888 | tf_op jit(solution)/shard_map/reduce_scatter | solution.py:561
  712.1 0.7 copy-start.14
  712.1 0.7 copy-start.17
  712.1 0.7 copy-start.19
  712.1 0.7 copy-start.22
  712.1 0.7 copy-start.26
  712.1 0.7 copy-start.29
  712.1 0.7 copy-start.31
  712.1 0.7 copy-start.38
  712.1 45.7 %reduce-scatter.24.cloned.1.call-start = ((), (), s32[]{:S(2)}) async-start(), calls=%async_computation.21 | async-start | bytes 36864 | tf_op jit(solution)/shard_map/reduce_scatter | solution.py:561
  715.5 145.3 %reduce-scatter.26.cloned.1.call-start = ((), (), s32[]{:S(2)}) async-start(), calls=%async_computation.22 | async-start | bytes 15925248 | tf_op jit(solution)/shard_map/reduce_scatter | solution.py:527
  744.1 0.7 copy-start.43
  744.1 1.9 copy-start.44
  744.1 320.3 %all-reduce.7.cloned.1.call-start = ((), (), s32[]{:S(2)}) async-start(), calls=%async_computation.24 | async-start | bytes 11010048 | tf_op jit(solution)/shard_map/psum | solution.py:560
  746.0 4.6 copy-start.4
  750.6 1.4 copy-start.1
  750.6 1.6 copy-start.6
  750.6 1.7 copy-start.12
  752.3 2.8 copy-start.39
  752.3 85.4 %copy-start.40 = (f32[512]{0:T(512)S(1)}, f32[512]{0:T(512)}, u32[]{:S(2)}) copy-start(f32[512]{0:T(512)} %get-tuple-element.74) | copy-start | bytes 6148
  1064.4 4.0 copy-start.8
  1068.4 2.8 copy-start.7
Sparse Core Ops, SparseCore 0:
  26.9 11.5 all-gather.12
  40.1 15.5 all-gather.10
  57.2 15.6 all-gather.14
  74.4 118.5 all-gather.16
  195.0 113.5 all-gather.18
  399.9 109.2 reduce-scatter.11
  511.5 111.2 reduce-scatter.9
  664.6 20.1 reduce-scatter.13
  688.0 9.3 reduce-scatter.19
  700.1 9.4 reduce-scatter.17
  712.6 13.7 reduce-scatter.21
  729.1 13.7 reduce-scatter.15
  745.8 8.5 reduce-scatter.23
  758.3 102.5 reduce-scatter.25
  868.3 196.0 all-reduce.6

commit v2 on v1

--- a/solution.py
+++ b/solution.py
@@ -21,6 +21,7 @@
 BF = jnp.bfloat16
 F32 = jnp.float32
 VMEM_LIMIT = 60 * 1024 * 1024
+MOE_VMEM = 63 * 1024 * 1024
 
 
 def mm(a, b):
@@ -283,163 +284,354 @@
     )(meta, q, k, v, do, lse, cos, sin, segk, segq)
 
 
-def expert_kernel(cap, tile, x_ref, cot_ref, srow_ref, scol_ref, grow_ref,
-                  gate_ref, up_ref, down_ref,
-                  py_ref, pdn_ref, dw_ref, xs_ref, dy_ref, hb_ref, dg_ref, du_ref,
-                  pick_ref, put_ref, cg_ref, ys_ref, acc_ref):
-    local = gate_ref.shape[0]
-    tokens, width = x_ref.shape[1], x_ref.shape[2]
-    hidden = gate_ref.shape[2]
-    weights = []
-    spread = lax.broadcasted_iota(jnp.int32, (tokens, local * cap), 1)
-    put = None
-    for e in range(local):
-        slot = lax.broadcasted_iota(jnp.int32, (cap, tokens), 0)
-        hit = slot == srow_ref[0, e : e + 1, :]
-        pick_ref[pl.ds(e * cap, cap), :] = jnp.where(hit, 1.0, 0.0).astype(BF)
-        weights.append(
-            jnp.sum(jnp.where(hit, grow_ref[0, e : e + 1, :], 0.0), axis=1, keepdims=True)
-        )
-        own = scol_ref[0, :, e : e + 1]
-        here = spread == jnp.where(own < 0, -1, own + e * cap)
-        put = here if put is None else put | here
-    put_ref[...] = jnp.where(put, 1.0, 0.0).astype(BF)
-
-    def gather(j, _):
+def remote(src, dst, ss, rs, axis, dev):
+    return pltpu.make_async_remote_copy(
+        src_ref=src, dst_ref=dst, send_sem=ss, recv_sem=rs, device_id={axis: dev},
+        device_id_type=pl.DeviceIdType.MESH,
+    )
+
+
+def moe_kernel(cap, tile, n,
+               x_hbm, cot_hbm, cotl_hbm, cotr_hbm, meta_hbm, gate_hbm, up_hbm, down_hbm,
+               dn_out, dw_out, py_out, grads_out, xall, cotall,
+               gate_ref, up_ref, down_ref, x_ref, cot_ref, metas, xs_ref, dy_ref, hb_ref, dg_ref,
+               du_ref, pdn_ref, py_ref, dws, pick_ref, put_ref, ys_ref, acc_ref, stage,
+               wsem, lsem, xs_send, xs_recv, cs_send, cs_recv, m_send, m_recv, dn_send, dn_recv,
+               dw_send, dw_recv, py_sem, own_sem, st_sem):
+    me = lax.axis_index("expert")
+    tokens, width = x_ref.shape
+    local, _, hidden = gate_ref.shape
+    edge = (me == 0) | (me == n - 1)
+
+    barrier = pltpu.get_barrier_semaphore()
+    for d in range(1, n):
+        pl.semaphore_signal(barrier, inc=1, device_id={"expert": lax.rem(me + d, n)},
+                            device_id_type=pl.DeviceIdType.MESH)
+    pl.semaphore_wait(barrier, n - 1)
+
+    def exists(direction, step):
+        return (me - 1 - step >= 0) if direction == 0 else (me + 1 + step <= n - 1)
+
+    def sends(direction, step):
+        if direction == 0:
+            return (me - step >= 0) & (me < n - 1)
+        return (me + step <= n - 1) & (me > 0)
+
+    def stream(direction, step, own, table, ss, rs, near=None):
+        block = me - step if direction == 0 else me + step
+        block = jnp.clip(block, 0, n - 1)
+        target = jnp.clip(me + 1 if direction == 0 else me - 1, 0, n - 1)
+        if step == 0:
+            src = own
+        elif step == 1 and near is not None:
+            src = near[direction]
+        else:
+            src = table.at[block]
+        return remote(src, table.at[block], ss.at[direction, step], rs.at[direction, step],
+                      "expert", target)
+
+    xcopy = lambda d, s: stream(d, s, x_hbm, xall, xs_send, xs_recv)
+    ccopy = lambda d, s: stream(d, s, cot_hbm, cotall, cs_send, cs_recv, (cotl_hbm, cotr_hbm))
+
+    for d in range(2):
+        @pl.when(sends(d, 0))
+        def _():
+            xcopy(d, 0).start()
+
+    def meta_copy(j):
+        return remote(meta_hbm.at[j], metas.at[me], m_send.at[j], m_recv.at[me], "expert", j)
+
+    for j in range(n):
+        @pl.when(me != j)
+        def _():
+            meta_copy(j).start()
+
+    loads = [pltpu.make_async_copy(a, b, wsem.at[k]) for k, (a, b) in enumerate(
+        ((gate_hbm, gate_ref), (up_hbm, up_ref), (down_hbm, down_ref)))]
+    for load in loads:
+        load.start()
+    own_meta = pltpu.make_async_copy(meta_hbm.at[me], metas.at[me], lsem.at[2])
+    own_meta.start()
+
+    def fetch(a, b):
+        cx = pltpu.make_async_copy(a, x_ref, lsem.at[0])
+        cc = pltpu.make_async_copy(b, cot_ref, lsem.at[1])
+        cx.start()
+        cc.start()
+        cx.wait()
+        cc.wait()
+
+    mirror = me >= 2
+    side = jnp.where(mirror, n - 1 - me, me)
+
+    def source_of(p):
+        base = jnp.where(p == 0, side, jnp.where(p == 1, 1 - side, p))
+        return jnp.where(mirror, n - 1 - base, base)
+
+    def arrive(direction, step):
+        @pl.when(exists(direction, step))
+        def _():
+            xcopy(direction, step).wait_recv()
+            if step > 0:
+                ccopy(direction, step).wait_recv()
+
+    def forward(direction, step):
+        @pl.when(sends(direction, step))
+        def _():
+            xcopy(direction, step).start()
+            ccopy(direction, step).start()
+
+    def one_source(p, _):
+        src = source_of(p)
+
+        @pl.when(p == 0)
+        def _():
+            fetch(x_hbm, cot_hbm)
+            own_meta.wait()
+            for load in loads:
+                load.wait()
+
+        @pl.when(p == 1)
+        def _():
+            for d in range(2):
+                arrive(d, 0)
+                forward(d, 1)
+
+        @pl.when(((p == 2) & edge) | ((p == 3) & jnp.logical_not(edge)))
+        def _():
+            for d in range(2):
+                arrive(d, 1)
+                forward(d, 2)
+
+        @pl.when((p == 3) & edge)
+        def _():
+            for d in range(2):
+                arrive(d, 2)
+
+        @pl.when((p > 0) & (src == me - 1))
+        def _():
+            fetch(xall.at[src], cotl_hbm)
+
+        @pl.when((p > 0) & (src == me + 1))
+        def _():
+            fetch(xall.at[src], cotr_hbm)
+
+        @pl.when((src < me - 1) | (src > me + 1))
+        def _():
+            fetch(xall.at[src], cotall.at[src])
+
+        @pl.when(p > 0)
+        def _():
+            remote(meta_hbm.at[src], metas.at[src], m_send.at[src], m_recv.at[src], "expert",
+                   src).wait_recv()
+
+        meta = metas[src]
+        columns = meta.T
+        spread = lax.broadcasted_iota(jnp.int32, (tokens, local * cap), 1).astype(F32)
+        slot = lax.broadcasted_iota(jnp.int32, (cap, tokens), 0).astype(F32)
+        weights, put = [], None
+        for e in range(local):
+            hit = slot == meta[e : e + 1, :]
+            pick_ref[pl.ds(e * cap, cap), :] = jnp.where(hit, 1.0, 0.0).astype(BF)
+            weights.append(
+                jnp.sum(jnp.where(hit, meta[local + e : local + e + 1, :], 0.0), axis=1,
+                        keepdims=True)
+            )
+            own = columns[:, e : e + 1]
+            here = spread == jnp.where(own < 0.0, -1.0, own + e * cap)
+            put = here if put is None else put | here
+        put_ref[...] = jnp.where(put, 1.0, 0.0).astype(BF)
+        mine = pl.ds(pl.multiple_of(p * cap, cap), cap)
+        buf = lax.rem(p, 2)
+
+        def gather(j, _):
+            cols = pl.ds(pl.multiple_of(j * tile, tile), tile)
+            xs = mm(pick_ref[...], x_ref[:, cols]).astype(BF)
+            cg = mm(pick_ref[...], cot_ref[:, cols])
+            for e in range(local):
+                rows = slice(e * cap, (e + 1) * cap)
+                xs_ref[e, mine, cols] = xs[rows]
+                dy_ref[e, mine, cols] = (weights[e] * cg[rows]).astype(BF)
+            return 0
+
+        lax.fori_loop(0, width // tile, gather, 0)
+
+        def middle(j, _):
+            cols = pl.ds(pl.multiple_of(j * tile, tile), tile)
+            for e in range(local):
+                g = mm(xs_ref[e, mine, :], gate_ref[e, :, cols])
+                u = mm(xs_ref[e, mine, :], up_ref[e, :, cols])
+                dh = mm(dy_ref[e, mine, :], down_ref[e, :, cols])
+                s = 1.0 / (1.0 + jnp.exp(-g))
+                act = g * s
+                hb_ref[e, mine, cols] = (act * u).astype(BF)
+                dg_ref[e, mine, cols] = (dh * u * (s * (1.0 + g * (1.0 - s)))).astype(BF)
+                du_ref[e, mine, cols] = (dh * act).astype(BF)
+            return 0
+
+        lax.fori_loop(0, hidden // tile, middle, 0)
+
+        @pl.when(p >= 2)
+        def _():
+            pltpu.make_async_copy(py_ref.at[buf], py_out.at[0], py_sem.at[buf]).wait()
+            @pl.when(p == 2)
+            def _():
+                pltpu.make_async_copy(pdn_ref.at[buf], dn_out.at[me], own_sem.at[0]).wait()
+            @pl.when(p == 3)
+            def _():
+                earlier = source_of(1)
+                remote(pdn_ref.at[buf], dn_out.at[me], dn_send.at[earlier], dn_recv.at[me],
+                       "expert", earlier).wait_send()
+
+        acc_ref[...] = jnp.zeros_like(acc_ref)
+
+        def back(j, _):
+            cols = pl.ds(pl.multiple_of(j * tile, tile), tile)
+            for e in range(local):
+                dxs = mm_nt(dg_ref[e, mine, :], gate_ref[e, cols, :])
+                dxs = dxs + mm_nt(du_ref[e, mine, :], up_ref[e, cols, :])
+                ys_ref[pl.ds(e * cap, cap), :] = dxs.astype(BF)
+            pdn_ref[buf, :, cols] = mm(put_ref[...], ys_ref[...]).astype(BF)
+            return 0
+
+        lax.fori_loop(0, width // tile, back, 0)
+
+        @pl.when(p == 0)
+        def _():
+            pltpu.make_async_copy(pdn_ref.at[buf], dn_out.at[me], own_sem.at[0]).start()
+
+        @pl.when(p > 0)
+        def _():
+            remote(pdn_ref.at[buf], dn_out.at[me], dn_send.at[src], dn_recv.at[me], "expert",
+                   src).start()
+
+        def ahead(j, _):
+            cols = pl.ds(pl.multiple_of(j * tile, tile), tile)
+            for e in range(local):
+                rows = pl.ds(e * cap, cap)
+                y = mm_nt(hb_ref[e, mine, :], down_ref[e, cols, :])
+                acc_ref[rows, :] += mm(pick_ref[rows, :], cot_ref[:, cols]) * y
+                ys_ref[rows, :] = (weights[e] * y).astype(BF)
+            py_ref[buf, :, cols] = mm(put_ref[...], ys_ref[...]).astype(BF)
+            return 0
+
+        lax.fori_loop(0, width // tile, ahead, 0)
+        pltpu.make_async_copy(py_ref.at[buf], py_out.at[src], py_sem.at[buf]).start()
+        dws[p] = jnp.zeros((8, tokens), F32)
+        for e in range(local):
+            dot = jnp.sum(acc_ref[pl.ds(e * cap, cap), :], axis=1, keepdims=True)
+            hit = slot == meta[e : e + 1, :]
+            dws[p, e : e + 1, :] = jnp.sum(jnp.where(hit, dot, 0.0), axis=0, keepdims=True)
+
+        @pl.when(p == 0)
+        def _():
+            pltpu.make_async_copy(dws.at[p], dw_out.at[me], own_sem.at[1]).start()
+
+        @pl.when(p > 0)
+        def _():
+            remote(dws.at[p], dw_out.at[me], dw_send.at[src], dw_recv.at[me], "expert",
+                   src).start()
+        return 0
+
+    lax.fori_loop(0, n, one_source, 0)
+
+    tiles = width // tile
+    store = lambda k, e, j: pltpu.make_async_copy(
+        stage.at[k], grads_out.at[e, pl.ds(pl.multiple_of(j * tile, tile), tile), :], st_sem.at[k])
+
+    def weight_grads(k, _):
+        e, j = lax.div(k, tiles), lax.rem(k, tiles)
         cols = pl.ds(pl.multiple_of(j * tile, tile), tile)
-        xs = mm(pick_ref[...], x_ref[0, :, cols]).astype(BF)
-        cg = mm(pick_ref[...], cot_ref[0, :, cols])
-        cg_ref[:, cols] = cg.astype(BF)
-        for e in range(local):
-            rows = slice(e * cap, (e + 1) * cap)
-            xs_ref[0, e, :, cols] = xs[rows]
-            dy_ref[0, e, :, cols] = (weights[e] * cg[rows]).astype(BF)
+        slot_k = lax.rem(k, 2)
+
+        @pl.when(k >= 2)
+        def _():
+            store(slot_k, 0, 0).wait()
+
+        xs = xs_ref[e, :, cols]
+        stage[slot_k, :, 0:hidden] = mm_tn(xs, dg_ref[e]).astype(BF)
+        stage[slot_k, :, hidden : 2 * hidden] = mm_tn(xs, du_ref[e]).astype(BF)
+        stage[slot_k, :, 2 * hidden : 3 * hidden] = mm_tn(dy_ref[e, :, cols], hb_ref[e]).astype(BF)
+        store(slot_k, e, j).start()
         return 0
 
-    lax.fori_loop(0, width // tile, gather, 0)
-
-    def middle(j, _):
-        cols = pl.ds(pl.multiple_of(j * tile, tile), tile)
-        for e in range(local):
-            g = mm(xs_ref[0, e], gate_ref[e, :, cols])
-            u = mm(xs_ref[0, e], up_ref[e, :, cols])
-            dh = mm(dy_ref[0, e], down_ref[e, :, cols])
-            s = 1.0 / (1.0 + jnp.exp(-g))
-            act = g * s
-            hb_ref[0, e, :, cols] = (act * u).astype(BF)
-            dg_ref[0, e, :, cols] = (dh * u * (s * (1.0 + g * (1.0 - s)))).astype(BF)
-            du_ref[0, e, :, cols] = (dh * act).astype(BF)
-        return 0
-
-    lax.fori_loop(0, hidden // tile, middle, 0)
-
-    acc_ref[...] = jnp.zeros_like(acc_ref)
-
-    def finish(j, _):
-        cols = pl.ds(pl.multiple_of(j * tile, tile), tile)
-        for e in range(local):
-            rows = pl.ds(e * cap, cap)
-            y = mm_nt(hb_ref[0, e], down_ref[e, cols, :])
-            acc_ref[rows, :] += cg_ref[rows, cols].astype(F32) * y
-            ys_ref[rows, :] = (weights[e] * y).astype(BF)
-        py_ref[0, :, cols] = mm(put_ref[...], ys_ref[...]).astype(BF)
-        for e in range(local):
-            rows = pl.ds(e * cap, cap)
-            dxs = mm_nt(dg_ref[0, e], gate_ref[e, cols, :])
-            dxs = dxs + mm_nt(du_ref[0, e], up_ref[e, cols, :])
-            ys_ref[rows, :] = dxs.astype(BF)
-        pdn_ref[0, :, cols] = mm(put_ref[...], ys_ref[...]).astype(BF)
-        return 0
-
-    lax.fori_loop(0, width // tile, finish, 0)
-    for e in range(local):
-        dot = jnp.sum(acc_ref[pl.ds(e * cap, cap), :], axis=1, keepdims=True)
-        slot = lax.broadcasted_iota(jnp.int32, (cap, tokens), 0)
-        hit = slot == srow_ref[0, e : e + 1, :]
-        dw_ref[0, e : e + 1, :] = jnp.sum(jnp.where(hit, dot, 0.0), axis=0, keepdims=True)
-
-
-def expert_block(x, cot, srow, scol, grow, gate, up, down, cap):
-    n, tokens, width = x.shape
+    lax.fori_loop(0, local * tiles, weight_grads, 0)
+    for k in range(2):
+        store(k, 0, 0).wait()
+
+    for k in range(2):
+        pltpu.make_async_copy(py_ref.at[k], py_out.at[0], py_sem.at[k]).wait()
+    pltpu.make_async_copy(dws.at[0], dw_out.at[me], own_sem.at[1]).wait()
+    for d in range(2):
+        for s in range(n - 1):
+            @pl.when(sends(d, s))
+            def _():
+                xcopy(d, s).wait_send()
+                if s > 0:
+                    ccopy(d, s).wait_send()
+    last = [source_of(p) for p in range(n)]
+    for p in (2, 3):
+        remote(pdn_ref.at[p % 2], dn_out.at[me], dn_send.at[last[p]], dn_recv.at[me], "expert",
+               last[p]).wait_send()
+    for j in range(n):
+        @pl.when(me != j)
+        def _():
+            meta_copy(j).wait_send()
+            remote(dws.at[0], dw_out.at[me], dw_send.at[j], dw_recv.at[me], "expert",
+                   j).wait_send()
+            remote(dws.at[0], dw_out.at[j], dw_send.at[j], dw_recv.at[j], "expert", j).wait_recv()
+            remote(pdn_ref.at[0], dn_out.at[j], dn_send.at[j], dn_recv.at[j], "expert",
+                   j).wait_recv()
+
+
+def moe(x, cot, cot_left, cot_right, meta, gate, up, down, cap):
+    n = meta.shape[0]
+    tokens, width = x.shape
     local, _, hidden = gate.shape
     tile = 256
-    by_source = lambda s: (s, 0, 0)
-    by_source4 = lambda s: (s, 0, 0, 0)
-    const3 = lambda s: (0, 0, 0)
-    weight_spec = pl.BlockSpec((local, width, hidden), const3, pipeline_mode=pl.Buffered(1))
-    slot_in = lambda d: jax.ShapeDtypeStruct((n, local, cap, d), BF)
-    slot_spec = lambda d: pl.BlockSpec((1, local, cap, d), by_source4)
+    anywhere = pl.BlockSpec(memory_space=pl.ANY)
+    dma = pltpu.SemaphoreType.DMA
+    shape = jax.ShapeDtypeStruct
     return pl.pallas_call(
-        functools.partial(expert_kernel, cap, tile),
+        functools.partial(moe_kernel, cap, tile, n),
         out_shape=(
-            jax.ShapeDtypeStruct((n, tokens, width), BF),
-            jax.ShapeDtypeStruct((n, tokens, width), BF),
-            jax.ShapeDtypeStruct((n, local, tokens), F32),
-            slot_in(width), slot_in(width), slot_in(hidden), slot_in(hidden), slot_in(hidden),
-        ),
-        grid=(n,),
-        in_specs=[
-            pl.BlockSpec((1, tokens, width), by_source),
-            pl.BlockSpec((1, tokens, width), by_source),
-            pl.BlockSpec((1, local, tokens), by_source),
-            pl.BlockSpec((1, tokens, local), by_source),
-            pl.BlockSpec((1, local, tokens), by_source),
-            weight_spec, weight_spec, weight_spec,
+            shape((n, tokens, width), BF), shape((n, 8, tokens), F32), shape((n, tokens, width), BF),
+            shape((local, width, 3 * hidden), BF),
+            shape((n, tokens, width), BF), shape((n, tokens, width), BF),
+        ),
+        in_specs=[anywhere] * 8,
+        out_specs=[anywhere] * 6,
+        scratch_shapes=[
+            pltpu.VMEM((local, width, hidden), BF), pltpu.VMEM((local, width, hidden), BF),
+            pltpu.VMEM((local, width, hidden), BF),
+            pltpu.VMEM((tokens, width), BF), pltpu.VMEM((tokens, width), BF),
+            pltpu.VMEM((n, 8, tokens), F32),
+            pltpu.VMEM((local, n * cap, width), BF), pltpu.VMEM((local, n * cap, width), BF),
+            pltpu.VMEM((local, n * cap, hidden), BF), pltpu.VMEM((local, n * cap, hidden), BF),
+            pltpu.VMEM((local, n * cap, hidden), BF),
+            pltpu.VMEM((2, tokens, width), BF), pltpu.VMEM((2, tokens, width), BF),
+            pltpu.VMEM((n, 8, tokens), F32),
+            pltpu.VMEM((local * cap, tokens), BF), pltpu.VMEM((tokens, local * cap), BF),
+            pltpu.VMEM((local * cap, tile), BF), pltpu.VMEM((local * cap, tile), F32),
+            pltpu.VMEM((2, tile, 3 * hidden), BF),
+            dma((3,)), dma((3,)), dma((2, n - 1)), dma((2, n - 1)), dma((2, n - 1)),
+            dma((2, n - 1)), dma((n,)), dma((n,)), dma((n,)), dma((n,)), dma((n,)), dma((n,)),
+            dma((2,)), dma((2,)), dma((2,)),
         ],
-        out_specs=[
-            pl.BlockSpec((1, tokens, width), by_source),
-            pl.BlockSpec((1, tokens, width), by_source),
-            pl.BlockSpec((1, local, tokens), by_source),
-            slot_spec(width), slot_spec(width), slot_spec(hidden), slot_spec(hidden),
-            slot_spec(hidden),
-        ],
-        scratch_shapes=[
-            pltpu.VMEM((local * cap, tokens), BF),
-            pltpu.VMEM((tokens, local * cap), BF),
-            pltpu.VMEM((local * cap, width), BF),
-            pltpu.VMEM((local * cap, tile), BF),
-            pltpu.VMEM((local * cap, tile), F32),
-        ],
-        compiler_params=pltpu.CompilerParams(vmem_limit_bytes=VMEM_LIMIT),
+        compiler_params=pltpu.CompilerParams(
+            vmem_limit_bytes=MOE_VMEM, collective_id=1, has_side_effects=True
+        ),
         cost_estimate=pl.CostEstimate(
-            flops=2 * n * local * cap * width * (6 * hidden + 4 * tokens),
+            flops=2 * n * local * cap * width * (9 * hidden + 5 * tokens),
             transcendentals=n * local * cap * hidden,
-            bytes_accessed=2 * (4 * n * tokens * width + 3 * local * width * hidden),
-        ),
-        name="experts",
-    )(x, cot, srow, scol, grow, gate, up, down)
-
-
-def expert_grad_kernel(xs_ref, dy_ref, hb_ref, dg_ref, du_ref, out_ref):
-    n, _, cap, tile = xs_ref.shape
-    hidden = hb_ref.shape[3]
-    flat = lambda ref: ref[...].reshape(n * cap, ref.shape[3])
-    xs = flat(xs_ref)
-    out_ref[0, :, 0:hidden] = mm_tn(xs, flat(dg_ref)).astype(BF)
-    out_ref[0, :, hidden : 2 * hidden] = mm_tn(xs, flat(du_ref)).astype(BF)
-    out_ref[0, :, 2 * hidden : 3 * hidden] = mm_tn(flat(dy_ref), flat(hb_ref)).astype(BF)
-
-
-def expert_grads(xs, dy, hb, dg, du):
-    n, local, cap, width = xs.shape
-    hidden = hb.shape[3]
-    tile = 256
-    wide = pl.BlockSpec((n, 1, cap, tile), lambda e, j: (0, e, 0, j))
-    deep = pl.BlockSpec((n, 1, cap, hidden), lambda e, j: (0, e, 0, 0))
-    return pl.pallas_call(
-        expert_grad_kernel,
-        out_shape=jax.ShapeDtypeStruct((local, width, 3 * hidden), BF),
-        grid=(local, width // tile),
-        in_specs=[wide, wide, deep, deep, deep],
-        out_specs=pl.BlockSpec((1, tile, 3 * hidden), lambda e, j: (e, j, 0)),
-        compiler_params=pltpu.CompilerParams(vmem_limit_bytes=VMEM_LIMIT),
-        cost_estimate=pl.CostEstimate(
-            flops=6 * n * local * cap * width * hidden,
-            transcendentals=0,
-            bytes_accessed=2 * n * local * cap * (2 * width + 3 * hidden),
-        ),
-        name="expert_grads",
-    )(xs, dy, hb, dg, du)
+            bytes_accessed=2 * (8 * n * tokens * width + 6 * local * width * hidden),
+        ),
+        name="moe",
+    )(x, cot, cot_left, cot_right, meta, gate, up, down)
+
+
+RIGHT = [(0, 1), (1, 2), (2, 3)]
+LEFT = [(1, 0), (2, 1), (3, 2)]
 
 
 def body(
@@ -449,14 +641,14 @@
 ):
     context_index = lax.axis_index("context")
     expert_size = lax.axis_size("expert")
-    expert_index = lax.axis_index("expert")
     rows = tokens.shape[1]
     length = segment_ids.shape[1]
     kv_width = KEY_VALUE_HEADS * HEAD_SIZE
     gather = lambda w: lax.all_gather(w, "context", axis=0, tiled=True)
 
     upstream_low = cotangent[0]
-    cot_all = lax.all_gather(upstream_low, "expert", axis=0)
+    cot_left = lax.ppermute(upstream_low, "expert", RIGHT)
+    cot_right = lax.ppermute(upstream_low, "expert", LEFT)
 
     expert_count = router_weight.shape[1]
     local = gate_weight.shape[0]
@@ -471,8 +663,6 @@
     slots = jnp.sum((order[:, :, None] < order[:, None, :]).astype(jnp.int32), axis=1)
     kept = routed.T & (slots < capacity)
     slots = jnp.where(kept, slots, -1)
-    slots_all = lax.all_gather(slots, "expert", axis=0)
-    slots_mine = lax.dynamic_slice_in_dim(slots_all, expert_index * local, local, axis=1)
     kept_float = kept.T.astype(F32)
 
     query_full, key_full, value_full, output_full, router_full, gain_first, gain_second = (
@@ -512,29 +702,26 @@
     gates = jax.nn.softmax(jnp.where(routed, logits, -jnp.inf), axis=-1)
     kept_gates = gates * kept_float
 
-    x_all = lax.all_gather(expert_input, "expert", axis=0)
-    gates_all = lax.all_gather(kept_gates.T, "expert", axis=0)
-    gates_mine = lax.dynamic_slice_in_dim(gates_all, expert_index * local, local, axis=1)
-    part_y, part_dn, dw, xs, dy, hb, dg, du = expert_block(
-        x_all, cot_all, slots_mine, slots_mine.transpose(0, 2, 1), gates_mine,
-        gate_weight, up_weight, down_weight, cap,
-    )
-    scatter = lambda v: lax.psum_scatter(v, "expert", scatter_dimension=0, tiled=False)
-    dn_low = scatter(part_dn)
-    dw_back = lax.all_to_all(dw, "expert", split_axis=0, concat_axis=0, tiled=True)
-    gate_dot = dw_back.reshape(expert_count, rows).T * kept_float
-    grads_low = expert_grads(xs, dy, hb, dg, du)
+    routing = jnp.stack([slots.astype(F32), kept_gates.T], axis=0)
+    routing = routing.reshape(2, expert_size, local, rows).transpose(1, 0, 2, 3)
+    routing = routing.reshape(expert_size, 2 * local, rows)
+    routing = jnp.pad(routing, ((0, 0), (0, 8 - 2 * local), (0, 0)))
+    dn_parts, dw_parts, part_y, grads_low, _, _ = moe(
+        expert_input, upstream_low, cot_left, cot_right, routing, gate_weight, up_weight,
+        down_weight, cap,
+    )
+    gate_dot = dw_parts[:, :local].reshape(expert_count, rows).T * kept_float
+    y_parts = lax.all_to_all(part_y, "expert", split_axis=0, concat_axis=0, tiled=True)
+    layer_out = (hidden + jnp.sum(y_parts.astype(F32), axis=0)).astype(BF)
     grads_shard = lax.psum_scatter(
         grads_low, ("dp", "context"), scatter_dimension=1, tiled=True
     ).astype(F32)
     ff = gate_weight.shape[2]
     gate_grad, up_grad, down_grad = (grads_shard[:, :, i * ff : (i + 1) * ff] for i in range(3))
-    mixture = scatter(part_y)
-    layer_out = (hidden + mixture.astype(F32)).astype(BF)
 
     upstream = upstream_low.astype(F32)
     logit_grad = gates * (gate_dot - jnp.sum(gates * gate_dot, axis=-1, keepdims=True))
-    normed_grad = dn_low.astype(F32) + precise_dims(logit_grad, router_float, ((1,), (1,)))
+    normed_grad = jnp.sum(dn_parts.astype(F32), axis=0) + precise_dims(logit_grad, router_float, ((1,), (1,)))
     router_local = precise_dims(normed, logit_grad, ((0,), (0,)))
     hidden_total = upstream + norm_back(hidden, root_second, gain_second, normed_grad)
     gain_second_grad = jnp.sum(normed_grad * hidden * root_second, axis=0)

time: 1090 us -> 998 us (0.916)
  waiting for transfers between devices: 619 us -> 394 us
  Pallas kernels: 168 us -> 333 us
  blocking collectives: 132 us -> 91.6 us
    reduce_scatter x2 -> x0, waiting for transfers between devices: 203 us -> none  [body(): lax.psum_scatter(v, 'expert', scatter_dimension=0, tiled=False)]
    pallas_call x2 -> x1, Pallas kernels: 120 us -> 285 us  [moe(): pl.pallas_call(functools.partial(moe_kernel, cap, tile, n), out_shape=(sh...]
    all_gather x2 -> x0, waiting for transfers between devices: 156 us -> none  [the longest x1 116 us: body(): x_all = lax.all_gather(expert_input, 'expert', axis=0)]
    all_to_all x1, waiting for transfers between devices: 5.99 us -> 128 us  [body(): lax.all_to_all(part_y, 'expert', split_axis=0, concat_axis=0, tiled=True)]
    all_gather x2 -> x0, blocking collectives: 31.3 us -> none  [the longest x1 16 us: body(): slots_all = lax.all_gather(slots, 'expert', axis=0)]
    reduce_scatter x5, waiting for transfers between devices: 0.08 us -> 26.8 us  [body(): lax.psum_scatter(v.astype(BF), 'context', scatter_dimension=0, tiled=True)]
    all_gather x3, waiting for transfers between devices: 12.7 us -> 0.01 us  [body(): gather = lambda w: lax.all_gather(w, 'context', axis=0, tiled=True)]
  transfers between devices with their start and end apart: 16 -> 14, of which waited for: 9 -> 6; matrix products, arithmetic and copies ran while one was open for 9% -> 10% of each run, Pallas kernels for 5% -> 2%
where the time goes in v2:
time: 998 us; the launch traced here: 993 us
  waiting for transfers between devices  394 us (39%)
  Pallas kernels  333 us (33%)
  blocking collectives  91.6 us (9%)
  matrix products  54.9 us (6%)
  other arithmetic  51.4 us (5%)
  local copies, waits for them, and re-layouts  32.5 us (3%)
  between operations  21 us (2%)
  starting transfers between devices  14.4 us (1%)
    pallas_call x1, Pallas kernels, moe(): pl.pallas_call(functools.partial(moe_kernel, cap, tile, n), out_shape=(sh...  285 us
    psum x1, waiting for transfers between devices, body(): lax.psum(lax.psum_scatter(v.astype(BF), 'context', scatter_dimension=0, t...  200 us
    all_to_all x1, waiting for transfers between devices, body(): lax.all_to_all(part_y, 'expert', split_axis=0, concat_axis=0, tiled=True)  128 us
    psum x1, blocking collectives, body(): lax.psum(lax.psum_scatter(v.astype(BF), 'context', scatter_dimension=0, t...  78.1 us
    pallas_call x1, Pallas kernels, attention_backward(): pl.pallas_call(functools.partial(attn_bwd_kernel, kb, tq), out_shape=(jax...  27.2 us
    reduce_scatter x5, waiting for transfers between devices, body(): lax.psum_scatter(v.astype(BF), 'context', scatter_dimension=0, tiled=True)  26.8 us
    pallas_call x1, Pallas kernels, attention_forward(): pl.pallas_call(functools.partial(attn_fwd_kernel, kb, tq), out_shape=(jax...  20.8 us
    dot_general x4, matrix products, mm_tn(): lax.dot_general(a, b, (((0,), (0,)), ((), ())), preferred_element_type=F32)  20.5 us
  transfers between devices with their start and end apart: 14, of which 6 were waited for; matrix products, arithmetic and copies ran while one was open for 10% of the time, Pallas kernels for 2%

profile of v2, /device:TPU:0, one launch (start us, length us, event | category | flops | bytes accessed | tf_op | source)
XLA Modules:
  0.0 993.4 jit_solution(6321702386246225535)
XLA Ops:
  7.3 1.9 fusion.6
  10.5 1.9 all-gather
  12.4 2.6 all_gather.26
  15.0 2.6 all_gather.27
  17.6 1.2 copy.100
  18.7 1.3 convolution_convert_fusion.5
  20.1 1.5 fusion.24
  21.6 1.8 fusion.38
  23.6 1.1 subtract_convert_fusion.1
  24.9 1.8 pad_maximum_fusion.2
  28.3 1.3 collective-permute-start.1
  29.6 6.6 collective-permute-start
  36.8 2.0 fusion.48
  43.9 1.8 all-gather.1
  48.0 1.0 convert_reduce_fusion.2
  50.3 1.0 copy.106.segk_ref
  51.9 2.1 all_gather.31
  54.6 2.2 fusion.56
  56.9 6.6 copy.96
  63.5 5.0 fusion.26
  69.2 1.6 copy.105.q_ref
  70.8 20.8 %attn_fwd.1 = (bf16[512,1536]{1,0:T(8,128)(2,1)}, f32[12,1,512]{2,1,0:T(1,128)}) custom-call(s32[5]{0:T(128)} %stack.32.meta, bf16[512,1536]{1,0:T(8,128)(2,1)} %copy.105.q_ref, bf16[1024,256]{1,0:T(8,128)(2,1)} %get-tuple-element.55.k_ref, bf16[1024,256]{1,0:T(8,128)(2,1)} %get-tuple-element.54.v_ref, s32[1024,1]{1,0:T(8,128)} %copy.106.segk_ref, ...), custom_call_target="tpu_custom_call" | custom-call | flops 2415919104 | bytes 3145728 | tf_op jit(solution)/shard_map/attn_fwd/pallas_call | solution.py:200
  91.6 6.0 multiply_reduce_fusion.2
  98.3 1.8 fusion.46
  101.3 1.3 stack.34
  102.6 1.4 maximum_bitcast_fusion
  104.0 1.4 reshape.216
  105.4 1.4 pad.4.meta_hbm
  106.8 2.2 fusion.20.x_hbm
  108.9 285.2 %moe.1 = (bf16[4,512,1536]{2,1,0:T(8,128)(2,1)}, f32[4,8,512]{2,1,0:T(8,128)}, bf16[4,512,1536]{2,1,0:T(8,128)(2,1)}, bf16[2,1536,2304]{2,1,0:T(8,128)(2,1)}, bf...) custom-call(bf16[512,1536]{1,0:T(8,128)(2,1)} %fusion.20.x_hbm, bf16[512,1536]{1,0:T(8,128)(2,1)} %bitcast.140, ...), custom_call_target="tpu_custom_call" | custom-call | flops 74490839040 | bytes 78643200 | tf_op jit(solution)/shard_map/moe/pallas_call | solution.py:595
  394.2 5.8 all-to-all-start
  400.1 1.0 pad_maximum_fusion.4
  401.1 0.8 slice.48
  402.1 4.2 convert_reduce_fusion
  406.5 4.4 multiply_reduce_fusion
  410.8 127.7 %all-to-all-done = bf16[4,512,1536]{2,1,0:T(8,128)(2,1)} async-done(((bf16[4,512,1536]{2,1,0:T(8,128)(2,1)}), bf16[4,512,1536]{2,1,0:T(8,128)(2,1)}, u32[]{:S(2)}, u32[]{:S(2)}) %all-to-all-start) | async-done | bytes 6291488 | tf_op jit(solution)/shard_map/all_to_all | solution.py:714
  538.5 4.3 convert_reduce_fusion.1
  542.9 2.2 subtract_add_fusion
  545.1 3.8 convolution_convert_fusion.2.do_ref
  548.9 27.2 %attn_bwd.1 = (bf16[512,1536]{1,0:T(8,128)(2,1)}, bf16[1024,256]{1,0:T(8,128)(2,1)}, bf16[1024,256]{1,0:T(8,128)(2,1)}) custom-call(s32[5]{0:T(128)} %stack.32.meta, bf16[512,1536]{1,0:T(8,128)(2,1)} %copy.105.q_ref, bf16[1024,256]{1,0:T(8,128)(2,1)} %get-tuple-element.55.k_ref, bf16[1024,256]{1,0:T(8,128)(2,1)} %get-tuple-element.54.v_ref, ...), custom_call_target="tpu_custom_call" | custom-call | flops 6442450944 | bytes 6291456 | tf_op jit(solution)/shard_map/attn_bwd/pallas_call | solution.py:242
  576.1 2.2 pad_maximum_fusion.1
  578.4 18.5 %reduce-scatter.8.cloned.1.call-done = bf16[512,512]{1,0:T(8,128)(2,1)} async-done(((bf16[1024,512]{1,0:T(8,128)(2,1)}), bf16[512,512]{1,0:T(8,128)(2,1)}) %reduce-scatter.8.cloned.1.call-update) | async-done | bytes 524304 | tf_op jit(solution)/shard_map/reduce_scatter | solution.py:735
  596.9 3.1 convolution_convert_fusion.3
  601.2 1.8 slice_convert_fusion
  602.9 2.0 copy.117
  605.0 1.2 multiply_subtract_fusion
  606.1 3.3 convolution_convert_fusion.4
  609.5 7.2 convolution_convert_fusion
  617.4 6.8 convolution_convert_fusion.1
  625.0 2.6 fusion.21
  628.4 10.1 %reduce-scatter.16.cloned.1.call-done = bf16[768,1536]{1,0:T(8,128)(2,1)} async-done(((bf16[1536,1536]{1,0:T(8,128)(2,1)}), bf16[768,1536]{1,0:T(8,128)(2,1)}) %reduce-scatter.16.cloned.1.call-update) | async-done | bytes 2359312 | tf_op jit(solution)/shard_map/reduce_scatter | solution.py:748
  638.5 16.7 %reduce-scatter.10.cloned.1.call-done = bf16[768,1536]{1,0:T(8,128)(2,1)} async-done(((bf16[1536,1536]{1,0:T(8,128)(2,1)}), bf16[768,1536]{1,0:T(8,128)(2,1)}) %reduce-scatter.10.cloned.1.call-update) | async-done | bytes 2359312 | tf_op jit(solution)/shard_map/reduce_scatter | solution.py:748
  656.5 4.6 fusion.57
  662.9 2.8 fusion.15
  665.7 2.5 all-reduce.5
  668.3 78.1 %all-reduce.3 = (bf16[768,8]{0,1:T(8,128)(2,1)S(1)}, bf16[768]{0:T(1024)(128)(2,1)S(1)}, bf16[768]{0:T(1024)(128)(2,1)S(1)}) all-reduce(bf16[768,8]{0,1:T(8,128)(2,1)} %reduce-scatter.18.cloned.1.call-done, bf16[768]{0:T(1024)(128)(2,1)S(1)} %dynamic-slice.4, ...), channel_id=1, replica_groups=mesh['dp'=4,'context'=2,'expert'=4] {'dp','expert'}, use_global_device_ids=true, to_apply=%region_24.25 | all-reduce | flops 7680 | bytes 30720 | tf_op jit(solution)/shard_map/psum | solution.py:747
  748.3 5.8 fusion.23
  754.1 19.0 %reduce-scatter.20.cloned.1.call-done = bf16[2,192,2304]{2,1,0:T(8,128)(2,1)} async-done(((bf16[2,1536,2304]{2,1,0:T(8,128)(2,1)}), bf16[2,192,2304]{2,1,0:T(8,128)(2,1)}) %reduce-scatter.20.cloned.1.call-update) | async-done | bytes 1769488 | tf_op jit(solution)/shard_map/reduce_scatter | solution.py:716
  773.1 3.3 fusion.55
  776.4 200.4 %all-reduce.8.cloned.1.call-done = (bf16[768,1536]{1,0:T(8,128)(2,1)}, bf16[768,256]{1,0:T(8,128)(2,1)}, bf16[768,256]{1,0:T(8,128)(2,1)}, bf16[768,1536]{1,0:T(8,128)(2,1)}) async-done(((bf16[768,1536]{1,0:T(8,128)(2,1)}, bf16[768,256]{1,0:T(8,128)(2,1)}, bf16[768,256]{1,0:T(8,128)(2,1)}, bf16[768,1536]{1,0:T(8,128)(2,1)}), (bf16[768,1536]{1,0:T(8,128)(2,1)}, bf16[768,256]{1,0:T(8,128)(2,1)}, ...) | async-done | bytes 5505040 | tf_op jit(solution)/shard_map/psum | solution.py:747
  976.8 2.1 convert_element_type.174
  978.9 1.9 convert_element_type.176
  980.8 2.8 convert_element_type.172
  983.7 2.8 convert_element_type.178
  (202 shorter events, 18.8 us)
Async XLA Ops:
  7.2 11.6 %copy-start.2 = (bf16[1,512,1536]{2,1,0:T(8,128)(2,1)S(1)}, bf16[1,512,1536]{2,1,0:T(8,128)(2,1)}, u32[]{:S(2)}) copy-start(bf16[1,512,1536]{2,1,0:T(8,128)(2,1)} %param.15) | copy-start | bytes 4718596
  7.2 47.4 %all-gather.8.cloned.1.call-start = ((), (), s32[]{:S(2)}) async-start(), calls=%async_computation.9 | async-start | bytes 1572864 | tf_op jit(solution)/shard_map/all_gather | solution.py:647
  9.8 53.7 %copy-start.52 = (f32[512]{0:T(512)}, f32[512]{0:T(512)S(1)}, u32[]{:S(2)}) copy-start(f32[512]{0:T(512)S(1)} %get-tuple-element.67) | copy-start | bytes 6148
  12.4 51.0 %copy-start.42 = (f32[1536]{0:T(1024)}, f32[1536]{0:T(1024)S(1)}, u32[]{:S(2)}) copy-start(f32[1536]{0:T(1024)S(1)} %reshape.227) | copy-start | bytes 18436
  15.0 5.1 copy-start.6
  17.6 4.0 copy-start.8
  23.4 4.2 copy-start.12
  24.9 11.3 %copy-start.49 = (s32[1,1024]{1,0:T(1,128)S(1)}, s32[1,1024]{1,0:T(1,128)}, u32[]{:S(2)}) copy-start(s32[1,1024]{1,0:T(1,128)} %param.17) | copy-start | bytes 12292
  24.9 19.0 %copy-start.59 = (bf16[768]{0:T(1024)(128)(2,1)S(1)}, bf16[768]{0:T(1024)(128)(2,1)}, u32[]{:S(2)}) copy-start(bf16[768]{0:T(1024)(128)(2,1)} %param.26) | copy-start | bytes 4612
  24.9 22.0 %copy-start.57 = (s32[1,1,2048]{2,1,0:T(1,128)S(1)}, s32[1,1,2048]{2,1,0:T(1,128)}, u32[]{:S(2)}) copy-start(s32[1,1,2048]{2,1,0:T(1,128)} %param.19) | copy-start | bytes 24580
  26.7 21.2 %copy-start.48 = (s32[1,512,4]{1,2,0:T(4,128)S(1)}, s32[1,512,4]{1,2,0:T(4,128)}, u32[]{:S(2)}) copy-start(s32[1,512,4]{1,2,0:T(4,128)} %param.18) | copy-start | bytes 24580
  26.8 25.1 %copy-start.55 = (bf16[768,8]{0,1:T(8,128)(2,1)S(1)}, bf16[768,8]{0,1:T(8,128)(2,1)}, u32[]{:S(2)}) copy-start(bf16[768,8]{0,1:T(8,128)(2,1)} %param.24) | copy-start | bytes 36868
  26.8 30.1 %all-gather.6.cloned.1.call-start = ((), (), s32[]{:S(2)}) async-start(), calls=%async_computation.8 | async-start | bytes 7077888 | tf_op jit(solution)/shard_map/all_gather | solution.py:647
  27.5 64.0 %all-gather.10.cloned.1.call-start = ((), (), s32[]{:S(2)}) async-start(), calls=%async_computation.10 | async-start | bytes 7077888 | tf_op jit(solution)/shard_map/all_gather | solution.py:647
  28.3 80.7 %collective-permute-start.1 = (bf16[512,1536]{1,0:T(8,128)(2,1)}, bf16[512,1536]{1,0:T(8,128)(2,1)}, u32[]{:S(2)}, u32[]{:S(2)}) collective-permute-start(bf16[512,1536]{1,0:T(8,128)(2,1)} %bitcast.138), channel_id=1, source_target_pairs={{1,0},{2,1},{3,2},{5,4},{6,5},{7,6},{9,8},{10,9},{11,10},{13,12},{... | collective-permute-start | bytes 4718600 | tf_op jit(solution)/shard_map/ppermute | solution.py:651
  29.6 79.4 %collective-permute-start = (bf16[512,1536]{1,0:T(8,128)(2,1)}, bf16[512,1536]{1,0:T(8,128)(2,1)}, u32[]{:S(2)}, u32[]{:S(2)}) collective-permute-start(bf16[512,1536]{1,0:T(8,128)(2,1)} %bitcast.139), channel_id=1, source_target_pairs={{0,1},{1,2},{2,3},{4,5},{5,6},{6,7},{8,9},{9,10},{10,11},{12,13},{... | collective-permute-start | bytes 4718600 | tf_op jit(solution)/shard_map/ppermute | solution.py:650
  48.0 15.5 %copy-start.19 = (pred[512,8]{0,1:T(8,128)(4,1)}, pred[512,8]{0,1:T(8,128)(4,1)S(1)}, u32[]{:S(2)}) copy-start(pred[512,8]{0,1:T(8,128)(4,1)S(1)} %fusion.39) | copy-start | bytes 12292
  91.6 6.7 copy-start.20
  91.6 6.7 copy-start.24
  91.6 6.6 copy-start.29
  97.6 11.3 %copy-start = (f32[512,1536]{1,0:T(8,128)}, f32[512,1536]{1,0:T(8,128)S(1)}, u32[]{:S(2)}) copy-start(f32[512,1536]{1,0:T(8,128)S(1)} %get-tuple-element.71) | copy-start | bytes 9437188
  97.6 3.0 copy-start.31
  98.2 1.8 copy-start.35
  394.2 5.9 copy-start.13
  394.2 5.9 copy-start.15
  394.2 7.8 copy-start.21
  394.2 7.8 copy-start.32
  394.2 7.8 copy-start.39
  394.2 7.8 copy-start.45
  394.2 144.2 %all-to-all-start = ((bf16[4,512,1536]{2,1,0:T(8,128)(2,1)}), bf16[4,512,1536]{2,1,0:T(8,128)(2,1)}, u32[]{:S(2)}, u32[]{:S(2)}) async-start(bf16[4,512,1536]{2,1,0:T(8,128)(2,1)} %get-tuple-element.22), calls=%async_computation | async-start | bytes 12582912 | tf_op jit(solution)/shard_map/all_to_all | solution.py:714
  400.1 196.9 %reduce-scatter.8.cloned.1.call-start = ((), (), s32[]{:S(2)}) async-start(), calls=%async_computation.11 | async-start | bytes 1572864 | tf_op jit(solution)/shard_map/reduce_scatter | solution.py:735
  402.0 4.3 copy-start.27
  402.0 4.3 copy-start.50
  402.1 4.3 copy-start.1
  402.1 4.3 copy-start.22
  402.1 4.3 copy-start.25
  402.1 4.3 copy-start.30
  402.1 4.3 copy-start.33
  402.1 4.3 copy-start.36
  402.1 4.3 copy-start.40
  402.1 4.3 copy-start.46
  410.8 132.0 %copy-start.56 = (f32[512]{0:T(512)S(1)}, f32[512]{0:T(512)}, u32[]{:S(2)}) copy-start(f32[512]{0:T(512)} %get-tuple-element.68) | copy-start | bytes 6148
  538.5 4.4 copy-start.5
  538.5 4.4 copy-start.14
  538.5 6.6 slice-start
  542.9 2.2 slice-start.1
  545.1 3.8 copy-start.4
  578.3 22.1 %copy-start.16 = (f32[512,64]{1,0:T(8,128)S(1)}, f32[512,64]{1,0:T(8,128)}, u32[]{:S(2)}) copy-start(f32[512,64]{1,0:T(8,128)} %get-tuple-element.62) | copy-start | bytes 393220
  578.3 50.1 %reduce-scatter.14.cloned.1.call-start = ((), (), s32[]{:S(2)}) async-start(), calls=%async_computation.14 | async-start | bytes 1179648 | tf_op jit(solution)/shard_map/reduce_scatter | solution.py:748
  600.1 28.3 %reduce-scatter.12.cloned.1.call-start = ((), (), s32[]{:S(2)}) async-start(), calls=%async_computation.13 | async-start | bytes 1179648 | tf_op jit(solution)/shard_map/reduce_scatter | solution.py:748
  609.5 29.0 %reduce-scatter.16.cloned.1.call-start = ((), (), s32[]{:S(2)}) async-start(), calls=%async_computation.15 | async-start | bytes 7077888 | tf_op jit(solution)/shard_map/reduce_scatter | solution.py:748
  616.8 38.4 %reduce-scatter.10.cloned.1.call-start = ((), (), s32[]{:S(2)}) async-start(), calls=%async_computation.12 | async-start | bytes 7077888 | tf_op jit(solution)/shard_map/reduce_scatter | solution.py:748
  624.3 44.0 %reduce-scatter.18.cloned.1.call-start = ((), (), s32[]{:S(2)}) async-start(), calls=%async_computation.16 | async-start | bytes 36864 | tf_op jit(solution)/shard_map/reduce_scatter | solution.py:748
  627.7 145.4 %reduce-scatter.20.cloned.1.call-start = ((), (), s32[]{:S(2)}) async-start(), calls=%async_computation.17 | async-start | bytes 15925248 | tf_op jit(solution)/shard_map/reduce_scatter | solution.py:716
  628.3 26.9 %copy-start.60 = (u32[32]{0:T(128)S(1)}, u32[32]{0:T(128)}, u32[]{:S(2)}) copy-start(u32[32]{0:T(128)} %constant.104) | copy-start | bytes 388
  628.3 28.2 %copy-start.61 = (bf16[512,1536]{1,0:T(8,128)(2,1)S(1)}, bf16[512,1536]{1,0:T(8,128)(2,1)}, u32[]{:S(2)}) copy-start(bf16[512,1536]{1,0:T(8,128)(2,1)} %get-tuple-element.26) | copy-start | bytes 4718596
  628.3 348.5 %all-reduce.8.cloned.1.call-start = ((), (), s32[]{:S(2)}) async-start(), calls=%async_computation.18 | async-start | bytes 11010048 | tf_op jit(solution)/shard_map/psum | solution.py:747
  656.5 4.6 copy-start.7
  661.1 1.6 copy-start.9
  661.1 1.7 copy-start.18
  662.9 2.8 copy-start.54
  662.9 85.4 %copy-start.58 = (f32[512]{0:T(512)S(1)}, f32[512]{0:T(512)}, u32[]{:S(2)}) copy-start(f32[512]{0:T(512)} %get-tuple-element.66) | copy-start | bytes 6148
  976.8 4.0 copy-start.11
  980.8 2.8 copy-start.10
  (14 other events, 11.0 us)
Sparse Core Ops, SparseCore 0:
  26.9 11.5 all-gather.7
  40.0 15.6 all-gather.5
  57.2 15.5 all-gather.9
  578.5 18.4 reduce-scatter.7
  600.2 9.3 reduce-scatter.13
  612.3 9.3 reduce-scatter.11
  624.7 13.7 reduce-scatter.15
  641.4 13.7 reduce-scatter.9
  658.0 8.5 reduce-scatter.17
  670.5 102.5 reduce-scatter.19
  780.7 196.0 all-reduce.7

commit v3 on v2

--- a/solution.py
+++ b/solution.py
@@ -632,6 +632,212 @@
 
 RIGHT = [(0, 1), (1, 2), (2, 3)]
 LEFT = [(1, 0), (2, 1), (3, 2)]
+
+
+WIDE = 512
+LINKS = 9
+
+
+def tail_kernel(ob_ref, da_ref, xa_ref, dq_ref, dkp_ref, dvp_ref, cos_ref, sin_ref, wq_ref, wk_ref,
+                wv_ref, dh_ref, x_ref, gain_ref, misc_ref,
+                qg_out, kg_out, vg_out, og_out, mg_out, gt_ref,
+                dkv_in, dkv_ref, part, buf0, buf1, buf2, buf3, buf4, res,
+                kv_sem, send_sem, recv_sem, out_sem):
+    ctx = lax.axis_index("context")
+    dp = lax.axis_index("dp")
+    z = lax.axis_index("expert")
+    tokens, width = xa_ref.shape
+    kv_width = dkp_ref.shape[1]
+    half = width // 2
+    chunks = 8
+    bit = lambda v: lax.rem(v, 2)
+    flip = lambda v: v + 1 - 2 * bit(v)
+    far = lambda v: lax.rem(v + 2, 4)
+    partner = {"c": ("context", 1 - ctx), "x": ("dp", flip(dp)), "y": ("dp", far(dp)),
+               "n": ("expert", flip(z)), "f": ("expert", far(z))}
+    side = {"c": ctx, "x": bit(dp), "y": lax.div(dp, 2), "n": bit(z), "f": lax.div(z, 2)}
+
+    barrier = pltpu.get_barrier_semaphore()
+    for axis, other in partner.values():
+        pl.semaphore_signal(barrier, inc=1, device_id={axis: other},
+                            device_id_type=pl.DeviceIdType.MESH)
+    pl.semaphore_wait(barrier, len(partner))
+
+    def exchange(src, dst, ss, rs, way):
+        axis, other = partner[way]
+        return remote(src, dst, ss, rs, axis, other)
+
+    theirs = pl.ds(pl.multiple_of((1 - ctx) * tokens, 16), tokens)
+    ours = pl.ds(pl.multiple_of(ctx * tokens, 16), tokens)
+    kv_copies = [
+        exchange(ref.at[theirs], dkv_in.at[k], kv_sem.at[0, k], kv_sem.at[1, k], "c")
+        for k, ref in enumerate((dkp_ref, dvp_ref))
+    ]
+    for copy in kv_copies:
+        copy.start()
+
+    sizes = [half // 2, half // 4, half // 8, half // 16]
+    bufs = [buf1, buf2, buf3, buf4]
+    columns = [WIDE] * (chunks - 1) + [128]
+
+    def flows(c):
+        w = columns[c] // 2 if columns[c] >= 256 else columns[c]
+        ways = [("x", "y", "n", "f"), ("y", "x", "n", "f")]
+        return [(k, k * w, w, ways[(k + c) % 2]) for k in range(columns[c] // w)]
+
+    def rows_at(ways, depth):
+        first = 0
+        for k in range(depth):
+            first = first + side[ways[k]] * sizes[k]
+        return pl.multiple_of(first, 16)
+
+    def plus(dst, drows, dcols, a, arows, size):
+        strip = 48
+        def one(k, _):
+            d = pl.ds(pl.multiple_of(drows + k * strip, 16), strip)
+            s = pl.ds(pl.multiple_of(arows + k * strip, 16), strip)
+            dst[d, dcols] = (dst[d, dcols].astype(F32) + a[s, dcols].astype(F32)).astype(BF)
+            return 0
+        lax.fori_loop(0, size // strip, one, 0)
+
+    def link(c, flow, level):
+        k, first, w, ways = flow
+        cols = pl.ds(first, w)
+        ss, rs = send_sem.at[c, k, level], recv_sem.at[c, k, level]
+        if level == 0:
+            src = part.at[c % 3, pl.ds(pl.multiple_of((1 - ctx) * half, 16), half), cols]
+            return exchange(src, buf0.at[c, :, cols], ss, rs, "c")
+        if level <= 4:
+            way, size = ways[level - 1], sizes[level - 1]
+            before = buf0 if level == 1 else bufs[level - 2]
+            src = before.at[c, pl.ds(pl.multiple_of((1 - side[way]) * size, 16), size), cols]
+            return exchange(src, bufs[level - 1].at[c, :, cols], ss, rs, way)
+        depth = 8 - level + 1
+        size = sizes[depth - 1]
+        rows = pl.ds(rows_at(ways, depth), size)
+        return exchange(res.at[c, rows, cols], res.at[c, rows, cols], ss, rs, ways[depth - 1])
+
+    def produce(c):
+        if c < 7:
+            left, right, first = ((ob_ref, da_ref, c * WIDE) if c < 3 else
+                                  (xa_ref, dq_ref, (c - 3) * WIDE) if c < 6 else
+                                  (xa_ref, dkv_ref, 0))
+            def one(j, _):
+                rows = pl.ds(pl.multiple_of(j * 256, 256), 256)
+                part[c % 3, rows, :] = mm_tn(left[:, rows], right[:, first : first + WIDE]).astype(BF)
+                return 0
+            lax.fori_loop(0, width // 256, one, 0)
+        else:
+            part[c % 3, :, 0:128] = misc_ref[...]
+            part[c % 3, :, 16:24] = gain_rows.T.astype(BF)
+
+    def finish(c):
+        for copy in out_copy(c):
+            copy.start()
+
+    def out_copy(c):
+        copy = lambda first, w, dst, at, k: pltpu.make_async_copy(
+            res.at[c, :, pl.ds(first, w)], dst.at[:, pl.ds(at, w)], out_sem.at[c, k])
+        if c < 3:
+            return [copy(0, WIDE, og_out, c * WIDE, 0)]
+        if c < 6:
+            return [copy(0, WIDE, qg_out, (c - 3) * WIDE, 0)]
+        if c == 6:
+            return [copy(0, kv_width, kg_out, 0, 0), copy(kv_width, kv_width, vg_out, 0, 1)]
+        return [copy(0, 128, mg_out, 0, 0)]
+
+    def do(c, level):
+        if level == 0:
+            produce(c)
+        for flow in flows(c):
+            k, first, w, ways = flow
+            cols = pl.ds(first, w)
+            if level > 0:
+                link(c, flow, level - 1).wait()
+            if level == 1:
+                plus(buf0.at[c], 0, cols, part.at[c % 3], ctx * half, half)
+            elif 1 < level <= 4:
+                before = buf0 if level == 2 else bufs[level - 3]
+                plus(bufs[level - 2].at[c], 0, cols, before.at[c],
+                     side[ways[level - 2]] * sizes[level - 2], sizes[level - 2])
+            elif level == 5:
+                rows = pl.ds(rows_at(ways, 4), sizes[3])
+                keep = pl.ds(pl.multiple_of(side[ways[3]] * sizes[3], 16), sizes[3])
+                res[c, rows, cols] = (buf4[c, :, cols].astype(F32)
+                                      + buf3[c, keep, cols].astype(F32)).astype(BF)
+            if level < LINKS:
+                link(c, flow, level).start()
+        if level == LINKS:
+            finish(c)
+
+    gain_rows = None
+    for t in range(chunks + LINKS):
+        for c in range(chunks):
+            if 0 <= t - c <= LINKS:
+                do(c, t - c)
+        if t == 1:
+            for copy in kv_copies:
+                copy.wait()
+            for h in range(kv_width // HEAD_SIZE):
+                at = slice(h * HEAD_SIZE, (h + 1) * HEAD_SIZE)
+                dk = dkp_ref[ours, at].astype(F32) + dkv_in[0, :, at].astype(F32)
+                turned = pltpu.roll(dk, HEAD_SIZE // 2, 1)
+                dkv_ref[:, at] = (dk * cos_ref[...] - turned * sin_ref[...]).astype(BF)
+            dv = dvp_ref[ours, :].astype(F32) + dkv_in[1].astype(F32)
+            dkv_ref[:, kv_width : 2 * kv_width] = dv.astype(BF)
+        if t == 2:
+            step = 64
+            def strip(k, total):
+                rows = pl.ds(pl.multiple_of(k * step, step), step)
+                dxa = mm_nt(dq_ref[rows, :], wq_ref[...])
+                dxa = dxa + mm_nt(dkv_ref[rows, 0:kv_width], wk_ref[...])
+                dxa = dxa + mm_nt(dkv_ref[rows, kv_width : 2 * kv_width], wv_ref[...])
+                v = x_ref[rows, :].astype(F32)
+                root = inverse_root(v)
+                back = dh_ref[rows, :] + norm_back(v, root, gain_ref[...], dxa)
+                gt_ref[rows, :] = back.astype(BF)
+                return total + fold_rows(dxa * v * root, jnp.sum)
+            total = lax.fori_loop(0, tokens // step, strip, jnp.zeros((8, width), F32))
+            gain_rows = jnp.broadcast_to(jnp.sum(total, axis=0, keepdims=True), (8, width))
+    for c in range(chunks):
+        for copy in out_copy(c):
+            copy.wait()
+
+
+def tail(ob, da, xa, dq, dk_part, dv_part, cos, sin, wq, wk, wv, dh, x, gain, misc):
+    tokens, width = xa.shape
+    kv_width = dk_part.shape[1]
+    half = width // 2
+    vmem = pl.BlockSpec(memory_space=pltpu.VMEM)
+    anywhere = pl.BlockSpec(memory_space=pl.ANY)
+    dma = pltpu.SemaphoreType.DMA
+    shape = jax.ShapeDtypeStruct
+    chunks = 8
+    return pl.pallas_call(
+        tail_kernel,
+        out_shape=(
+            shape((half, width), BF), shape((half, kv_width), BF), shape((half, kv_width), BF),
+            shape((half, width), BF), shape((half, 128), BF), shape((tokens, width), BF),
+        ),
+        in_specs=[vmem] * 15,
+        out_specs=[anywhere] * 5 + [vmem],
+        scratch_shapes=[
+            pltpu.VMEM((2, tokens, kv_width), BF), pltpu.VMEM((tokens, 2 * kv_width), BF),
+            pltpu.VMEM((3, width, WIDE), BF),
+            pltpu.VMEM((chunks, half, WIDE), BF), pltpu.VMEM((chunks, half // 2, WIDE), BF),
+            pltpu.VMEM((chunks, half // 4, WIDE), BF), pltpu.VMEM((chunks, half // 8, WIDE), BF),
+            pltpu.VMEM((chunks, half // 16, WIDE), BF), pltpu.VMEM((chunks, half, WIDE), BF),
+            dma((2, 2)), dma((chunks, 2, LINKS)), dma((chunks, 2, LINKS)), dma((chunks, 2)),
+        ],
+        compiler_params=pltpu.CompilerParams(
+            vmem_limit_bytes=MOE_VMEM, collective_id=2, has_side_effects=True
+        ),
+        cost_estimate=pl.CostEstimate(
+            flops=2 * tokens * width * (2 * width + 4 * kv_width + width),
+            transcendentals=0, bytes_accessed=16 * width * width,
+        ),
+        name="tail",
+    )(ob, da, xa, dq, dk_part, dv_part, cos, sin, wq, wk, wv, dh, x, gain, misc)
 
 
 def body(
@@ -712,7 +918,6 @@
     )
     gate_dot = dw_parts[:, :local].reshape(expert_count, rows).T * kept_float
     y_parts = lax.all_to_all(part_y, "expert", split_axis=0, concat_axis=0, tiled=True)
-    layer_out = (hidden + jnp.sum(y_parts.astype(F32), axis=0)).astype(BF)
     grads_shard = lax.psum_scatter(
         grads_low, ("dp", "context"), scatter_dimension=1, tiled=True
     ).astype(F32)
@@ -726,34 +931,48 @@
     hidden_total = upstream + norm_back(hidden, root_second, gain_second, normed_grad)
     gain_second_grad = jnp.sum(normed_grad * hidden * root_second, axis=0)
     attn_grad_low = hidden_total.astype(BF)
-    output_local = mm_tn(mixed, attn_grad_low)
     mixed_grad_low = mm_nt(attn_grad_low, output_full).astype(BF)
 
     dq_low, dk_part, dv_part = attention_backward(
         q, k_all, v_all, mixed_grad_low, lse, cos_full, sin_full, meta, segk, segq
     )
-    dkv = lax.psum_scatter(
-        jnp.concatenate([dk_part, dv_part], axis=1), "context", scatter_dimension=0, tiled=True
-    )
-    dk_low = turn(dkv[:, :kv_width].astype(F32), KEY_VALUE_HEADS, -1.0).astype(BF)
-    dv_low = dkv[:, kv_width:]
-    input_total = mm_nt(dq_low, query_full) + mm_nt(dk_low, key_full) + mm_nt(dv_low, value_full)
-    query_local = mm_tn(attn_input, dq_low)
-    key_local = mm_tn(attn_input, dk_low)
-    value_local = mm_tn(attn_input, dv_low)
-    grad_tokens = (hidden_total + norm_back(residual, root_first, gain_first, input_total)).astype(BF)
-    gain_first_grad = jnp.sum(input_total * residual * root_first, axis=0)
-
-    reduce_rows = lambda v: lax.psum(
-        lax.psum_scatter(v.astype(BF), "context", scatter_dimension=0, tiled=True), ("dp", "expert")
-    ).astype(F32)
-    return (
-        layer_out[None], grad_tokens[None],
-        reduce_rows(query_local), reduce_rows(key_local), reduce_rows(value_local),
-        reduce_rows(output_local), reduce_rows(router_local),
-        reduce_rows(gain_first_grad), reduce_rows(gain_second_grad),
-        gate_grad, up_grad, down_grad,
-    )
+    if (lax.axis_size("dp"), lax.axis_size("context"), expert_size) == (4, 2, 4):
+        misc = jnp.concatenate([router_local, gain_second_grad[:, None]], axis=1)
+        misc = jnp.pad(misc, ((0, 0), (0, 128 - misc.shape[1]))).astype(BF)
+        query_grad, key_grad, value_grad, output_grad, misc_grad, grad_tokens = tail(
+            mixed, attn_grad_low, attn_input, dq_low, dk_part, dv_part, cos_full, sin_full,
+            query_full, key_full, value_full, hidden_total, tokens[0], gain_first[None], misc,
+        )
+        query_grad, key_grad, value_grad, output_grad, misc_grad = (
+            v.astype(F32) for v in (query_grad, key_grad, value_grad, output_grad, misc_grad)
+        )
+        sums = (
+            query_grad, key_grad, value_grad, output_grad, misc_grad[:, :expert_count],
+            misc_grad[:, 16], misc_grad[:, expert_count],
+        )
+    else:
+        dkv = lax.psum_scatter(
+            jnp.concatenate([dk_part, dv_part], axis=1), "context", scatter_dimension=0, tiled=True
+        )
+        dk_low = turn(dkv[:, :kv_width].astype(F32), KEY_VALUE_HEADS, -1.0).astype(BF)
+        dv_low = dkv[:, kv_width:]
+        input_total = mm_nt(dq_low, query_full) + mm_nt(dk_low, key_full) + mm_nt(dv_low, value_full)
+        query_local = mm_tn(attn_input, dq_low)
+        key_local = mm_tn(attn_input, dk_low)
+        value_local = mm_tn(attn_input, dv_low)
+        grad_tokens = (hidden_total + norm_back(residual, root_first, gain_first, input_total)).astype(BF)
+        gain_first_grad = jnp.sum(input_total * residual * root_first, axis=0)
+
+        reduce_rows = lambda v: lax.psum(
+            lax.psum_scatter(v.astype(BF), "context", scatter_dimension=0, tiled=True), ("dp", "expert")
+        ).astype(F32)
+        sums = tuple(reduce_rows(v) for v in (
+            query_local, key_local, value_local, mm_tn(mixed, attn_grad_low), router_local,
+            gain_first_grad, gain_second_grad,
+        ))
+    late, grad_tokens = lax.optimization_barrier((hidden, grad_tokens))
+    layer_out = (late + jnp.sum(y_parts.astype(F32), axis=0)).astype(BF)
+    return (layer_out[None], grad_tokens[None], *sums, gate_grad, up_grad, down_grad)
 
 
 def solution(mesh):

time: 998 us -> 670 us (0.67)
  waiting for transfers between devices: 394 us -> 2.03 us
  Pallas kernels: 333 us -> 513 us
  blocking collectives: 91.6 us -> 12.5 us
  matrix products: 54.9 us -> 28.3 us
    psum x1 -> x0, waiting for transfers between devices: 200 us -> none  [body(): lax.psum(lax.psum_scatter(v.astype(BF), 'context', scatter_dimension=0, t...]
    pallas_call x0 -> x1, Pallas kernels: none -> 179 us  [tail(): pl.pallas_call(tail_kernel, out_shape=(shape((half, width), BF), shape((h...]
    all_to_all x1, waiting for transfers between devices: 128 us -> 0.01 us  [body(): lax.all_to_all(part_y, 'expert', split_axis=0, concat_axis=0, tiled=True)]
    psum x1 -> x0, blocking collectives: 78.1 us -> none  [body(): lax.psum(lax.psum_scatter(v.astype(BF), 'context', scatter_dimension=0, t...]
    reduce_scatter x6 -> x0, waiting for transfers between devices: 45.4 us -> none  [the longest x5 26.8 us: body(): lax.psum_scatter(v.astype(BF), 'context', scatter_dimension=0, tiled=True)]
    dot_general x4 -> x0, matrix products: 20.5 us -> none  [mm_tn(): lax.dot_general(a, b, (((0,), (0,)), ((), ())), preferred_element_type=F32)]
    reduce_scatter x1, waiting for transfers between devices: 19 us -> 0.01 us  [body(): lax.psum_scatter(grads_low, ('dp', 'context'), scatter_dimension=1, tiled...]
  transfers between devices with their start and end apart: 14 -> 7, of which waited for: 6 -> 1; matrix products, arithmetic and copies ran while one was open for 10% -> 12% of each run, Pallas kernels for 2% -> 34%
where the time goes in v3:
time: 670 us; the launch traced here: 669 us
  Pallas kernels  513 us (77%)
  other arithmetic  41.8 us (6%)
  local copies, waits for them, and re-layouts  29.2 us (4%)
  matrix products  28.3 us (4%)
  starting transfers between devices  22.1 us (3%)
  between operations  19.7 us (3%)
  blocking collectives  12.5 us (2%)
    pallas_call x1, Pallas kernels, moe(): pl.pallas_call(functools.partial(moe_kernel, cap, tile, n), out_shape=(sh...  286 us
    pallas_call x1, Pallas kernels, tail(): pl.pallas_call(tail_kernel, out_shape=(shape((half, width), BF), shape((h...  179 us
    pallas_call x1, Pallas kernels, attention_backward(): pl.pallas_call(functools.partial(attn_bwd_kernel, kb, tq), out_shape=(jax...  27.1 us
    pallas_call x1, Pallas kernels, attention_forward(): pl.pallas_call(functools.partial(attn_fwd_kernel, kb, tq), out_shape=(jax...  20.8 us
    all_to_all x1, starting transfers between devices, body(): lax.all_to_all(part_y, 'expert', split_axis=0, concat_axis=0, tiled=True)  14.2 us
    dot_general x4, matrix products, mm(): return jnp.dot(a, b, preferred_element_type=F32)  13.5 us
  transfers between devices with their start and end apart: 7, of which 1 were waited for; matrix products, arithmetic and copies ran while one was open for 12% of the time, Pallas kernels for 34%

profile of v3, /device:TPU:0, one launch (start us, length us, event | category | flops | bytes accessed | tf_op | source)
XLA Modules:
  0.0 668.7 jit_solution(17154349524420030628)
XLA Ops:
  7.3 1.8 fusion
  9.1 0.8 reshape.178
  9.9 1.9 all-gather
  12.4 1.8 fusion.17
  14.3 0.6 copy-done.7
  15.0 2.4 all_gather.26.wk_ref
  17.4 4.2 all_gather.27.wv_ref
  21.6 1.2 copy.112
  22.8 1.6 fusion.2.xa_ref
  24.4 0.7 fusion.13
  25.3 2.2 convolution_convert_fusion.1
  27.5 0.8 pad_maximum_fusion.1
  28.5 0.7 all-gather.6.cloned.1.call-update
  29.2 0.7 all-gather.10.cloned.1.call-update
  30.0 1.3 collective-permute-start.1
  31.3 6.5 collective-permute-start
  37.7 0.6 constant_dynamic-slice_fusion.2
  38.3 1.9 fusion.27
  45.5 1.8 all-gather.1
  47.8 0.7 reduce.13
  48.9 1.0 convert_reduce_fusion.2
  50.0 1.0 copy.103.segk_ref
  51.0 0.6 stack.32.meta
  51.6 2.2 all_gather.31
  53.8 0.6 constant_dynamic-slice_fusion.segq_ref
  54.4 2.2 fusion.30
  56.6 0.6 all-gather.6.cloned.1.call-done.wq_ref
  57.2 6.6 copy.93
  63.8 4.7 fusion.15
  69.3 1.6 copy.102.q_ref
  70.9 20.8 %attn_fwd.1 = (bf16[512,1536]{1,0:T(8,128)(2,1)}, f32[12,1,512]{2,1,0:T(1,128)}) custom-call(s32[5]{0:T(128)} %stack.32.meta, bf16[512,1536]{1,0:T(8,128)(2,1)} %copy.102.q_ref, bf16[1024,256]{1,0:T(8,128)(2,1)} %get-tuple-element.122.k_ref, bf16[1024,256]{1,0:T(8,128)(2,1)} %get-tuple-element.121.v_ref, s32[1024,1]{1,0:T(8,128)} %copy.103.segk_ref, ...), custom_call_target="tpu_custom_call" | custom-call | flops 2415919104 | bytes 3145728 | tf_op jit(solution)/shard_map/attn_fwd/pallas_call | solution.py:200
  91.6 6.0 multiply_reduce_fusion.2
  97.6 0.6 multiply_multiply_fusion.5
  98.2 1.8 fusion.25
  100.7 0.6 pad.9.meta_hbm
  101.3 1.5 fusion.5.x_hbm
  102.8 286.0 %moe.1 = (bf16[4,512,1536]{2,1,0:T(8,128)(2,1)}, f32[4,8,512]{2,1,0:T(8,128)}, bf16[4,512,1536]{2,1,0:T(8,128)(2,1)}, bf16[2,1536,2304]{2,1,0:T(8,128)(2,1)}, bf...) custom-call(bf16[512,1536]{1,0:T(8,128)(2,1)} %fusion.5.x_hbm, bf16[512,1536]{1,0:T(8,128)(2,1)} %bitcast.17.cot_hbm, ...), custom_call_target="tpu_custom_call" | custom-call | flops 74490839040 | bytes 78643200 | tf_op jit(solution)/shard_map/moe/pallas_call | solution.py:595
  388.8 14.2 %all-to-all-start = ((bf16[4,512,1536]{2,1,0:T(8,128)(2,1)}), bf16[4,512,1536]{2,1,0:T(8,128)(2,1)}, u32[]{:S(2)}, u32[]{:S(2)}) async-start(bf16[4,512,1536]{2,1,0:T(8,128)(2,1)} %get-tuple-element.38), calls=%async_computation | async-start | bytes 12582912 | tf_op jit(solution)/shard_map/all_to_all | solution.py:920
  403.1 0.6 convert.32.gain_ref
  403.7 1.0 pad_maximum_fusion.3
  404.7 0.9 slice.45
  405.6 6.0 convert_reduce_fusion.1
  411.6 4.3 multiply_reduce_fusion
  415.9 2.0 fusion.6
  417.9 0.6 pad_maximum_fusion.5
  418.6 1.0 copy.109
  419.6 0.8 pad.10.misc_ref
  420.5 0.6 broadcast_multiply_fusion
  421.1 4.9 fusion.28
  426.0 6.7 %convolution_convert_fusion.do_ref = bf16[512,1536]{1,0:T(8,128)(2,1)} fusion(bf16[512,1536]{1,0:T(8,128)(2,1)S(1)} %get-tuple-element.112.da_ref, bf16[1536,1536]{1,0:T(8,128)(2,1)} %all-gather.10.cloned.1.call-done), kind=kOutput, calls=%fused_computation.17 | convolution fusion | flops 2416705536 | bytes 7864320 | tf_op jit(solution)/shard_map/dot_general | solution.py:32
  432.7 27.1 %attn_bwd.1 = (bf16[512,1536]{1,0:T(8,128)(2,1)}, bf16[1024,256]{1,0:T(8,128)(2,1)}, bf16[1024,256]{1,0:T(8,128)(2,1)}) custom-call(s32[5]{0:T(128)} %stack.32.meta, bf16[512,1536]{1,0:T(8,128)(2,1)} %copy.102.q_ref, bf16[1024,256]{1,0:T(8,128)(2,1)} %get-tuple-element.122.k_ref, bf16[1024,256]{1,0:T(8,128)(2,1)} %get-tuple-element.121.v_ref, ...), custom_call_target="tpu_custom_call" | custom-call | flops 6442450944 | bytes 6291456 | tf_op jit(solution)/shard_map/attn_bwd/pallas_call | solution.py:242
  459.9 179.2 %tail.1 = (bf16[768,1536]{1,0:T(8,128)(2,1)}, bf16[768,256]{1,0:T(8,128)(2,1)}, bf16[768,256]{1,0:T(8,128)(2,1)}, bf16[768,1536]{1,0:T(8,128)(2,1)}, bf16[768,12...) custom-call(bf16[512,1536]{1,0:T(8,128)(2,1)} %get-tuple-element.29.ob_ref, bf16[512,1536]{1,0:T(8,128)(2,1)} %copy-done.10, ...), custom_call_target="tpu_custom_call" | custom-call | flops 8858370048 | bytes 37748736 | tf_op jit(solution)/shard_map/tail/pallas_call | solution.py:816
  639.1 1.1 slice.58
  640.2 1.0 convert_element_type.123
  641.2 0.7 copy.110
  641.9 1.9 convert_element_type.120
  643.9 0.9 convert_element_type.121
  644.8 2.8 convert_element_type.119
  647.7 2.8 convert_element_type.122
  650.5 1.1 slice_reduce_fusion
  651.6 4.2 convert_reduce_fusion
  655.8 1.6 fusion.8
  657.4 3.4 fusion.29
  660.8 1.1 copy.115
  (90 shorter events, 3.8 us)
Async XLA Ops:
  7.2 7.9 %copy-start.13 = (bf16[768,256]{1,0:T(8,128)(2,1)S(1)}, bf16[768,256]{1,0:T(8,128)(2,1)}, u32[]{:S(2)}) copy-start(bf16[768,256]{1,0:T(8,128)(2,1)} %param.21) | copy-start | bytes 1179652
  7.2 47.2 %all-gather.8.cloned.1.call-start = ((), (), s32[]{:S(2)}) async-start(), calls=%async_computation.3 | async-start | bytes 1572864 | tf_op jit(solution)/shard_map/all_gather | solution.py:853
  9.1 13.7 %copy-start.3 = (bf16[1,512,1536]{2,1,0:T(8,128)(2,1)S(1)}, bf16[1,512,1536]{2,1,0:T(8,128)(2,1)}, u32[]{:S(2)}) copy-start(bf16[1,512,1536]{2,1,0:T(8,128)(2,1)} %param.15) | copy-start | bytes 4718596
  11.8 0.6 copy-start.15
  14.2 0.7 copy-start.7
  17.4 7.6 %copy-start.4 = (bf16[1536,256]{1,0:T(8,128)(2,1)}, bf16[1536,256]{1,0:T(8,128)(2,1)S(1)}, u32[]{:S(2)}) copy-start(bf16[1536,256]{1,0:T(8,128)(2,1)S(1)} %all_gather.26.wk_ref) | copy-start | bytes 2359300
  22.8 1.6 copy-start.12
  27.5 10.2 %copy-start.20 = (s32[1,1024]{1,0:T(1,128)S(1)}, s32[1,1024]{1,0:T(1,128)}, u32[]{:S(2)}) copy-start(s32[1,1024]{1,0:T(1,128)} %param.17) | copy-start | bytes 12292
  27.5 17.9 %copy-start.23 = (bf16[768]{0:T(1024)(128)(2,1)S(1)}, bf16[768]{0:T(1024)(128)(2,1)}, u32[]{:S(2)}) copy-start(bf16[768]{0:T(1024)(128)(2,1)} %param.26) | copy-start | bytes 4612
  27.5 20.3 %copy-start.22 = (s32[1,1,2048]{2,1,0:T(1,128)S(1)}, s32[1,1,2048]{2,1,0:T(1,128)}, u32[]{:S(2)}) copy-start(s32[1,1,2048]{2,1,0:T(1,128)} %param.19) | copy-start | bytes 24580
  28.4 20.5 %copy-start.19 = (s32[1,512,4]{1,2,0:T(4,128)S(1)}, s32[1,512,4]{1,2,0:T(4,128)}, u32[]{:S(2)}) copy-start(s32[1,512,4]{1,2,0:T(4,128)} %param.18) | copy-start | bytes 24580
  28.4 23.2 %copy-start.21 = (bf16[768,8]{0,1:T(8,128)(2,1)S(1)}, bf16[768,8]{0,1:T(8,128)(2,1)}, u32[]{:S(2)}) copy-start(bf16[768,8]{0,1:T(8,128)(2,1)} %param.24) | copy-start | bytes 36868
  28.4 28.8 %all-gather.6.cloned.1.call-start = ((), (), s32[]{:S(2)}) async-start(), calls=%async_computation.2 | async-start | bytes 7077888 | tf_op jit(solution)/shard_map/all_gather | solution.py:853
  29.2 62.4 %all-gather.10.cloned.1.call-start = ((), (), s32[]{:S(2)}) async-start(), calls=%async_computation.4 | async-start | bytes 7077888 | tf_op jit(solution)/shard_map/all_gather | solution.py:853
  29.9 627.5 %reduce-scatter.2.cloned.1.call-start = ((), (), s32[]{:S(2)}) async-start(), calls=%async_computation.5 | async-start | bytes 15925248 | tf_op jit(solution)/shard_map/reduce_scatter | solution.py:921
  30.0 72.8 %collective-permute-start.1 = (bf16[512,1536]{1,0:T(8,128)(2,1)}, bf16[512,1536]{1,0:T(8,128)(2,1)}, u32[]{:S(2)}, u32[]{:S(2)}) collective-permute-start(bf16[512,1536]{1,0:T(8,128)(2,1)} %bitcast.17.cot_hbm), channel_id=1, source_target_pairs={{1,0},{2,1},{3,2},{5,4},{6,5},{7,6},{9,8},{10,9},{11,10},{13,12},{... | collective-permute-start | bytes 4718600 | tf_op jit(solution)/shard_map/ppermute | solution.py:857
  31.3 71.5 %collective-permute-start = (bf16[512,1536]{1,0:T(8,128)(2,1)}, bf16[512,1536]{1,0:T(8,128)(2,1)}, u32[]{:S(2)}, u32[]{:S(2)}) collective-permute-start(bf16[512,1536]{1,0:T(8,128)(2,1)} %bitcast.17.cot_hbm), channel_id=1, source_target_pairs={{0,1},{1,2},{2,3},{4,5},{5,6},{6,7},{8,9},{9,10},{10,11},{12,13},{... | collective-permute-start | bytes 4718600 | tf_op jit(solution)/shard_map/ppermute | solution.py:856
  97.6 5.2 copy-start
  100.1 0.5 copy-start.17
  388.8 14.3 %copy-start.16 = (bf16[2,1,768]{2,1,0:T(2,128)(2,1)S(1)}, bf16[2,1,768]{2,1,0:T(2,128)(2,1)}, u32[]{:S(2)}) copy-start(bf16[2,1,768]{2,1,0:T(2,128)(2,1)} %copy-done.15) | copy-start | bytes 9220
  388.8 14.9 %copy-start.8 = (f32[512,64]{1,0:T(8,128)S(1)}, f32[512,64]{1,0:T(8,128)}, u32[]{:S(2)}) copy-start(f32[512,64]{1,0:T(8,128)} %copy-done.7) | copy-start | bytes 393220
  388.8 14.9 %copy-start.11 = (f32[512,64]{1,0:T(8,128)S(1)}, f32[512,64]{1,0:T(8,128)}, u32[]{:S(2)}) copy-start(f32[512,64]{1,0:T(8,128)} %get-tuple-element.127) | copy-start | bytes 393220
  388.8 16.8 %copy-start.18 = (f32[512]{0:T(512)S(1)}, f32[512]{0:T(512)}, u32[]{:S(2)}) copy-start(f32[512]{0:T(512)} %copy-done.17) | copy-start | bytes 6148
  388.8 262.7 %all-to-all-start = ((bf16[4,512,1536]{2,1,0:T(8,128)(2,1)}), bf16[4,512,1536]{2,1,0:T(8,128)(2,1)}, u32[]{:S(2)}, u32[]{:S(2)}) async-start(bf16[4,512,1536]{2,1,0:T(8,128)(2,1)} %get-tuple-element.38), calls=%async_computation | async-start | bytes 12582912 | tf_op jit(solution)/shard_map/all_to_all | solution.py:920
  405.6 6.0 copy-start.1
  426.0 6.7 %copy-start.10 = (bf16[512,1536]{1,0:T(8,128)(2,1)}, bf16[512,1536]{1,0:T(8,128)(2,1)S(1)}, u32[]{:S(2)}) copy-start(bf16[512,1536]{1,0:T(8,128)(2,1)S(1)} %get-tuple-element.112.da_ref) | copy-start | bytes 4718596
  639.1 4.8 copy-start.14
  639.1 5.7 copy-start.6
  644.8 2.8 copy-start.5
  651.6 4.2 copy-start.2
  657.4 3.4 copy-start.9
Sparse Core Ops, SparseCore 0:
  28.5 11.4 all-gather.7
  41.6 15.5 all-gather.5
  58.8 15.6 all-gather.9
  388.9 107.5 reduce-scatter.1

commit v4 on v3

--- a/solution.py
+++ b/solution.py
@@ -17,6 +17,7 @@
 norm_eps = 1e-06
 rope_base = 10000.0
 NEG = -1e30
+HEADS_AT_ONCE = 3
 SCALE = 1.0 / math.sqrt(HEAD_SIZE)
 BF = jnp.bfloat16
 F32 = jnp.float32
@@ -34,12 +35,6 @@
 
 def mm_tn(a, b):
     return lax.dot_general(a, b, (((0,), (0,)), ((), ())), preferred_element_type=F32)
-
-
-def precise_dims(a, b, dims):
-    return lax.dot_general(
-        a, b, (dims, ((), ())), precision=lax.Precision.HIGHEST, preferred_element_type=F32
-    )
 
 
 def inverse_root(v):
@@ -83,95 +78,117 @@
 
 def attn_fwd_kernel(kb, tq, meta, q_ref, k_ref, v_ref, segk_ref, segq_ref, o_ref, lse_ref,
                     bias_ref, s_ref, vt_ref):
-    head = pl.program_id(0)
+    step = pl.program_id(0)
     tokens = q_ref.shape[0]
 
-    @pl.when(head == 0)
+    @pl.when(step == 0)
     def _():
         make_bias(meta[0], tokens, segk_ref, segq_ref, bias_ref)
 
-    @pl.when(lax.rem(head, GROUP) == 0)
+    @pl.when(lax.rem(step * HEADS_AT_ONCE, GROUP) == 0)
     def _():
         vt_ref[...] = v_ref[...].astype(F32).T.astype(BF)
 
+    heads = [slice(h * HEAD_SIZE, (h + 1) * HEAD_SIZE) for h in range(HEADS_AT_ONCE)]
     for part in range(tokens // tq):
         cols = pl.ds(part * tq, tq)
-        q = q_ref[cols, :]
         low, high = meta[1 + 2 * part], meta[2 + 2 * part]
 
-        def score(i, top):
+        def score(i, tops):
             rows = pl.ds(pl.multiple_of(i * kb, kb), kb)
-            s = mm_nt(k_ref[rows, :], q) * SCALE + bias_ref[rows, cols]
-            s_ref[rows, :] = s
-            return jnp.maximum(top, fold_rows(s, jnp.max))
-
-        top = lax.fori_loop(low, high, score, jnp.full((8, tq), NEG, F32))
-        top = jnp.max(top, axis=0, keepdims=True)
+            key, bias = k_ref[rows, :], bias_ref[rows, cols]
+            out = []
+            for h, at in enumerate(heads):
+                s = mm_nt(key, q_ref[cols, at]) * SCALE + bias
+                s_ref[h, rows, :] = s
+                out.append(jnp.maximum(tops[h], fold_rows(s, jnp.max)))
+            return tuple(out)
+
+        tops = lax.fori_loop(low, high, score,
+                             tuple(jnp.full((8, tq), NEG, F32) for _ in heads))
+        tops = [jnp.max(t, axis=0, keepdims=True) for t in tops]
 
         def value(i, carry):
-            total, out = carry
+            totals, outs = carry
             rows = pl.ds(pl.multiple_of(i * kb, kb), kb)
-            p = jnp.exp(s_ref[rows, :] - top)
-            total = total + fold_rows(p, jnp.sum)
-            return total, out + mm(vt_ref[:, rows], p.astype(BF))
-
-        total, out = lax.fori_loop(
-            low, high, value, (jnp.zeros((8, tq), F32), jnp.zeros((HEAD_SIZE, tq), F32))
-        )
-        total = jnp.sum(total, axis=0, keepdims=True)
-        o_ref[cols, :] = (out / total).T.astype(BF)
-        lse_ref[0, :, cols] = top + jnp.log(total)
+            vt = vt_ref[:, rows]
+            new_totals, new_outs = [], []
+            for h in range(HEADS_AT_ONCE):
+                p = jnp.exp(s_ref[h, rows, :] - tops[h])
+                new_totals.append(totals[h] + fold_rows(p, jnp.sum))
+                new_outs.append(outs[h] + mm(vt, p.astype(BF)))
+            return tuple(new_totals), tuple(new_outs)
+
+        totals, outs = lax.fori_loop(
+            low, high, value, (tuple(jnp.zeros((8, tq), F32) for _ in heads),
+                               tuple(jnp.zeros((HEAD_SIZE, tq), F32) for _ in heads)))
+        for h, at in enumerate(heads):
+            total = jnp.sum(totals[h], axis=0, keepdims=True)
+            o_ref[cols, at] = (outs[h] / total).T.astype(BF)
+            lse_ref[h, :, cols] = tops[h] + jnp.log(total)
 
 
 def attn_bwd_kernel(kb, tq, meta, q_ref, k_ref, v_ref, do_ref, lse_ref, cos_ref, sin_ref,
                     segk_ref, segq_ref, dq_ref, dk_ref, dv_ref,
                     bias_ref, p_ref, dp_ref, kt_ref, dk_acc, dv_acc):
-    head = pl.program_id(0)
+    step = pl.program_id(0)
     tokens = q_ref.shape[0]
 
-    @pl.when(head == 0)
+    @pl.when(step == 0)
     def _():
         make_bias(meta[0], tokens, segk_ref, segq_ref, bias_ref)
 
-    @pl.when(lax.rem(head, GROUP) == 0)
+    place = lax.rem(step * HEADS_AT_ONCE, GROUP)
+
+    @pl.when(place == 0)
     def _():
         kt_ref[...] = k_ref[...].astype(F32).T.astype(BF)
         dk_acc[...] = jnp.zeros_like(dk_acc)
         dv_acc[...] = jnp.zeros_like(dv_acc)
 
+    heads = [slice(h * HEAD_SIZE, (h + 1) * HEAD_SIZE) for h in range(HEADS_AT_ONCE)]
     for part in range(tokens // tq):
         cols = pl.ds(part * tq, tq)
-        q = q_ref[cols, :]
-        do = do_ref[cols, :]
-        lse = lse_ref[0, :, cols]
         low, high = meta[1 + 2 * part], meta[2 + 2 * part]
 
-        def score(i, delta):
+        def score(i, deltas):
             rows = pl.ds(pl.multiple_of(i * kb, kb), kb)
-            s = mm_nt(k_ref[rows, :], q) * SCALE + bias_ref[rows, cols]
-            p = jnp.exp(s - lse)
-            dp = mm_nt(v_ref[rows, :], do)
-            p_ref[rows, :] = p
-            dp_ref[rows, :] = dp
-            return delta + fold_rows(p * dp, jnp.sum)
-
-        delta = lax.fori_loop(low, high, score, jnp.zeros((8, tq), F32))
-        delta = jnp.sum(delta, axis=0, keepdims=True)
-
-        def grads(i, dq):
+            key, value, bias = k_ref[rows, :], v_ref[rows, :], bias_ref[rows, cols]
+            out = []
+            for h, at in enumerate(heads):
+                s = mm_nt(key, q_ref[cols, at]) * SCALE + bias
+                p = jnp.exp(s - lse_ref[h, :, cols])
+                dp = mm_nt(value, do_ref[cols, at])
+                p_ref[h, rows, :] = p
+                dp_ref[h, rows, :] = dp
+                out.append(deltas[h] + fold_rows(p * dp, jnp.sum))
+            return tuple(out)
+
+        deltas = lax.fori_loop(low, high, score, tuple(jnp.zeros((8, tq), F32) for _ in heads))
+        deltas = [jnp.sum(d, axis=0, keepdims=True) for d in deltas]
+
+        def grads(i, dqs):
             rows = pl.ds(pl.multiple_of(i * kb, kb), kb)
-            p = p_ref[rows, :]
-            ds = (p * (dp_ref[rows, :] - delta)).astype(BF)
-            dv_acc[rows, :] += mm(p.astype(BF), do)
-            dk_acc[rows, :] += mm(ds, q)
-            return dq + mm(kt_ref[:, rows], ds)
-
-        dq = lax.fori_loop(low, high, grads, jnp.zeros((HEAD_SIZE, tq), F32))
-        dq = dq.T * SCALE
-        turned = pltpu.roll(dq, HEAD_SIZE // 2, 1)
-        dq_ref[cols, :] = (dq * cos_ref[cols, :] - turned * sin_ref[cols, :]).astype(BF)
-
-    @pl.when(lax.rem(head, GROUP) == GROUP - 1)
+            kt = kt_ref[:, rows]
+            out, dk, dv = [], dk_acc[rows, :], dv_acc[rows, :]
+            for h, at in enumerate(heads):
+                p = p_ref[h, rows, :]
+                ds = (p * (dp_ref[h, rows, :] - deltas[h])).astype(BF)
+                dv = dv + mm(p.astype(BF), do_ref[cols, at])
+                dk = dk + mm(ds, q_ref[cols, at])
+                out.append(dqs[h] + mm(kt, ds))
+            dk_acc[rows, :] = dk
+            dv_acc[rows, :] = dv
+            return tuple(out)
+
+        dqs = lax.fori_loop(low, high, grads,
+                            tuple(jnp.zeros((HEAD_SIZE, tq), F32) for _ in heads))
+        for h, at in enumerate(heads):
+            dq = dqs[h].T * SCALE
+            turned = pltpu.roll(dq, HEAD_SIZE // 2, 1)
+            dq_ref[cols, at] = (dq * cos_ref[cols, :] - turned * sin_ref[cols, :]).astype(BF)
+
+    @pl.when(place == GROUP - HEADS_AT_ONCE)
     def _():
         dk_ref[...] = (dk_acc[...] * SCALE).astype(BF)
         dv_ref[...] = dv_acc[...].astype(BF)
@@ -193,8 +210,8 @@
     return jnp.stack(entries).astype(jnp.int32)
 
 
-def attention_forward(q, k, v, meta, segk, segq):
-    tokens, length = q.shape[0], k.shape[0]
+def attention_forward(q, kv, meta, segk, segq):
+    tokens, length = q.shape[0], kv.shape[0]
     tq, kb = attention_sizes(tokens, length)
     const = lambda h, m: (0, 0)
     return pl.pallas_call(
@@ -205,21 +222,21 @@
         ),
         grid_spec=pltpu.PrefetchScalarGridSpec(
             num_scalar_prefetch=1,
-            grid=(QUERY_HEADS,),
+            grid=(QUERY_HEADS // HEADS_AT_ONCE,),
             in_specs=[
-                pl.BlockSpec((tokens, HEAD_SIZE), lambda h, m: (0, h)),
-                pl.BlockSpec((length, HEAD_SIZE), lambda h, m: (0, h // GROUP)),
-                pl.BlockSpec((length, HEAD_SIZE), lambda h, m: (0, h // GROUP)),
+                pl.BlockSpec((tokens, HEADS_AT_ONCE * HEAD_SIZE), lambda h, m: (0, h)),
+                pl.BlockSpec((length, HEAD_SIZE), lambda h, m: (0, h * HEADS_AT_ONCE // GROUP)),
+                pl.BlockSpec((length, HEAD_SIZE), lambda h, m: (0, KEY_VALUE_HEADS + h * HEADS_AT_ONCE // GROUP)),
                 pl.BlockSpec((length, 1), const),
                 pl.BlockSpec((1, tokens), const),
             ],
             out_specs=[
-                pl.BlockSpec((tokens, HEAD_SIZE), lambda h, m: (0, h)),
-                pl.BlockSpec((1, 1, tokens), lambda h, m: (h, 0, 0)),
+                pl.BlockSpec((tokens, HEADS_AT_ONCE * HEAD_SIZE), lambda h, m: (0, h)),
+                pl.BlockSpec((HEADS_AT_ONCE, 1, tokens), lambda h, m: (h, 0, 0)),
             ],
             scratch_shapes=[
                 pltpu.VMEM((length, tokens), F32),
-                pltpu.VMEM((length, tq), F32),
+                pltpu.VMEM((HEADS_AT_ONCE, length, tq), F32),
                 pltpu.VMEM((HEAD_SIZE, length), BF),
             ],
         ),
@@ -230,45 +247,45 @@
             bytes_accessed=4 * tokens * MODEL_WIDTH,
         ),
         name="attn_fwd",
-    )(meta, q, k, v, segk, segq)
-
-
-def attention_backward(q, k, v, do, lse, cos, sin, meta, segk, segq):
-    tokens, length = q.shape[0], k.shape[0]
+    )(meta, q, kv, kv, segk, segq)
+
+
+def attention_backward(q, kv, do, lse, cos, sin, meta, segk, segq):
+    tokens, length = q.shape[0], kv.shape[0]
     tq, kb = attention_sizes(tokens, length)
     const = lambda h, m: (0, 0)
     by_head = lambda h, m: (0, h)
-    by_group = lambda h, m: (0, h // GROUP)
+    by_group = lambda h, m: (0, h * HEADS_AT_ONCE // GROUP)
     return pl.pallas_call(
         functools.partial(attn_bwd_kernel, kb, tq),
         out_shape=(
             jax.ShapeDtypeStruct(q.shape, BF),
-            jax.ShapeDtypeStruct(k.shape, BF),
-            jax.ShapeDtypeStruct(v.shape, BF),
+            jax.ShapeDtypeStruct((length, KEY_VALUE_HEADS * HEAD_SIZE), BF),
+            jax.ShapeDtypeStruct((length, KEY_VALUE_HEADS * HEAD_SIZE), BF),
         ),
         grid_spec=pltpu.PrefetchScalarGridSpec(
             num_scalar_prefetch=1,
-            grid=(QUERY_HEADS,),
+            grid=(QUERY_HEADS // HEADS_AT_ONCE,),
             in_specs=[
-                pl.BlockSpec((tokens, HEAD_SIZE), by_head),
+                pl.BlockSpec((tokens, HEADS_AT_ONCE * HEAD_SIZE), by_head),
                 pl.BlockSpec((length, HEAD_SIZE), by_group),
-                pl.BlockSpec((length, HEAD_SIZE), by_group),
-                pl.BlockSpec((tokens, HEAD_SIZE), by_head),
-                pl.BlockSpec((1, 1, tokens), lambda h, m: (h, 0, 0)),
+                pl.BlockSpec((length, HEAD_SIZE), lambda h, m: (0, KEY_VALUE_HEADS + h * HEADS_AT_ONCE // GROUP)),
+                pl.BlockSpec((tokens, HEADS_AT_ONCE * HEAD_SIZE), by_head),
+                pl.BlockSpec((HEADS_AT_ONCE, 1, tokens), lambda h, m: (h, 0, 0)),
                 pl.BlockSpec((tokens, HEAD_SIZE), const),
                 pl.BlockSpec((tokens, HEAD_SIZE), const),
                 pl.BlockSpec((length, 1), const),
                 pl.BlockSpec((1, tokens), const),
             ],
             out_specs=[
-                pl.BlockSpec((tokens, HEAD_SIZE), by_head),
+                pl.BlockSpec((tokens, HEADS_AT_ONCE * HEAD_SIZE), by_head),
                 pl.BlockSpec((length, HEAD_SIZE), by_group),
                 pl.BlockSpec((length, HEAD_SIZE), by_group),
             ],
             scratch_shapes=[
                 pltpu.VMEM((length, tokens), F32),
-                pltpu.VMEM((length, tq), F32),
-                pltpu.VMEM((length, tq), F32),
+                pltpu.VMEM((HEADS_AT_ONCE, length, tq), F32),
+                pltpu.VMEM((HEADS_AT_ONCE, length, tq), F32),
                 pltpu.VMEM((HEAD_SIZE, length), BF),
                 pltpu.VMEM((length, HEAD_SIZE), F32),
                 pltpu.VMEM((length, HEAD_SIZE), F32),
@@ -281,7 +298,7 @@
             bytes_accessed=8 * tokens * MODEL_WIDTH,
         ),
         name="attn_bwd",
-    )(meta, q, k, v, do, lse, cos, sin, segk, segq)
+    )(meta, q, kv, kv, do, lse, cos, sin, segk, segq)
 
 
 def remote(src, dst, ss, rs, axis, dev):
@@ -292,11 +309,11 @@
 
 
 def moe_kernel(cap, tile, n,
-               x_hbm, cot_hbm, cotl_hbm, cotr_hbm, meta_hbm, gate_hbm, up_hbm, down_hbm,
-               dn_out, dw_out, py_out, grads_out, xall, cotall,
+               x_hbm, cot_hbm, cotl_hbm, cotr_hbm, cot2_hbm, meta_hbm, gate_hbm, up_hbm, down_hbm,
+               dn_out, dw_out, py_out, grads_out, xall, cotfar,
                gate_ref, up_ref, down_ref, x_ref, cot_ref, metas, xs_ref, dy_ref, hb_ref, dg_ref,
-               du_ref, pdn_ref, py_ref, dws, pick_ref, put_ref, ys_ref, acc_ref, stage,
-               wsem, lsem, xs_send, xs_recv, cs_send, cs_recv, m_send, m_recv, dn_send, dn_recv,
+               du_ref, pdn_ref, transit, py_ref, dws, pick_ref, put_ref, ys_ref, acc_ref, stage,
+               wsem, lsem, xs_send, xs_recv, far_sem, m_send, m_recv, dn_send, dn_recv,
                dw_send, dw_recv, py_sem, own_sem, st_sem):
     me = lax.axis_index("expert")
     tokens, width = x_ref.shape
@@ -317,26 +334,27 @@
             return (me - step >= 0) & (me < n - 1)
         return (me + step <= n - 1) & (me > 0)
 
-    def stream(direction, step, own, table, ss, rs, near=None):
-        block = me - step if direction == 0 else me + step
-        block = jnp.clip(block, 0, n - 1)
+    def xcopy(direction, step):
+        block = jnp.clip(me - step if direction == 0 else me + step, 0, n - 1)
         target = jnp.clip(me + 1 if direction == 0 else me - 1, 0, n - 1)
-        if step == 0:
-            src = own
-        elif step == 1 and near is not None:
-            src = near[direction]
-        else:
-            src = table.at[block]
-        return remote(src, table.at[block], ss.at[direction, step], rs.at[direction, step],
-                      "expert", target)
-
-    xcopy = lambda d, s: stream(d, s, x_hbm, xall, xs_send, xs_recv)
-    ccopy = lambda d, s: stream(d, s, cot_hbm, cotall, cs_send, cs_recv, (cotl_hbm, cotr_hbm))
+        src = x_hbm if step == 0 else xall.at[block]
+        return remote(src, xall.at[block], xs_send.at[direction, step],
+                      xs_recv.at[direction, step], "expert", target)
+
+    outward = jnp.where(me < 2, 0, n - 1)
+    inward = n - 1 - jnp.clip(me, 1, n - 2)
+    inner = jnp.where(me < 2, 1, n - 2)
+    far_copy = lambda: remote(cot2_hbm, cotfar, far_sem.at[0], far_sem.at[1], "expert", outward)
+    middle_device = jnp.logical_not(edge)
 
     for d in range(2):
         @pl.when(sends(d, 0))
         def _():
             xcopy(d, 0).start()
+
+    @pl.when(middle_device)
+    def _():
+        far_copy().start()
 
     def meta_copy(j):
         return remote(meta_hbm.at[j], metas.at[me], m_send.at[j], m_recv.at[me], "expert", j)
@@ -361,6 +379,21 @@
         cx.wait()
         cc.wait()
 
+    pieces = 4
+    part_rows = tokens // pieces
+    piece = lambda part: pl.ds(part * part_rows, part_rows)
+
+    def edge_copy(kind, part):
+        dst = dn_out.at[1, piece(part)] if kind == 0 else transit.at[kind - 1, piece(part)]
+        return remote(pdn_ref.at[kind, piece(part)], dst, dn_send.at[kind, part],
+                      dn_recv.at[kind, part], "expert", inner)
+
+    def pass_copy(kind, part):
+        dst = transit.at[2, piece(part)] if kind == 1 else dn_out.at[2, piece(part)]
+        arrival = dn_recv.at[3, part] if kind != 1 else dn_recv.at[4, part]
+        return remote(transit.at[kind, piece(part)], dst, dn_send.at[kind, part], arrival,
+                      "expert", outward if kind == 2 else inward)
+
     mirror = me >= 2
     side = jnp.where(mirror, n - 1 - me, me)
 
@@ -372,14 +405,11 @@
         @pl.when(exists(direction, step))
         def _():
             xcopy(direction, step).wait_recv()
-            if step > 0:
-                ccopy(direction, step).wait_recv()
 
     def forward(direction, step):
         @pl.when(sends(direction, step))
         def _():
             xcopy(direction, step).start()
-            ccopy(direction, step).start()
 
     def one_source(p, _):
         src = source_of(p)
@@ -407,6 +437,7 @@
         def _():
             for d in range(2):
                 arrive(d, 2)
+            far_copy().wait_recv()
 
         @pl.when((p > 0) & (src == me - 1))
         def _():
@@ -416,9 +447,13 @@
         def _():
             fetch(xall.at[src], cotr_hbm)
 
-        @pl.when((src < me - 1) | (src > me + 1))
-        def _():
-            fetch(xall.at[src], cotall.at[src])
+        @pl.when((src == me - 2) | (src == me + 2))
+        def _():
+            fetch(xall.at[src], cot2_hbm)
+
+        @pl.when((src == me - 3) | (src == me + 3))
+        def _():
+            fetch(xall.at[src], cotfar)
 
         @pl.when(p > 0)
         def _():
@@ -442,7 +477,7 @@
             put = here if put is None else put | here
         put_ref[...] = jnp.where(put, 1.0, 0.0).astype(BF)
         mine = pl.ds(pl.multiple_of(p * cap, cap), cap)
-        buf = lax.rem(p, 2)
+        buf = lax.rem(p + 2, 3)
 
         def gather(j, _):
             cols = pl.ds(pl.multiple_of(j * tile, tile), tile)
@@ -471,17 +506,13 @@
 
         lax.fori_loop(0, hidden // tile, middle, 0)
 
-        @pl.when(p >= 2)
-        def _():
-            pltpu.make_async_copy(py_ref.at[buf], py_out.at[0], py_sem.at[buf]).wait()
-            @pl.when(p == 2)
-            def _():
-                pltpu.make_async_copy(pdn_ref.at[buf], dn_out.at[me], own_sem.at[0]).wait()
-            @pl.when(p == 3)
-            def _():
-                earlier = source_of(1)
-                remote(pdn_ref.at[buf], dn_out.at[me], dn_send.at[earlier], dn_recv.at[me],
-                       "expert", earlier).wait_send()
+        @pl.when(p > 0)
+        def _():
+            pltpu.make_async_copy(py_ref, py_out.at[0], py_sem.at[0]).wait()
+
+        @pl.when(p == 3)
+        def _():
+            pltpu.make_async_copy(pdn_ref.at[2], dn_out.at[0], own_sem.at[0]).wait()
 
         acc_ref[...] = jnp.zeros_like(acc_ref)
 
@@ -498,12 +529,13 @@
 
         @pl.when(p == 0)
         def _():
-            pltpu.make_async_copy(pdn_ref.at[buf], dn_out.at[me], own_sem.at[0]).start()
-
-        @pl.when(p > 0)
-        def _():
-            remote(pdn_ref.at[buf], dn_out.at[me], dn_send.at[src], dn_recv.at[me], "expert",
-                   src).start()
+            pltpu.make_async_copy(pdn_ref.at[2], dn_out.at[0], own_sem.at[0]).start()
+
+        for kind in range(3):
+            @pl.when(edge & (p == kind + 1))
+            def _():
+                for part in range(pieces):
+                    edge_copy(kind, part).start()
 
         def ahead(j, _):
             cols = pl.ds(pl.multiple_of(j * tile, tile), tile)
@@ -512,11 +544,11 @@
                 y = mm_nt(hb_ref[e, mine, :], down_ref[e, cols, :])
                 acc_ref[rows, :] += mm(pick_ref[rows, :], cot_ref[:, cols]) * y
                 ys_ref[rows, :] = (weights[e] * y).astype(BF)
-            py_ref[buf, :, cols] = mm(put_ref[...], ys_ref[...]).astype(BF)
+            py_ref[:, cols] = mm(put_ref[...], ys_ref[...]).astype(BF)
             return 0
 
         lax.fori_loop(0, width // tile, ahead, 0)
-        pltpu.make_async_copy(py_ref.at[buf], py_out.at[src], py_sem.at[buf]).start()
+        pltpu.make_async_copy(py_ref, py_out.at[src], py_sem.at[0]).start()
         dws[p] = jnp.zeros((8, tokens), F32)
         for e in range(local):
             dot = jnp.sum(acc_ref[pl.ds(e * cap, cap), :], axis=1, keepdims=True)
@@ -559,20 +591,37 @@
     for k in range(2):
         store(k, 0, 0).wait()
 
-    for k in range(2):
-        pltpu.make_async_copy(py_ref.at[k], py_out.at[0], py_sem.at[k]).wait()
+    @pl.when(middle_device)
+    def _():
+        for kind, own in ((0, 1), (1, 2), (2, 0)):
+            for part in range(pieces):
+                landed = (edge_copy(kind + 1, part) if kind < 2 else pass_copy(1, part))
+                landed.wait_recv()
+                rows = piece(part)
+                transit[kind, rows, :] = (transit[kind, rows, :].astype(F32)
+                                          + pdn_ref[own, rows, :].astype(F32)).astype(BF)
+                pass_copy(kind, part).start()
+        for part in range(pieces):
+            edge_copy(0, part).wait_recv()
+            pass_copy(0, part).wait_recv()
+            for kind in range(3):
+                pass_copy(kind, part).wait_send()
+        far_copy().wait_send()
+
+    @pl.when(edge)
+    def _():
+        for part in range(pieces):
+            pass_copy(0, part).wait_recv()
+            for kind in range(3):
+                edge_copy(kind, part).wait_send()
+
+    pltpu.make_async_copy(py_ref, py_out.at[0], py_sem.at[0]).wait()
     pltpu.make_async_copy(dws.at[0], dw_out.at[me], own_sem.at[1]).wait()
     for d in range(2):
         for s in range(n - 1):
             @pl.when(sends(d, s))
             def _():
                 xcopy(d, s).wait_send()
-                if s > 0:
-                    ccopy(d, s).wait_send()
-    last = [source_of(p) for p in range(n)]
-    for p in (2, 3):
-        remote(pdn_ref.at[p % 2], dn_out.at[me], dn_send.at[last[p]], dn_recv.at[me], "expert",
-               last[p]).wait_send()
     for j in range(n):
         @pl.when(me != j)
         def _():
@@ -580,11 +629,9 @@
             remote(dws.at[0], dw_out.at[me], dw_send.at[j], dw_recv.at[me], "expert",
                    j).wait_send()
             remote(dws.at[0], dw_out.at[j], dw_send.at[j], dw_recv.at[j], "expert", j).wait_recv()
-            remote(pdn_ref.at[0], dn_out.at[j], dn_send.at[j], dn_recv.at[j], "expert",
-                   j).wait_recv()
-
-
-def moe(x, cot, cot_left, cot_right, meta, gate, up, down, cap):
+
+
+def moe(x, cot, cot_left, cot_right, cot_second, meta, gate, up, down, cap):
     n = meta.shape[0]
     tokens, width = x.shape
     local, _, hidden = gate.shape
@@ -595,11 +642,11 @@
     return pl.pallas_call(
         functools.partial(moe_kernel, cap, tile, n),
         out_shape=(
-            shape((n, tokens, width), BF), shape((n, 8, tokens), F32), shape((n, tokens, width), BF),
+            shape((3, tokens, width), BF), shape((n, 8, tokens), F32), shape((n, tokens, width), BF),
             shape((local, width, 3 * hidden), BF),
-            shape((n, tokens, width), BF), shape((n, tokens, width), BF),
-        ),
-        in_specs=[anywhere] * 8,
+            shape((n, tokens, width), BF), shape((tokens, width), BF),
+        ),
+        in_specs=[anywhere] * 9,
         out_specs=[anywhere] * 6,
         scratch_shapes=[
             pltpu.VMEM((local, width, hidden), BF), pltpu.VMEM((local, width, hidden), BF),
@@ -609,14 +656,13 @@
             pltpu.VMEM((local, n * cap, width), BF), pltpu.VMEM((local, n * cap, width), BF),
             pltpu.VMEM((local, n * cap, hidden), BF), pltpu.VMEM((local, n * cap, hidden), BF),
             pltpu.VMEM((local, n * cap, hidden), BF),
-            pltpu.VMEM((2, tokens, width), BF), pltpu.VMEM((2, tokens, width), BF),
-            pltpu.VMEM((n, 8, tokens), F32),
+            pltpu.VMEM((3, tokens, width), BF), pltpu.VMEM((3, tokens, width), BF),
+            pltpu.VMEM((tokens, width), BF), pltpu.VMEM((n, 8, tokens), F32),
             pltpu.VMEM((local * cap, tokens), BF), pltpu.VMEM((tokens, local * cap), BF),
             pltpu.VMEM((local * cap, tile), BF), pltpu.VMEM((local * cap, tile), F32),
             pltpu.VMEM((2, tile, 3 * hidden), BF),
-            dma((3,)), dma((3,)), dma((2, n - 1)), dma((2, n - 1)), dma((2, n - 1)),
-            dma((2, n - 1)), dma((n,)), dma((n,)), dma((n,)), dma((n,)), dma((n,)), dma((n,)),
-            dma((2,)), dma((2,)), dma((2,)),
+            dma((3,)), dma((3,)), dma((2, n - 1)), dma((2, n - 1)), dma((2,)), dma((n,)), dma((n,)),
+            dma((3, 4)), dma((5, 4)), dma((n,)), dma((n,)), dma((1,)), dma((2,)), dma((2,)),
         ],
         compiler_params=pltpu.CompilerParams(
             vmem_limit_bytes=MOE_VMEM, collective_id=1, has_side_effects=True
@@ -627,11 +673,252 @@
             bytes_accessed=2 * (8 * n * tokens * width + 6 * local * width * hidden),
         ),
         name="moe",
-    )(x, cot, cot_left, cot_right, meta, gate, up, down)
+    )(x, cot, cot_left, cot_right, cot_second, meta, gate, up, down)
 
 
 RIGHT = [(0, 1), (1, 2), (2, 3)]
 LEFT = [(1, 0), (2, 1), (3, 2)]
+RIGHT_ON = [(1, 2), (2, 3)]
+LEFT_ON = [(1, 0), (2, 1)]
+
+
+def project_kernel(x_ref, wq_own, wk_own, wv_own, small_own, cos_ref, sin_ref,
+                   q_ref, xa_ref, kv_ref, wq_ref, wk_ref, wv_ref, small_ref,
+                   small_in, root_ref, acc_ref, send_sem, recv_sem, own_sem):
+    ctx = lax.axis_index("context")
+    tokens, width = x_ref.shape
+    kv_width = wk_ref.shape[1]
+    half = width // 2
+    barrier = pltpu.get_barrier_semaphore()
+    pl.semaphore_signal(barrier, inc=1, device_id={"context": 1 - ctx},
+                        device_id_type=pl.DeviceIdType.MESH)
+    pl.semaphore_wait(barrier, 1)
+
+    own = pl.ds(pl.multiple_of(ctx * half, 128), half)
+    other = pl.ds(pl.multiple_of((1 - ctx) * half, 128), half)
+    ours = pl.ds(pl.multiple_of(ctx * tokens, 16), tokens)
+    give = lambda k, src, dst: remote(src, dst, send_sem.at[k], recv_sem.at[k], "context", 1 - ctx)
+    weights = ((wk_own, wk_ref), (wv_own, wv_ref), (wq_own, wq_ref))
+    sends = [give(0, small_own, small_in)]
+    sends += [give(1 + k, a, b.at[own, :]) for k, (a, b) in enumerate(weights)]
+    for copy in sends:
+        copy.start()
+    keeps = [pltpu.make_async_copy(a, b.at[own, :], own_sem.at[k])
+             for k, (a, b) in enumerate(weights)]
+    for copy in keeps:
+        copy.start()
+
+    strip = 64
+
+    def scale(k, _):
+        rows = pl.ds(pl.multiple_of(k * strip, strip), strip)
+        root = inverse_root(x_ref[rows, :].astype(F32))
+        root_ref[rows, :] = root
+        xa_ref[rows, own] = (x_ref[rows, own].astype(F32) * root * small_own[0:1, :]).astype(BF)
+        return 0
+
+    lax.fori_loop(0, tokens // strip, scale, 0)
+    for copy in keeps:
+        copy.wait()
+
+    acc_ref[:, 0:kv_width] = mm(xa_ref[:, own], wk_ref[own, :])
+    acc_ref[:, kv_width : 2 * kv_width] = mm(xa_ref[:, own], wv_ref[own, :])
+    tile = 256
+
+    def first(j, _):
+        cols = pl.ds(pl.multiple_of(j * tile, tile), tile)
+        at = pl.ds(pl.multiple_of(2 * kv_width + j * tile, tile), tile)
+        acc_ref[:, at] = mm(xa_ref[:, own], wq_ref[own, cols])
+        return 0
+
+    lax.fori_loop(0, width // tile, first, 0)
+
+    sends[0].wait()
+    small_ref[:, own] = small_own[...]
+    small_ref[:, other] = small_in[...]
+
+    def rest(k, _):
+        rows = pl.ds(pl.multiple_of(k * strip, strip), strip)
+        xa_ref[rows, other] = (x_ref[rows, other].astype(F32) * root_ref[rows, :]
+                               * small_in[0:1, :]).astype(BF)
+        return 0
+
+    lax.fori_loop(0, tokens // strip, rest, 0)
+
+    def rope(v):
+        parts = []
+        for h in range(v.shape[1] // HEAD_SIZE):
+            t = v[:, h * HEAD_SIZE : (h + 1) * HEAD_SIZE]
+            t = t * cos_ref[...] + pltpu.roll(t, HEAD_SIZE // 2, 1) * sin_ref[...]
+            parts.append(t.astype(BF))
+        return jnp.concatenate(parts, axis=1)
+
+    sends[1].wait()
+    sends[2].wait()
+    k = acc_ref[:, 0:kv_width] + mm(xa_ref[:, other], wk_ref[other, :])
+    v = acc_ref[:, kv_width : 2 * kv_width] + mm(xa_ref[:, other], wv_ref[other, :])
+    kv_ref[ours, 0:kv_width] = rope(k)
+    kv_ref[ours, kv_width : 2 * kv_width] = v.astype(BF)
+    kv_copy = give(4, kv_ref.at[ours, :], kv_ref.at[ours, :])
+    kv_copy.start()
+    sends[3].wait()
+
+    def second(j, _):
+        cols = pl.ds(pl.multiple_of(j * tile, tile), tile)
+        at = pl.ds(pl.multiple_of(2 * kv_width + j * tile, tile), tile)
+        q_ref[:, cols] = rope(acc_ref[:, at] + mm(xa_ref[:, other], wq_ref[other, cols]))
+        return 0
+
+    lax.fori_loop(0, width // tile, second, 0)
+    kv_copy.wait()
+
+
+def project(x, wq, wk, wv, small, cos, sin):
+    tokens, width = x.shape
+    kv_width = wk.shape[1]
+    vmem = pl.BlockSpec(memory_space=pltpu.VMEM)
+    anywhere = pl.BlockSpec(memory_space=pl.ANY)
+    dma = pltpu.SemaphoreType.DMA
+    shape = jax.ShapeDtypeStruct
+    return pl.pallas_call(
+        project_kernel,
+        out_shape=(
+            shape((tokens, width), BF), shape((tokens, width), BF),
+            shape((2 * tokens, 2 * kv_width), BF), shape((width, width), BF),
+            shape((width, kv_width), BF), shape((width, kv_width), BF),
+            shape((small.shape[0], width), F32),
+        ),
+        in_specs=[vmem, anywhere, anywhere, anywhere, vmem, vmem, vmem],
+        out_specs=[vmem] * 7,
+        scratch_shapes=[
+            pltpu.VMEM(small.shape, F32), pltpu.VMEM((tokens, 1), F32),
+            pltpu.VMEM((tokens, width + 2 * kv_width), F32), dma((5,)), dma((5,)), dma((3,)),
+        ],
+        compiler_params=pltpu.CompilerParams(
+            vmem_limit_bytes=VMEM_LIMIT, collective_id=3, has_side_effects=True
+        ),
+        cost_estimate=pl.CostEstimate(
+            flops=2 * tokens * width * (width + 2 * kv_width), transcendentals=0,
+            bytes_accessed=8 * width * width,
+        ),
+        name="project",
+    )(x, wq, wk, wv, small, cos, sin)
+
+
+def exact(a, b, dims):
+    return lax.dot_general(a, b, (dims, ((), ())), precision=lax.Precision.HIGHEST,
+                           preferred_element_type=F32)
+
+
+def mix_kernel(strip, ob_ref, x_ref, wo_ref, small_ref, routed_ref,
+               hidden_ref, xq_ref, gates_ref):
+    j = pl.program_id(0)
+    tile = wo_ref.shape[1]
+    cols = pl.ds(pl.multiple_of(j * tile, tile), tile)
+    hidden_ref[:, cols] = x_ref[:, cols].astype(F32) + mm(ob_ref[...], wo_ref[...])
+
+    @pl.when(j == pl.num_programs(0) - 1)
+    def _():
+        def one(k, _):
+            rows = pl.ds(pl.multiple_of(k * strip, strip), strip)
+            h = hidden_ref[rows, :]
+            normed = h * inverse_root(h) * small_ref[1:2, :]
+            xq_ref[rows, :] = normed.astype(BF)
+            logits = exact(normed, small_ref[8:16, :], ((1,), (1,)))
+            routed = routed_ref[rows, :] > 0.0
+            top = jnp.max(jnp.where(routed, logits, NEG), axis=1, keepdims=True)
+            power = jnp.where(routed, jnp.exp(jnp.where(routed, logits, top) - top), 0.0)
+            gates_ref[rows, :] = power / jnp.sum(power, axis=1, keepdims=True)
+            return 0
+
+        lax.fori_loop(0, hidden_ref.shape[0] // strip, one, 0)
+
+
+def row_strip(tokens):
+    return 128 if tokens % 128 == 0 else 64
+
+
+def mix(ob, x, wo, small, routed):
+    tokens, width = x.shape
+    tile = 256
+    shape = jax.ShapeDtypeStruct
+    const = lambda v: pl.BlockSpec(v.shape, lambda j: (0, 0), pipeline_mode=pl.Buffered(1))
+    whole = lambda d: pl.BlockSpec((tokens, d), lambda j: (0, 0))
+    experts = routed.shape[1]
+    return pl.pallas_call(
+        functools.partial(mix_kernel, row_strip(tokens)),
+        out_shape=(shape((tokens, width), F32), shape((tokens, width), BF),
+                   shape((tokens, experts), F32)),
+        grid=(width // tile,),
+        in_specs=[const(ob), const(x), pl.BlockSpec((width, tile), lambda j: (0, j)), const(small),
+                  const(routed)],
+        out_specs=[whole(width), whole(width), whole(experts)],
+        compiler_params=pltpu.CompilerParams(vmem_limit_bytes=VMEM_LIMIT),
+        cost_estimate=pl.CostEstimate(
+            flops=2 * tokens * width * width, transcendentals=0, bytes_accessed=4 * width * width),
+        name="mix",
+    )(ob, x, wo, small, routed)
+
+
+def turn_kernel(strip, flags, dn_ref, dot_ref, gates_ref, hidden_ref, cot_ref, wo_ref, small_ref,
+                dh_ref, da_ref, dob_ref, misc_ref, normed_ref, dlog_ref):
+    j = pl.program_id(0)
+
+    @pl.when(j == 0)
+    def _():
+        gain = small_ref[1:2, :]
+
+        def one(k, total):
+            rows = pl.ds(pl.multiple_of(k * strip, strip), strip)
+            gates, dot = gates_ref[rows, :], dot_ref[rows, :]
+            dlogits = gates * (dot - jnp.sum(gates * dot, axis=1, keepdims=True))
+            dn = exact(dlogits, small_ref[8:16, :], ((1,), (0,)))
+            for part in range(dn_ref.shape[0]):
+                dn = dn + jnp.where(flags[part] > 0, dn_ref[part, rows, :].astype(F32), 0.0)
+            h = hidden_ref[rows, :]
+            root = inverse_root(h)
+            scaled = h * root
+            normed_ref[rows, :] = scaled * gain
+            dlog_ref[rows, :] = dlogits
+            dh = cot_ref[rows, :].astype(F32) + norm_back(h, root, gain, dn)
+            dh_ref[rows, :] = dh
+            da_ref[rows, :] = dh.astype(BF)
+            return total + fold_rows(dn * scaled, jnp.sum)
+
+        tokens, width = dh_ref.shape
+        misc_ref[8:16, :] = lax.fori_loop(0, tokens // strip, one, jnp.zeros((8, width), F32))
+
+    tile = wo_ref.shape[0]
+    cols = pl.ds(pl.multiple_of(j * tile, tile), tile)
+    dob_ref[:, cols] = mm_nt(da_ref[...], wo_ref[...]).astype(BF)
+    misc_ref[0:8, cols] = exact(dlog_ref[...], normed_ref[:, cols], ((0,), (0,)))
+
+
+def turn(flags, dn_parts, dot, gates, hidden, cot, wo, small):
+    tokens, width = cot.shape
+    tile = 256
+    shape = jax.ShapeDtypeStruct
+    once = pl.Buffered(1)
+    const = lambda v: pl.BlockSpec(v.shape, lambda j, f: (0,) * v.ndim, pipeline_mode=once)
+    whole = lambda r: pl.BlockSpec((r, width), lambda j, f: (0, 0))
+    return pl.pallas_call(
+        functools.partial(turn_kernel, row_strip(tokens)),
+        out_shape=(shape((tokens, width), F32), shape((tokens, width), BF),
+                   shape((tokens, width), BF), shape((16, width), F32)),
+        grid_spec=pltpu.PrefetchScalarGridSpec(
+            num_scalar_prefetch=1,
+            grid=(width // tile,),
+            in_specs=[const(dn_parts), const(dot), const(gates), const(hidden), const(cot),
+                      pl.BlockSpec((tile, width), lambda j, f: (j, 0)), const(small)],
+            out_specs=[whole(tokens), whole(tokens), whole(tokens), whole(16)],
+            scratch_shapes=[pltpu.VMEM((tokens, width), F32),
+                            pltpu.VMEM((tokens, gates.shape[1]), F32)],
+        ),
+        compiler_params=pltpu.CompilerParams(vmem_limit_bytes=VMEM_LIMIT),
+        cost_estimate=pl.CostEstimate(
+            flops=2 * tokens * width * width, transcendentals=0, bytes_accessed=8 * width * width),
+        name="turn",
+    )(flags, dn_parts, dot, gates, hidden, cot, wo, small)
 
 
 WIDE = 512
@@ -728,7 +1015,8 @@
                 return 0
             lax.fori_loop(0, width // 256, one, 0)
         else:
-            part[c % 3, :, 0:128] = misc_ref[...]
+            part[c % 3, :, 0:128] = jnp.zeros((width, 128), BF)
+            part[c % 3, :, 0:16] = misc_rows.T.astype(BF)
             part[c % 3, :, 16:24] = gain_rows.T.astype(BF)
 
     def finish(c):
@@ -771,6 +1059,7 @@
             finish(c)
 
     gain_rows = None
+    misc_rows = misc_ref[...]
     for t in range(chunks + LINKS):
         for c in range(chunks):
             if 0 <= t - c <= LINKS:
@@ -846,15 +1135,16 @@
     gate_weight, up_weight, down_weight,
 ):
     context_index = lax.axis_index("context")
+    context_size = lax.axis_size("context")
     expert_size = lax.axis_size("expert")
     rows = tokens.shape[1]
     length = segment_ids.shape[1]
     kv_width = KEY_VALUE_HEADS * HEAD_SIZE
-    gather = lambda w: lax.all_gather(w, "context", axis=0, tiled=True)
-
-    upstream_low = cotangent[0]
-    cot_left = lax.ppermute(upstream_low, "expert", RIGHT)
-    cot_right = lax.ppermute(upstream_low, "expert", LEFT)
+    gather = lambda w, axis=0: lax.all_gather(w, "context", axis=axis, tiled=True)
+    x, upstream = tokens[0], cotangent[0]
+
+    cot_left = lax.ppermute(upstream, "expert", RIGHT)
+    cot_right = lax.ppermute(upstream, "expert", LEFT)
 
     expert_count = router_weight.shape[1]
     local = gate_weight.shape[0]
@@ -868,52 +1158,57 @@
     order = jnp.where(routed, order, rows * TOP).T
     slots = jnp.sum((order[:, :, None] < order[:, None, :]).astype(jnp.int32), axis=1)
     kept = routed.T & (slots < capacity)
-    slots = jnp.where(kept, slots, -1)
+    slots = jnp.where(kept, slots, -1).astype(F32)
     kept_float = kept.T.astype(F32)
 
-    query_full, key_full, value_full, output_full, router_full, gain_first, gain_second = (
-        gather(query_weight), gather(key_projection_weight), gather(value_projection_weight),
-        gather(output_weight), gather(router_weight), gather(gain_attention), gather(gain_experts),
-    )
-    router_float = router_full.astype(F32)
-    gain_first = gain_first.astype(F32)
-    gain_second = gain_second.astype(F32)
-    residual = tokens[0].astype(F32)
-    root_first = inverse_root(residual)
-    attn_input = (residual * root_first * gain_first).astype(BF)
+    small = jnp.concatenate([
+        gain_attention[None], gain_experts[None], jnp.zeros((6, gain_attention.shape[0]), BF),
+        router_weight.T,
+    ]).astype(F32)
     positions = context_index * rows + jnp.arange(rows, dtype=jnp.int32)
     cosine, sine = rope_tables(positions)
     cos_full = jnp.concatenate([cosine, cosine], axis=-1)
     sin_full = jnp.concatenate([-sine, sine], axis=-1)
-    turn = lambda v, heads, d: apply_rotary(
+    turned = lambda v, heads, d: apply_rotary(
         v.reshape(rows, heads, HEAD_SIZE), cosine, sine, d
     ).reshape(rows, heads * HEAD_SIZE)
-    q = turn(mm(attn_input, query_full), QUERY_HEADS, 1.0).astype(BF)
-    k_own = turn(mm(attn_input, key_full), KEY_VALUE_HEADS, 1.0).astype(BF)
-    v_own = mm(attn_input, value_full).astype(BF)
-    kv = gather(jnp.concatenate([k_own, v_own], axis=1))
-    k_all, v_all = kv[:, :kv_width], kv[:, kv_width:]
+    output_full = gather(output_weight)
+    if context_size == 2:
+        q, attn_input, kv, query_full, key_full, value_full, small = project(
+            x, query_weight, key_projection_weight, value_projection_weight, small,
+            cos_full, sin_full,
+        )
+    else:
+        query_full, key_full, value_full = (
+            gather(query_weight), gather(key_projection_weight), gather(value_projection_weight)
+        )
+        small = gather(small.astype(BF), 1).astype(F32)
+        residual = x.astype(F32)
+        attn_input = (residual * inverse_root(residual) * small[0]).astype(BF)
+        q = turned(mm(attn_input, query_full), QUERY_HEADS, 1.0).astype(BF)
+        k_own = turned(mm(attn_input, key_full), KEY_VALUE_HEADS, 1.0).astype(BF)
+        kv = gather(jnp.concatenate([k_own, mm(attn_input, value_full).astype(BF)], axis=1))
     segments = segment_ids[0]
     tq, kb = attention_sizes(rows, length)
-    meta = attention_meta(context_index, rows, segments, tq, kb)
+    spans = attention_meta(context_index, rows, segments, tq, kb)
     segk = segments[:, None]
     segq = lax.dynamic_slice_in_dim(segments, context_index * rows, rows)[None, :]
-    mixed, lse = attention_forward(q, k_all, v_all, meta, segk, segq)
-
-    hidden = residual + mm(mixed, output_full)
-    root_second = inverse_root(hidden)
-    normed = hidden * root_second * gain_second
-    expert_input = normed.astype(BF)
-    logits = precise_dims(normed, router_float, ((1,), (0,)))
-    gates = jax.nn.softmax(jnp.where(routed, logits, -jnp.inf), axis=-1)
-    kept_gates = gates * kept_float
-
-    routing = jnp.stack([slots.astype(F32), kept_gates.T], axis=0)
+    cot_left, cot_right, q, kv, spans, segk, segq, slots, kept_float, routed_float = (
+        lax.optimization_barrier((cot_left, cot_right, q, kv, spans, segk, segq, slots, kept_float,
+                                  routed.astype(F32))))
+    second_left = lax.ppermute(cot_left, "expert", RIGHT_ON)
+    second_right = lax.ppermute(cot_right, "expert", LEFT_ON)
+    mixed, lse = attention_forward(q, kv, spans, segk, segq)
+
+    hidden, expert_input, gates = mix(mixed, x, output_full, small, routed_float)
+    second_left, second_right, gates = lax.optimization_barrier((second_left, second_right, gates))
+    cot_second = second_left + second_right
+    routing = jnp.stack([slots, (gates * kept_float).T], axis=0)
     routing = routing.reshape(2, expert_size, local, rows).transpose(1, 0, 2, 3)
     routing = routing.reshape(expert_size, 2 * local, rows)
     routing = jnp.pad(routing, ((0, 0), (0, 8 - 2 * local), (0, 0)))
     dn_parts, dw_parts, part_y, grads_low, _, _ = moe(
-        expert_input, upstream_low, cot_left, cot_right, routing, gate_weight, up_weight,
+        expert_input, upstream, cot_left, cot_right, cot_second, routing, gate_weight, up_weight,
         down_weight, cap,
     )
     gate_dot = dw_parts[:, :local].reshape(expert_count, rows).T * kept_float
@@ -924,51 +1219,45 @@
     ff = gate_weight.shape[2]
     gate_grad, up_grad, down_grad = (grads_shard[:, :, i * ff : (i + 1) * ff] for i in range(3))
 
-    upstream = upstream_low.astype(F32)
-    logit_grad = gates * (gate_dot - jnp.sum(gates * gate_dot, axis=-1, keepdims=True))
-    normed_grad = jnp.sum(dn_parts.astype(F32), axis=0) + precise_dims(logit_grad, router_float, ((1,), (1,)))
-    router_local = precise_dims(normed, logit_grad, ((0,), (0,)))
-    hidden_total = upstream + norm_back(hidden, root_second, gain_second, normed_grad)
-    gain_second_grad = jnp.sum(normed_grad * hidden * root_second, axis=0)
-    attn_grad_low = hidden_total.astype(BF)
-    mixed_grad_low = mm_nt(attn_grad_low, output_full).astype(BF)
-
+    expert_index = lax.axis_index("expert")
+    between = (expert_index > 0) & (expert_index < expert_size - 1)
+    flags = jnp.where(between, jnp.array([1, 1, 1], jnp.int32), jnp.array([1, 0, 1], jnp.int32))
+    hidden_total, attn_grad_low, mixed_grad_low, misc = turn(
+        flags, dn_parts, gate_dot, gates, hidden, upstream, output_full, small
+    )
     dq_low, dk_part, dv_part = attention_backward(
-        q, k_all, v_all, mixed_grad_low, lse, cos_full, sin_full, meta, segk, segq
+        q, kv, mixed_grad_low, lse, cos_full, sin_full, spans, segk, segq
     )
-    if (lax.axis_size("dp"), lax.axis_size("context"), expert_size) == (4, 2, 4):
-        misc = jnp.concatenate([router_local, gain_second_grad[:, None]], axis=1)
-        misc = jnp.pad(misc, ((0, 0), (0, 128 - misc.shape[1]))).astype(BF)
-        query_grad, key_grad, value_grad, output_grad, misc_grad, grad_tokens = tail(
+    if (lax.axis_size("dp"), context_size, expert_size) == (4, 2, 4):
+        *sums, grad_tokens = tail(
             mixed, attn_grad_low, attn_input, dq_low, dk_part, dv_part, cos_full, sin_full,
-            query_full, key_full, value_full, hidden_total, tokens[0], gain_first[None], misc,
+            query_full, key_full, value_full, hidden_total, x, small[0:1], misc,
         )
-        query_grad, key_grad, value_grad, output_grad, misc_grad = (
-            v.astype(F32) for v in (query_grad, key_grad, value_grad, output_grad, misc_grad)
-        )
+        query_grad, key_grad, value_grad, output_grad, misc_grad = (v.astype(F32) for v in sums)
         sums = (
             query_grad, key_grad, value_grad, output_grad, misc_grad[:, :expert_count],
-            misc_grad[:, 16], misc_grad[:, expert_count],
+            misc_grad[:, 16], jnp.sum(misc_grad[:, 8:16], axis=1),
         )
     else:
         dkv = lax.psum_scatter(
             jnp.concatenate([dk_part, dv_part], axis=1), "context", scatter_dimension=0, tiled=True
         )
-        dk_low = turn(dkv[:, :kv_width].astype(F32), KEY_VALUE_HEADS, -1.0).astype(BF)
+        dk_low = turned(dkv[:, :kv_width].astype(F32), KEY_VALUE_HEADS, -1.0).astype(BF)
         dv_low = dkv[:, kv_width:]
-        input_total = mm_nt(dq_low, query_full) + mm_nt(dk_low, key_full) + mm_nt(dv_low, value_full)
-        query_local = mm_tn(attn_input, dq_low)
-        key_local = mm_tn(attn_input, dk_low)
-        value_local = mm_tn(attn_input, dv_low)
-        grad_tokens = (hidden_total + norm_back(residual, root_first, gain_first, input_total)).astype(BF)
-        gain_first_grad = jnp.sum(input_total * residual * root_first, axis=0)
-
+        input_total = (
+            mm_nt(dq_low, query_full) + mm_nt(dk_low, key_full) + mm_nt(dv_low, value_full)
+        )
+        residual = x.astype(F32)
+        root = inverse_root(residual)
+        grad_tokens = (hidden_total + norm_back(residual, root, small[0], input_total)).astype(BF)
         reduce_rows = lambda v: lax.psum(
-            lax.psum_scatter(v.astype(BF), "context", scatter_dimension=0, tiled=True), ("dp", "expert")
+            lax.psum_scatter(v.astype(BF), "context", scatter_dimension=0, tiled=True),
+            ("dp", "expert"),
         ).astype(F32)
         sums = tuple(reduce_rows(v) for v in (
-            query_local, key_local, value_local, mm_tn(mixed, attn_grad_low), router_local,
-            gain_first_grad, gain_second_grad,
+            mm_tn(attn_input, dq_low), mm_tn(attn_input, dk_low), mm_tn(attn_input, dv_low),
+            mm_tn(mixed, attn_grad_low), misc[:8].T,
+            jnp.sum(input_total * residual * root, axis=0), jnp.sum(misc[8:16], axis=0),
         ))
     late, grad_tokens = lax.optimization_barrier((hidden, grad_tokens))
     layer_out = (late + jnp.sum(y_parts.astype(F32), axis=0)).astype(BF)

time: 670 us -> 578 us (0.86)
  Pallas kernels: 513 us -> 480 us
  matrix products: 28.3 us -> 0 us
  waiting for transfers between devices: 2.03 us -> 17 us
  local copies, waits for them, and re-layouts: 29.2 us -> 15.5 us
  blocking collectives: 12.5 us -> 0 us
  other arithmetic: 41.8 us -> 29.3 us
  starting transfers between devices: 22.1 us -> 15.1 us
    pallas_call x1, Pallas kernels: 286 us -> 220 us  [moe(): pl.pallas_call(functools.partial(moe_kernel, cap, tile, n), out_shape=(sh...]
    pallas_call x0 -> x3, Pallas kernels: none -> 47.4 us  [the longest x1 19.5 us: turn(): pl.pallas_call(functools.partial(turn_kernel, row_strip(tokens)), out_sha...]
    dot_general x8 -> x0, matrix products: 28.3 us -> none  [the longest x4 13.5 us: mm(): return jnp.dot(a, b, preferred_element_type=F32)]
    ppermute x2 -> x4, waiting for transfers between devices: 0.01 us -> 16.3 us  [the longest x1 10.2 us: body(): second_right = lax.ppermute(cot_right, 'expert', LEFT_ON)]
    all_gather x5 -> x0, blocking collectives: 12.5 us -> none  [body(): gather = lambda w: lax.all_gather(w, 'context', axis=0, tiled=True)]
    pallas_call x1, Pallas kernels: 27.1 us -> 18 us  [attention_backward(): pl.pallas_call(functools.partial(attn_bwd_kernel, kb, tq), out_shape=(jax...]
    all_to_all x1, starting transfers between devices: 14.2 us -> 5.46 us  [body(): lax.all_to_all(part_y, 'expert', split_axis=0, concat_axis=0, tiled=True)]
    pallas_call x1, Pallas kernels: 20.8 us -> 12.2 us  [attention_forward(): pl.pallas_call(functools.partial(attn_fwd_kernel, kb, tq), out_shape=(jax...]
  transfers between devices with their start and end apart: 7 -> 7, of which waited for: 1 -> 3; matrix products, arithmetic and copies ran while one was open for 12% -> 6% of each run, Pallas kernels for 34% -> 45%
where the time goes in v4:
time: 578 us; the launch traced here: 577 us
  Pallas kernels  480 us (83%)
  other arithmetic  29.3 us (5%)
  between operations  19.7 us (3%)
  waiting for transfers between devices  17 us (3%)
  local copies, waits for them, and re-layouts  15.5 us (3%)
  starting transfers between devices  15.1 us (3%)
    pallas_call x1, Pallas kernels, moe(): pl.pallas_call(functools.partial(moe_kernel, cap, tile, n), out_shape=(sh...  220 us
    pallas_call x1, Pallas kernels, tail(): pl.pallas_call(tail_kernel, out_shape=(shape((half, width), BF), shape((h...  183 us
    pallas_call x1, Pallas kernels, turn(): pl.pallas_call(functools.partial(turn_kernel, row_strip(tokens)), out_sha...  19.5 us
    pallas_call x1, Pallas kernels, attention_backward(): pl.pallas_call(functools.partial(attn_bwd_kernel, kb, tq), out_shape=(jax...  18 us
    pallas_call x1, Pallas kernels, project(): pl.pallas_call(project_kernel, out_shape=(shape((tokens, width), BF), sha...  14.5 us
    pallas_call x1, Pallas kernels, mix(): pl.pallas_call(functools.partial(mix_kernel, row_strip(tokens)), out_shap...  13.4 us
    pallas_call x1, Pallas kernels, attention_forward(): pl.pallas_call(functools.partial(attn_fwd_kernel, kb, tq), out_shape=(jax...  12.2 us
  transfers between devices with their start and end apart: 7, of which 3 were waited for; matrix products, arithmetic and copies ran while one was open for 6% of the time, Pallas kernels for 45%

profile of v4, /device:TPU:0, one launch (start us, length us, event | category | flops | bytes accessed | tf_op | source)
XLA Modules:
  0.0 576.8 jit_solution(13040700300795571356)
XLA Ops:
  7.2 0.0 all-gather.2.cloned.1.call-start
  7.3 0.7 all-gather.2.cloned.1.call-update
  8.0 0.0 reduce-scatter.2.cloned.1.call-start
  8.0 0.6 copy-done.3
  8.6 6.0 %collective-permute-start = (bf16[512,1536]{1,0:T(8,128)(2,1)S(1)}, bf16[512,1536]{1,0:T(8,128)(2,1)}, u32[]{:S(2)}, u32[]{:S(2)}) collective-permute-start(bf16[512,1536]{1,0:T(8,128)(2,1)S(1)} %bitcast.35), channel_id=1, source_target_pairs={{0,1},{1,2},{2,3},{4,5},{5,6},{6,7},{8,9},{9,10},{10,11},{12,13},{... | collective-permute-start | bytes 4718600 | tf_op jit(solution)/shard_map/ppermute | solution.py:1146
  14.6 1.3 collective-permute-start.1
  15.9 0.6 constant_dynamic-slice_fusion.2
  16.5 1.9 fusion.5
  23.8 0.5 broadcast.36
  24.3 0.7 reduce.7
  25.0 0.3 broadcast_in_dim.46
  25.3 0.1 copy.46
  25.4 0.1 copy.47
  25.6 0.2 copy.45
  25.8 0.1 copy.48
  25.9 1.0 convert_reduce_fusion.1
  26.9 0.1 copy.50
  27.0 0.1 pad.13.clone
  27.1 0.7 stack.32.meta
  27.8 0.6 constant_dynamic-slice_fusion.segq_ref
  28.4 1.0 fusion.2
  29.4 1.0 pad_maximum_fusion
  30.4 0.7 maximum_convert_fusion.small_own
  31.1 0.1 select_convert_fusion
  31.1 0.8 fusion.7
  31.9 14.5 %project.1 = (bf16[512,1536]{1,0:T(8,128)(2,1)}, bf16[512,1536]{1,0:T(8,128)(2,1)}, bf16[1024,512]{1,0:T(8,128)(2,1)}, bf16[1536,1536]{1,0:T(8,128)(2,1)}, bf16[...) custom-call(bf16[512,1536]{1,0:T(8,128)(2,1)} %bitcast.41, bf16[768,1536]{1,0:T(8,128)(2,1)} %wq_own.1, ...), custom_call_target="tpu_custom_call" | custom-call | flops 3221225472 | bytes 18874368 | tf_op jit(solution)/shard_map/project/pallas_call | solution.py:783
  46.4 0.8 collective-permute-done.cotl_hbm
  47.2 5.3 collective-permute-done.1.cotr_hbm
  52.5 0.8 collective-permute-start.2
  53.2 1.5 collective-permute-start.3
  54.7 1.0 copy.54.segk_ref
  55.7 0.1 copy.55
  55.9 12.2 %attn_fwd.1 = (bf16[512,1536]{1,0:T(8,128)(2,1)}, f32[12,1,512]{2,1,0:T(1,128)}) custom-call(s32[5]{0:T(128)} %stack.32.meta, bf16[512,1536]{1,0:T(8,128)(2,1)} %get-tuple-element.59.q_ref, bf16[1024,512]{1,0:T(8,128)(2,1)} %get-tuple-element.60.k_ref.v_ref, bf16[1024,512]{1,0:T(8,128)(2,1)} %get-tuple-element.60.k_ref.v_ref, s32[1024,1]{1,0:T(8,128)} %copy.54.segk_ref, ...), custom_call_target="tpu_custom_call" | custom-call | flops 2415919104 | bytes 3145728 | tf_op jit(solution)/shard_map/attn_fwd/pallas_call | solution.py:217
  68.1 13.4 %mix.1 = (f32[512,1536]{1,0:T(8,128)}, bf16[512,1536]{1,0:T(8,128)(2,1)}, f32[512,8]{1,0:T(8,128)}) custom-call(bf16[512,1536]{1,0:T(8,128)(2,1)} %get-tuple-element.63.ob_ref, bf16[512,1536]{1,0:T(8,128)(2,1)} %bitcast.42, bf16[1536,1536]{1,0:T(8,128)(2,1)} %all-gather.2.cloned.1.call-done.wo_ref, f32[16,1536]{1,0:T(8,128)} %get-tuple-element.64.small_ref, ...), custom_call_target="tpu_custom_call" | custom-call | flops 2415919104 | bytes 9437184 | tf_op jit(solution)/shard_map/mix/pallas_call | solution.py:848
  81.5 10.2 %collective-permute-done.3 = bf16[512,1536]{1,0:T(8,128)(2,1)} collective-permute-done((bf16[512,1536]{1,0:T(8,128)(2,1)}, bf16[512,1536]{1,0:T(8,128)(2,1)}, u32[]{:S(2)}, u32[]{:S(2)}) %collective-permute-start.3) | collective-permute-done | bytes 1572896 | tf_op jit(solution)/shard_map/ppermute | solution.py:1200
  91.7 1.0 multiply_bitcast_fusion
  92.7 0.1 copy.56
  92.8 2.9 add.55.cot2_hbm
  95.8 0.6 pad.4.meta_hbm
  96.4 219.6 %moe.1 = (bf16[3,512,1536]{2,1,0:T(8,128)(2,1)}, f32[4,8,512]{2,1,0:T(8,128)}, bf16[4,512,1536]{2,1,0:T(8,128)(2,1)}, bf16[2,1536,2304]{2,1,0:T(8,128)(2,1)}, bf...) custom-call(bf16[512,1536]{1,0:T(8,128)(2,1)} %get-tuple-element.67.x_hbm, bf16[512,1536]{1,0:T(8,128)(2,1)} %bitcast.33, ...), custom_call_target="tpu_custom_call" | custom-call | flops 74490839040 | bytes 78643200 | tf_op jit(solution)/shard_map/moe/pallas_call | solution.py:642
  316.1 0.0 reduce-scatter.2.cloned.1.call-update
  316.1 5.5 all-to-all-start
  321.6 1.4 slice.25.gain_ref
  323.0 0.5 broadcast_select_fusion.flags
  323.5 0.9 slice.24
  324.4 0.1 copy.58
  324.5 0.7 bitcast_multiply_fusion.dot_ref
  325.3 19.5 %turn.1 = (f32[512,1536]{1,0:T(8,128)}, bf16[512,1536]{1,0:T(8,128)(2,1)}, bf16[512,1536]{1,0:T(8,128)(2,1)}, f32[16,1536]{1,0:T(8,128)}) custom-call(s32[3]{0:T(128)} %broadcast_select_fusion.flags, bf16[3,512,1536]{2,1,0:T(8,128)(2,1)} %get-tuple-element.76.dn_ref, f32[512,8]{1,0:T(8,128)} %bitcast_multiply_fusion.dot_ref, ...), custom_call_target="tpu_custom_call" | custom-call | flops 2415919104 | bytes 18874368 | tf_op jit(solution)/shard_map/turn/pallas_call | solution.py:904
  344.7 18.0 %attn_bwd.1 = (bf16[512,1536]{1,0:T(8,128)(2,1)}, bf16[1024,256]{1,0:T(8,128)(2,1)}, bf16[1024,256]{1,0:T(8,128)(2,1)}) custom-call(s32[5]{0:T(128)} %stack.32.meta, bf16[512,1536]{1,0:T(8,128)(2,1)} %get-tuple-element.59.q_ref, bf16[1024,512]{1,0:T(8,128)(2,1)} %get-tuple-element.60.k_ref.v_ref, bf16[1024,512]{1,0:T(8,128)(2,1)} %get-tuple-element.60.k_ref.v_ref, ...), custom_call_target="tpu_custom_call" | custom-call | flops 6442450944 | bytes 6291456 | tf_op jit(solution)/shard_map/attn_bwd/pallas_call | solution.py:259
  362.7 183.0 %tail.1 = (bf16[768,1536]{1,0:T(8,128)(2,1)}, bf16[768,256]{1,0:T(8,128)(2,1)}, bf16[768,256]{1,0:T(8,128)(2,1)}, bf16[768,1536]{1,0:T(8,128)(2,1)}, bf16[768,12...) custom-call(bf16[512,1536]{1,0:T(8,128)(2,1)} %get-tuple-element.63.ob_ref, bf16[512,1536]{1,0:T(8,128)(2,1)} %get-tuple-element.78.da_ref, ...), custom_call_target="tpu_custom_call" | custom-call | flops 8858370048 | bytes 37748736 | tf_op jit(solution)/shard_map/tail/pallas_call | solution.py:1105
  545.8 1.0 slice.32
  546.7 1.0 convert_element_type.70
  547.7 4.6 convert_element_type.66
  552.3 0.9 convert_element_type.67
  553.2 0.9 convert_element_type.68
  554.2 0.1 copy-done.1
  554.2 2.8 convert_element_type.69
  557.1 0.7 copy.60
  557.8 0.9 slice_reduce_fusion.1
  558.7 0.9 slice_reduce_fusion
  559.6 4.2 convert_reduce_fusion
  563.8 1.6 fusion
  565.4 3.4 fusion.6
  568.8 1.1 copy.62
  (42 shorter events, 0.3 us)
Async XLA Ops:
  7.2 1.4 copy-start.3
  7.2 8.7 %copy-start.7 = (s32[1,1024]{1,0:T(1,128)S(1)}, s32[1,1024]{1,0:T(1,128)}, u32[]{:S(2)}) copy-start(s32[1,1024]{1,0:T(1,128)} %param.19) | copy-start | bytes 12292
  7.2 16.5 %copy-start.10 = (bf16[768]{0:T(1024)(128)(2,1)S(1)}, bf16[768]{0:T(1024)(128)(2,1)}, u32[]{:S(2)}) copy-start(bf16[768]{0:T(1024)(128)(2,1)} %param.28) | copy-start | bytes 4612
  7.2 16.5 %copy-start.11 = (bf16[768]{0:T(1024)(128)(2,1)S(1)}, bf16[768]{0:T(1024)(128)(2,1)}, u32[]{:S(2)}) copy-start(bf16[768]{0:T(1024)(128)(2,1)} %param.27) | copy-start | bytes 4612
  7.2 17.1 %copy-start.9 = (s32[1,1,2048]{2,1,0:T(1,128)S(1)}, s32[1,1,2048]{2,1,0:T(1,128)}, u32[]{:S(2)}) copy-start(s32[1,1,2048]{2,1,0:T(1,128)} %param.21) | copy-start | bytes 24580
  7.2 18.2 %copy-start.6 = (s32[1,512,4]{1,2,0:T(4,128)S(1)}, s32[1,512,4]{1,2,0:T(4,128)}, u32[]{:S(2)}) copy-start(s32[1,512,4]{1,2,0:T(4,128)} %param.20) | copy-start | bytes 24580
  7.2 60.9 %all-gather.2.cloned.1.call-start = ((), (), s32[]{:S(2)}) async-start(), calls=%async_computation.2 | async-start | bytes 7077888 | tf_op jit(solution)/shard_map/all_gather | solution.py:1143
  8.0 22.4 %copy-start.8 = (bf16[768,8]{0,1:T(8,128)(2,1)S(1)}, bf16[768,8]{0,1:T(8,128)(2,1)}, u32[]{:S(2)}) copy-start(bf16[768,8]{0,1:T(8,128)(2,1)} %param.26) | copy-start | bytes 36868
  8.0 557.4 %reduce-scatter.2.cloned.1.call-start = ((), (), s32[]{:S(2)}) async-start(), calls=%async_computation.3 | async-start | bytes 15925248 | tf_op jit(solution)/shard_map/reduce_scatter | solution.py:1216
  8.6 38.6 %collective-permute-start = (bf16[512,1536]{1,0:T(8,128)(2,1)S(1)}, bf16[512,1536]{1,0:T(8,128)(2,1)}, u32[]{:S(2)}, u32[]{:S(2)}) collective-permute-start(bf16[512,1536]{1,0:T(8,128)(2,1)S(1)} %bitcast.35), channel_id=1, source_target_pairs={{0,1},{1,2},{2,3},{4,5},{5,6},{6,7},{8,9},{9,10},{10,11},{12,13},{... | collective-permute-start | bytes 4718600 | tf_op jit(solution)/shard_map/ppermute | solution.py:1146
  14.6 37.8 %collective-permute-start.1 = (bf16[512,1536]{1,0:T(8,128)(2,1)S(1)}, bf16[512,1536]{1,0:T(8,128)(2,1)}, u32[]{:S(2)}, u32[]{:S(2)}) collective-permute-start(bf16[512,1536]{1,0:T(8,128)(2,1)S(1)} %bitcast.36), channel_id=1, source_target_pairs={{1,0},{2,1},{3,2},{5,4},{6,5},{7,6},{9,8},{10,9},{11,10},{13,12},{... | collective-permute-start | bytes 4718600 | tf_op jit(solution)/shard_map/ppermute | solution.py:1147
  52.5 29.0 %collective-permute-start.2 = (bf16[512,1536]{1,0:T(8,128)(2,1)}, bf16[512,1536]{1,0:T(8,128)(2,1)S(1)}, u32[]{:S(2)}, u32[]{:S(2)}) collective-permute-start(bf16[512,1536]{1,0:T(8,128)(2,1)} %collective-permute-done.cotl_hbm), channel_id=1, source_target_pairs={{1,2},{2,3},{5,6},{6,7},{9,10},{10,11},{13,14},{14,15},{17,18},{18... | collective-permute-start | bytes 4718600 | tf_op jit(solution)/shard_map/ppermute | solution.py:1199
  53.2 38.4 %collective-permute-start.3 = (bf16[512,1536]{1,0:T(8,128)(2,1)}, bf16[512,1536]{1,0:T(8,128)(2,1)}, u32[]{:S(2)}, u32[]{:S(2)}) collective-permute-start(bf16[512,1536]{1,0:T(8,128)(2,1)} %collective-permute-done.1.cotr_hbm), channel_id=1, source_target_pairs={{1,0},{2,1},{5,4},{6,5},{9,8},{10,9},{13,12},{14,13},{17,16},{18,1... | collective-permute-start | bytes 4718600 | tf_op jit(solution)/shard_map/ppermute | solution.py:1200
  316.1 6.9 %copy-start.12 = (s32[3]{0:T(128)S(1)}, s32[3]{0:T(128)}, u32[]{:S(2)}) copy-start(s32[3]{0:T(128)} %constant.89.clone) | copy-start | bytes 40
  316.1 243.5 %all-to-all-start = ((bf16[4,512,1536]{2,1,0:T(8,128)(2,1)}), bf16[4,512,1536]{2,1,0:T(8,128)(2,1)}, u32[]{:S(2)}, u32[]{:S(2)}) async-start(bf16[4,512,1536]{2,1,0:T(8,128)(2,1)} %get-tuple-element.92), calls=%async_computation | async-start | bytes 12582912 | tf_op jit(solution)/shard_map/all_to_all | solution.py:1215
  547.7 4.6 copy-start.5
  547.7 5.5 copy-start.4
  552.3 1.9 copy-start.1
  559.6 4.2 copy-start
  565.4 3.4 copy-start.2
Sparse Core Ops, SparseCore 0:
  9.6 17.1 all-gather.1
  316.2 115.8 reduce-scatter.1

commit v5 on v4

--- a/solution.py
+++ b/solution.py
@@ -310,11 +310,11 @@
 
 def moe_kernel(cap, tile, n,
                x_hbm, cot_hbm, cotl_hbm, cotr_hbm, cot2_hbm, meta_hbm, gate_hbm, up_hbm, down_hbm,
-               dn_out, dw_out, py_out, grads_out, xall, cotfar,
+               dn_out, dw_out, y_own, y_near, y_second, y_third, y_in, grads_out, xall, cotfar,
                gate_ref, up_ref, down_ref, x_ref, cot_ref, metas, xs_ref, dy_ref, hb_ref, dg_ref,
                du_ref, pdn_ref, transit, py_ref, dws, pick_ref, put_ref, ys_ref, acc_ref, stage,
                wsem, lsem, xs_send, xs_recv, far_sem, m_send, m_recv, dn_send, dn_recv,
-               dw_send, dw_recv, py_sem, own_sem, st_sem):
+               dw_send, dw_recv, py_sem, own_sem, st_sem, y_send, y_recv):
     me = lax.axis_index("expert")
     tokens, width = x_ref.shape
     local, _, hidden = gate_ref.shape
@@ -351,10 +351,6 @@
         @pl.when(sends(d, 0))
         def _():
             xcopy(d, 0).start()
-
-    @pl.when(middle_device)
-    def _():
-        far_copy().start()
 
     def meta_copy(j):
         return remote(meta_hbm.at[j], metas.at[me], m_send.at[j], m_recv.at[me], "expert", j)
@@ -379,19 +375,24 @@
         cx.wait()
         cc.wait()
 
-    pieces = 4
-    part_rows = tokens // pieces
-    piece = lambda part: pl.ds(part * part_rows, part_rows)
+    pieces = width // tile
+    piece = lambda part: pl.ds(pl.multiple_of(part * tile, tile), tile)
 
     def edge_copy(kind, part):
-        dst = dn_out.at[1, piece(part)] if kind == 0 else transit.at[kind - 1, piece(part)]
-        return remote(pdn_ref.at[kind, piece(part)], dst, dn_send.at[kind, part],
+        dst = (dn_out.at[1, :, piece(part)] if kind == 0 else
+               transit.at[kind - 1, :, piece(part)])
+        return remote(pdn_ref.at[kind, :, piece(part)], dst, dn_send.at[kind, part],
                       dn_recv.at[kind, part], "expert", inner)
 
+    def y_copy(kind):
+        target = jnp.where(edge, inner, outward) if kind == 0 else inward
+        return remote(y_near.at[kind], y_in.at[kind], y_send.at[kind], y_recv.at[kind], "expert",
+                      target)
+
     def pass_copy(kind, part):
-        dst = transit.at[2, piece(part)] if kind == 1 else dn_out.at[2, piece(part)]
+        dst = transit.at[2, :, piece(part)] if kind == 1 else dn_out.at[2, :, piece(part)]
         arrival = dn_recv.at[3, part] if kind != 1 else dn_recv.at[4, part]
-        return remote(transit.at[kind, piece(part)], dst, dn_send.at[kind, part], arrival,
+        return remote(transit.at[kind, :, piece(part)], dst, dn_send.at[kind, part], arrival,
                       "expert", outward if kind == 2 else inward)
 
     mirror = me >= 2
@@ -416,44 +417,7 @@
 
         @pl.when(p == 0)
         def _():
-            fetch(x_hbm, cot_hbm)
             own_meta.wait()
-            for load in loads:
-                load.wait()
-
-        @pl.when(p == 1)
-        def _():
-            for d in range(2):
-                arrive(d, 0)
-                forward(d, 1)
-
-        @pl.when(((p == 2) & edge) | ((p == 3) & jnp.logical_not(edge)))
-        def _():
-            for d in range(2):
-                arrive(d, 1)
-                forward(d, 2)
-
-        @pl.when((p == 3) & edge)
-        def _():
-            for d in range(2):
-                arrive(d, 2)
-            far_copy().wait_recv()
-
-        @pl.when((p > 0) & (src == me - 1))
-        def _():
-            fetch(xall.at[src], cotl_hbm)
-
-        @pl.when((p > 0) & (src == me + 1))
-        def _():
-            fetch(xall.at[src], cotr_hbm)
-
-        @pl.when((src == me - 2) | (src == me + 2))
-        def _():
-            fetch(xall.at[src], cot2_hbm)
-
-        @pl.when((src == me - 3) | (src == me + 3))
-        def _():
-            fetch(xall.at[src], cotfar)
 
         @pl.when(p > 0)
         def _():
@@ -476,6 +440,64 @@
             here = spread == jnp.where(own < 0.0, -1.0, own + e * cap)
             put = here if put is None else put | here
         put_ref[...] = jnp.where(put, 1.0, 0.0).astype(BF)
+        @pl.when(p == 0)
+        def _():
+            fetch(x_hbm, cot_hbm)
+            for load in loads:
+                load.wait()
+
+        @pl.when(p == 1)
+        def _():
+            for d in range(2):
+                arrive(d, 0)
+                forward(d, 1)
+
+            @pl.when(middle_device)
+            def _():
+                far_copy().start()
+
+        @pl.when(p > 0)
+        def _():
+            pltpu.make_async_copy(py_ref, y_own, py_sem.at[0]).wait()
+
+        @pl.when(middle_device & (p == 3))
+        def _():
+            y_copy(1).start()
+
+        @pl.when(edge & (p == 2))
+        def _():
+            for part in range(pieces):
+                edge_copy(0, part).wait_send()
+            y_copy(0).start()
+
+        @pl.when(((p == 2) & edge) | ((p == 3) & jnp.logical_not(edge)))
+        def _():
+            for d in range(2):
+                arrive(d, 1)
+                forward(d, 2)
+
+        @pl.when((p == 3) & edge)
+        def _():
+            for d in range(2):
+                arrive(d, 2)
+            far_copy().wait_recv()
+
+        @pl.when((p > 0) & (src == me - 1))
+        def _():
+            fetch(xall.at[src], cotl_hbm)
+
+        @pl.when((p > 0) & (src == me + 1))
+        def _():
+            fetch(xall.at[src], cotr_hbm)
+
+        @pl.when((src == me - 2) | (src == me + 2))
+        def _():
+            fetch(xall.at[src], cot2_hbm)
+
+        @pl.when((src == me - 3) | (src == me + 3))
+        def _():
+            fetch(xall.at[src], cotfar)
+
         mine = pl.ds(pl.multiple_of(p * cap, cap), cap)
         buf = lax.rem(p + 2, 3)
 
@@ -506,9 +528,6 @@
 
         lax.fori_loop(0, hidden // tile, middle, 0)
 
-        @pl.when(p > 0)
-        def _():
-            pltpu.make_async_copy(py_ref, py_out.at[0], py_sem.at[0]).wait()
 
         @pl.when(p == 3)
         def _():
@@ -523,6 +542,10 @@
                 dxs = dxs + mm_nt(du_ref[e, mine, :], up_ref[e, cols, :])
                 ys_ref[pl.ds(e * cap, cap), :] = dxs.astype(BF)
             pdn_ref[buf, :, cols] = mm(put_ref[...], ys_ref[...]).astype(BF)
+            for kind in range(3):
+                @pl.when(edge & (p == kind + 1))
+                def _():
+                    edge_copy(kind, j).start()
             return 0
 
         lax.fori_loop(0, width // tile, back, 0)
@@ -530,12 +553,6 @@
         @pl.when(p == 0)
         def _():
             pltpu.make_async_copy(pdn_ref.at[2], dn_out.at[0], own_sem.at[0]).start()
-
-        for kind in range(3):
-            @pl.when(edge & (p == kind + 1))
-            def _():
-                for part in range(pieces):
-                    edge_copy(kind, part).start()
 
         def ahead(j, _):
             cols = pl.ds(pl.multiple_of(j * tile, tile), tile)
@@ -548,7 +565,13 @@
             return 0
 
         lax.fori_loop(0, width // tile, ahead, 0)
-        pltpu.make_async_copy(py_ref, py_out.at[src], py_sem.at[0]).start()
+        for dst, when in ((y_own, p == 0), (y_near.at[0], p == 1),
+                          (y_near.at[1], middle_device & (p == 2)),
+                          (y_second, (edge & (p == 2)) | (middle_device & (p == 3))),
+                          (y_third, edge & (p == 3))):
+            @pl.when(when)
+            def _():
+                pltpu.make_async_copy(py_ref, dst, py_sem.at[0]).start()
         dws[p] = jnp.zeros((8, tokens), F32)
         for e in range(local):
             dot = jnp.sum(acc_ref[pl.ds(e * cap, cap), :], axis=1, keepdims=True)
@@ -593,32 +616,40 @@
 
     @pl.when(middle_device)
     def _():
+        far_copy().wait_send()
+        for d in range(2):
+            @pl.when(sends(d, n - 2))
+            def _():
+                xcopy(d, n - 2).wait_send()
+        y_copy(0).start()
         for kind, own in ((0, 1), (1, 2), (2, 0)):
             for part in range(pieces):
                 landed = (edge_copy(kind + 1, part) if kind < 2 else pass_copy(1, part))
                 landed.wait_recv()
-                rows = piece(part)
-                transit[kind, rows, :] = (transit[kind, rows, :].astype(F32)
-                                          + pdn_ref[own, rows, :].astype(F32)).astype(BF)
+                cols = piece(part)
+                transit[kind, :, cols] = (transit[kind, :, cols].astype(F32)
+                                          + pdn_ref[own, :, cols].astype(F32)).astype(BF)
                 pass_copy(kind, part).start()
+        for kind in range(2):
+            y_copy(kind).wait()
         for part in range(pieces):
             edge_copy(0, part).wait_recv()
             pass_copy(0, part).wait_recv()
             for kind in range(3):
                 pass_copy(kind, part).wait_send()
-        far_copy().wait_send()
 
     @pl.when(edge)
     def _():
         for part in range(pieces):
             pass_copy(0, part).wait_recv()
-            for kind in range(3):
+            for kind in (1, 2):
                 edge_copy(kind, part).wait_send()
-
-    pltpu.make_async_copy(py_ref, py_out.at[0], py_sem.at[0]).wait()
+        y_copy(0).wait()
+
+    pltpu.make_async_copy(py_ref, y_own, py_sem.at[0]).wait()
     pltpu.make_async_copy(dws.at[0], dw_out.at[me], own_sem.at[1]).wait()
     for d in range(2):
-        for s in range(n - 1):
+        for s in range(n - 2):
             @pl.when(sends(d, s))
             def _():
                 xcopy(d, s).wait_send()
@@ -642,12 +673,14 @@
     return pl.pallas_call(
         functools.partial(moe_kernel, cap, tile, n),
         out_shape=(
-            shape((3, tokens, width), BF), shape((n, 8, tokens), F32), shape((n, tokens, width), BF),
+            shape((3, tokens, width), BF), shape((n, 8, tokens), F32), shape((tokens, width), BF),
+            shape((2, tokens, width), BF), shape((tokens, width), BF), shape((tokens, width), BF),
+            shape((2, tokens, width), BF),
             shape((local, width, 3 * hidden), BF),
             shape((n, tokens, width), BF), shape((tokens, width), BF),
         ),
         in_specs=[anywhere] * 9,
-        out_specs=[anywhere] * 6,
+        out_specs=[anywhere] * 10,
         scratch_shapes=[
             pltpu.VMEM((local, width, hidden), BF), pltpu.VMEM((local, width, hidden), BF),
             pltpu.VMEM((local, width, hidden), BF),
@@ -662,7 +695,8 @@
             pltpu.VMEM((local * cap, tile), BF), pltpu.VMEM((local * cap, tile), F32),
             pltpu.VMEM((2, tile, 3 * hidden), BF),
             dma((3,)), dma((3,)), dma((2, n - 1)), dma((2, n - 1)), dma((2,)), dma((n,)), dma((n,)),
-            dma((3, 4)), dma((5, 4)), dma((n,)), dma((n,)), dma((1,)), dma((2,)), dma((2,)),
+            dma((3, width // tile)), dma((5, width // tile)), dma((n,)), dma((n,)), dma((1,)), dma((2,)), dma((2,)),
+            dma((2,)), dma((2,)),
         ],
         compiler_params=pltpu.CompilerParams(
             vmem_limit_bytes=MOE_VMEM, collective_id=1, has_side_effects=True
@@ -680,6 +714,8 @@
 LEFT = [(1, 0), (2, 1), (3, 2)]
 RIGHT_ON = [(1, 2), (2, 3)]
 LEFT_ON = [(1, 0), (2, 1)]
+ACROSS = [(0, 2), (1, 3), (2, 0), (3, 1)]
+FAR = [(0, 3), (3, 0)]
 
 
 def project_kernel(x_ref, wq_own, wk_own, wv_own, small_own, cos_ref, sin_ref,
@@ -810,6 +846,14 @@
                            preferred_element_type=F32)
 
 
+def three_parts(a, b):
+    high = a.astype(BF)
+    rest = a - high.astype(F32)
+    middle = rest.astype(BF)
+    low = (rest - middle.astype(F32)).astype(BF)
+    return mm_nt(high, b) + mm_nt(middle, b) + mm_nt(low, b)
+
+
 def mix_kernel(strip, ob_ref, x_ref, wo_ref, small_ref, routed_ref,
                hidden_ref, xq_ref, gates_ref):
     j = pl.program_id(0)
@@ -824,7 +868,7 @@
             h = hidden_ref[rows, :]
             normed = h * inverse_root(h) * small_ref[1:2, :]
             xq_ref[rows, :] = normed.astype(BF)
-            logits = exact(normed, small_ref[8:16, :], ((1,), (1,)))
+            logits = three_parts(normed, small_ref[8:16, :].astype(BF))
             routed = routed_ref[rows, :] > 0.0
             top = jnp.max(jnp.where(routed, logits, NEG), axis=1, keepdims=True)
             power = jnp.where(routed, jnp.exp(jnp.where(routed, logits, top) - top), 0.0)
@@ -872,7 +916,9 @@
             rows = pl.ds(pl.multiple_of(k * strip, strip), strip)
             gates, dot = gates_ref[rows, :], dot_ref[rows, :]
             dlogits = gates * (dot - jnp.sum(gates * dot, axis=1, keepdims=True))
-            dn = exact(dlogits, small_ref[8:16, :], ((1,), (0,)))
+            dn = jnp.zeros((strip, dh_ref.shape[1]), F32)
+            for e in range(dlogits.shape[1]):
+                dn = dn + dlogits[:, e : e + 1] * small_ref[8 + e : 9 + e, :]
             for part in range(dn_ref.shape[0]):
                 dn = dn + jnp.where(flags[part] > 0, dn_ref[part, rows, :].astype(F32), 0.0)
             h = hidden_ref[rows, :]
@@ -1060,10 +1106,11 @@
 
     gain_rows = None
     misc_rows = misc_ref[...]
-    for t in range(chunks + LINKS):
+    begin = [0, 0, 0, 1, 1, 1, 3, 3]
+    for t in range(max(begin) + LINKS + 1):
         for c in range(chunks):
-            if 0 <= t - c <= LINKS:
-                do(c, t - c)
+            if 0 <= t - begin[c] <= LINKS:
+                do(c, t - begin[c])
         if t == 1:
             for copy in kv_copies:
                 copy.wait()
@@ -1127,6 +1174,71 @@
         ),
         name="tail",
     )(ob, da, xa, dq, dk_part, dv_part, cos, sin, wq, wk, wv, dh, x, gain, misc)
+
+
+def finish_kernel(flags, qg_ref, kg_ref, vg_ref, og_ref, misc_ref, y0_ref, y1_ref, y2_ref, y3_ref,
+                  hidden_ref, shard_ref,
+                  q_out, k_out, v_out, o_out, router_out, gains_out, layer_out,
+                  gate_out, up_out, down_out):
+    for src, dst in ((qg_ref, q_out), (kg_ref, k_out), (vg_ref, v_out), (og_ref, o_out)):
+        dst[...] = src[...].astype(F32)
+    out = hidden_ref[...]
+    for ref in (y0_ref, y2_ref, y3_ref):
+        out = out + ref[...].astype(F32)
+    out = out + y1_ref[0].astype(F32)
+    out = out + jnp.where(flags[1] > 0, y1_ref[1].astype(F32), 0.0)
+    layer_out[...] = out.astype(BF)
+    hidden = gate_out.shape[2]
+    for k, dst in enumerate((gate_out, up_out, down_out)):
+        dst[...] = shard_ref[:, :, k * hidden : (k + 1) * hidden].astype(F32)
+
+    @pl.when(pl.program_id(0) == 0)
+    def _():
+        misc = misc_ref[...].astype(F32)
+        router_out[...] = misc[:, 0 : router_out.shape[1]]
+        rows = misc.T
+        gains_out[0:1, :] = rows[16:17, :]
+        gains_out[1:2, :] = jnp.sum(rows[8:16, :], axis=0, keepdims=True)
+
+
+def finish(flags, qg, kg, vg, og, misc, y_own, y_in, y_far, hidden, shard, experts):
+    half, width = qg.shape
+    kv_width = kg.shape[1]
+    tokens = hidden.shape[0]
+    local, rows, three = shard.shape
+    ff = three // 3
+    grid = 4
+    shape = jax.ShapeDtypeStruct
+    cut = lambda r, d: pl.BlockSpec((r // grid, d), lambda i, f: (i, 0))
+    const = lambda r, d: pl.BlockSpec((r, d), lambda i, f: (0, 0))
+    grads = lambda d: pl.BlockSpec((local, rows // grid, d), lambda i, f: (0, i, 0))
+    return pl.pallas_call(
+        finish_kernel,
+        out_shape=(
+            shape((half, width), F32), shape((half, kv_width), F32), shape((half, kv_width), F32),
+            shape((half, width), F32), shape((half, experts), F32), shape((2, half), F32),
+            shape((tokens, width), BF), shape((local, rows, ff), F32),
+            shape((local, rows, ff), F32), shape((local, rows, ff), F32),
+        ),
+        grid_spec=pltpu.PrefetchScalarGridSpec(
+            num_scalar_prefetch=1,
+            grid=(grid,),
+            in_specs=[
+                cut(half, width), cut(half, kv_width), cut(half, kv_width), cut(half, width),
+                const(half, 128), cut(tokens, width),
+                pl.BlockSpec((2, tokens // grid, width), lambda i, f: (0, i, 0)),
+                cut(tokens, width), cut(tokens, width), cut(tokens, width), grads(three),
+            ],
+            out_specs=[
+                cut(half, width), cut(half, kv_width), cut(half, kv_width), cut(half, width),
+                const(half, experts), const(2, half), cut(tokens, width), grads(ff), grads(ff),
+                grads(ff),
+            ],
+        ),
+        compiler_params=pltpu.CompilerParams(vmem_limit_bytes=VMEM_LIMIT),
+        cost_estimate=pl.CostEstimate(flops=0, transcendentals=0, bytes_accessed=16 * half * width),
+        name="finish",
+    )(flags, qg, kg, vg, og, misc, y_own, y_in, *y_far, hidden, shard)
 
 
 def body(
@@ -1207,17 +1319,15 @@
     routing = routing.reshape(2, expert_size, local, rows).transpose(1, 0, 2, 3)
     routing = routing.reshape(expert_size, 2 * local, rows)
     routing = jnp.pad(routing, ((0, 0), (0, 8 - 2 * local), (0, 0)))
-    dn_parts, dw_parts, part_y, grads_low, _, _ = moe(
+    dn_parts, dw_parts, y_own, _, y_second, y_third, y_in, grads_low, _, _ = moe(
         expert_input, upstream, cot_left, cot_right, cot_second, routing, gate_weight, up_weight,
         down_weight, cap,
     )
     gate_dot = dw_parts[:, :local].reshape(expert_count, rows).T * kept_float
-    y_parts = lax.all_to_all(part_y, "expert", split_axis=0, concat_axis=0, tiled=True)
+    y_far = (lax.ppermute(y_third, "expert", FAR), lax.ppermute(y_second, "expert", ACROSS))
     grads_shard = lax.psum_scatter(
         grads_low, ("dp", "context"), scatter_dimension=1, tiled=True
-    ).astype(F32)
-    ff = gate_weight.shape[2]
-    gate_grad, up_grad, down_grad = (grads_shard[:, :, i * ff : (i + 1) * ff] for i in range(3))
+    )
 
     expert_index = lax.axis_index("expert")
     between = (expert_index > 0) & (expert_index < expert_size - 1)
@@ -1233,11 +1343,10 @@
             mixed, attn_grad_low, attn_input, dq_low, dk_part, dv_part, cos_full, sin_full,
             query_full, key_full, value_full, hidden_total, x, small[0:1], misc,
         )
-        query_grad, key_grad, value_grad, output_grad, misc_grad = (v.astype(F32) for v in sums)
-        sums = (
-            query_grad, key_grad, value_grad, output_grad, misc_grad[:, :expert_count],
-            misc_grad[:, 16], jnp.sum(misc_grad[:, 8:16], axis=1),
-        )
+        late, grad_tokens = lax.optimization_barrier((hidden, grad_tokens))
+        (query_grad, key_grad, value_grad, output_grad, router_grad, gains, layer_out,
+         *expert_sums) = finish(flags, *sums, y_own, y_in, y_far, late, grads_shard, expert_count)
+        sums = (query_grad, key_grad, value_grad, output_grad, router_grad, gains[0], gains[1])
     else:
         dkv = lax.psum_scatter(
             jnp.concatenate([dk_part, dv_part], axis=1), "context", scatter_dimension=0, tiled=True
@@ -1259,9 +1368,13 @@
             mm_tn(mixed, attn_grad_low), misc[:8].T,
             jnp.sum(input_total * residual * root, axis=0), jnp.sum(misc[8:16], axis=0),
         ))
-    late, grad_tokens = lax.optimization_barrier((hidden, grad_tokens))
-    layer_out = (late + jnp.sum(y_parts.astype(F32), axis=0)).astype(BF)
-    return (layer_out[None], grad_tokens[None], *sums, gate_grad, up_grad, down_grad)
+        mixture = sum(v.astype(F32) for v in (y_own, y_in[0], *y_far))
+        mixture = mixture + jnp.where(between, y_in[1].astype(F32), 0.0)
+        layer_out = (hidden + mixture).astype(BF)
+        ff = gate_weight.shape[2]
+        wide = grads_shard.astype(F32)
+        expert_sums = [wide[:, :, i * ff : (i + 1) * ff] for i in range(3)]
+    return (layer_out[None], grad_tokens[None], *sums, *expert_sums)
 
 
 def solution(mesh):

time: 578 us -> 535 us (0.926)
  Pallas kernels: 480 us -> 458 us
  other arithmetic: 29.3 us -> 12.4 us
    pallas_call x1, Pallas kernels: 183 us -> 157 us  [tail(): pl.pallas_call(tail_kernel, out_shape=(shape((half, width), BF), shape((h...]
    pallas_call x0 -> x1, Pallas kernels: none -> 12.8 us  [finish(): pl.pallas_call(finish_kernel, out_shape=(shape((half, width), F32), shape...]
    convert_element_type x5 -> x0, other arithmetic: 10.2 us -> none  [body(): v.astype(F32)]
    pallas_call x1, Pallas kernels: 220 us -> 211 us  [moe(): pl.pallas_call(functools.partial(moe_kernel, cap, tile, n), out_shape=(sh...]
  transfers between devices with their start and end apart: 7 -> 8, of which waited for: 3 -> 3; matrix products, arithmetic and copies ran while one was open for 6% -> 3% of each run, Pallas kernels for 45% -> 44%
where the time goes in v5:
time: 535 us; the launch traced here: 534 us
  Pallas kernels  458 us (86%)
  between operations  19.7 us (4%)
  waiting for transfers between devices  18.3 us (3%)
  starting transfers between devices  13.2 us (2%)
  local copies, waits for them, and re-layouts  12.5 us (2%)
  other arithmetic  12.4 us (2%)
    pallas_call x1, Pallas kernels, moe(): pl.pallas_call(functools.partial(moe_kernel, cap, tile, n), out_shape=(sh...  211 us
    pallas_call x1, Pallas kernels, tail(): pl.pallas_call(tail_kernel, out_shape=(shape((half, width), BF), shape((h...  157 us
    pallas_call x1, Pallas kernels, turn(): pl.pallas_call(functools.partial(turn_kernel, row_strip(tokens)), out_sha...  20.4 us
    pallas_call x1, Pallas kernels, attention_backward(): pl.pallas_call(functools.partial(attn_bwd_kernel, kb, tq), out_shape=(jax...  17.6 us
    pallas_call x1, Pallas kernels, project(): pl.pallas_call(project_kernel, out_shape=(shape((tokens, width), BF), sha...  14.4 us
    pallas_call x1, Pallas kernels, finish(): pl.pallas_call(finish_kernel, out_shape=(shape((half, width), F32), shape...  12.8 us
    pallas_call x1, Pallas kernels, attention_forward(): pl.pallas_call(functools.partial(attn_fwd_kernel, kb, tq), out_shape=(jax...  12.3 us
    pallas_call x1, Pallas kernels, mix(): pl.pallas_call(functools.partial(mix_kernel, row_strip(tokens)), out_shap...  12.2 us
  transfers between devices with their start and end apart: 8, of which 3 were waited for; matrix products, arithmetic and copies ran while one was open for 3% of the time, Pallas kernels for 44%

profile of v5, /device:TPU:0, one launch (start us, length us, event | category | flops | bytes accessed | tf_op | source)
XLA Modules:
  0.0 534.1 jit_solution(16137383743222649651)
XLA Ops:
  7.2 0.0 copy-start.1
  7.2 0.0 all-gather.2.cloned.1.call-start
  7.3 0.7 all-gather.2.cloned.1.call-update
  8.0 0.0 reduce-scatter.2.cloned.1.call-start
  8.0 0.6 copy-done.1
  8.6 6.1 %collective-permute-start = (bf16[512,1536]{1,0:T(8,128)(2,1)S(1)}, bf16[512,1536]{1,0:T(8,128)(2,1)}, u32[]{:S(2)}, u32[]{:S(2)}) collective-permute-start(bf16[512,1536]{1,0:T(8,128)(2,1)S(1)} %bitcast.34), channel_id=1, source_target_pairs={{0,1},{1,2},{2,3},{4,5},{5,6},{6,7},{8,9},{9,10},{10,11},{12,13},{... | collective-permute-start | bytes 4718600 | tf_op jit(solution)/shard_map/ppermute | solution.py:1258
  14.6 1.3 collective-permute-start.1
  15.9 0.0 copy-done.3
  15.9 0.6 constant_dynamic-slice_fusion.2
  16.5 1.9 fusion.4
  23.8 0.0 copy-done.6
  23.8 0.2 copy.45
  24.0 0.5 broadcast.37
  24.5 0.7 reduce.9
  25.2 0.3 broadcast_in_dim.46
  25.5 0.1 copy.46
  25.6 0.1 copy.47
  25.7 0.0 copy-start.4
  25.8 0.1 copy.48
  25.9 1.0 convert_reduce_fusion
  26.9 0.1 copy.50
  27.0 0.1 pad.13.clone
  27.1 0.6 stack.32.meta
  27.8 0.6 constant_dynamic-slice_fusion.segq_ref
  28.3 1.0 fusion.1
  29.3 1.0 pad_maximum_fusion
  30.3 0.7 maximum_convert_fusion.small_own
  31.0 0.1 select_convert_fusion
  31.1 0.8 fusion.5
  31.9 14.4 %project.1 = (bf16[512,1536]{1,0:T(8,128)(2,1)}, bf16[512,1536]{1,0:T(8,128)(2,1)}, bf16[1024,512]{1,0:T(8,128)(2,1)}, bf16[1536,1536]{1,0:T(8,128)(2,1)}, bf16[...) custom-call(bf16[512,1536]{1,0:T(8,128)(2,1)} %bitcast.40, bf16[768,1536]{1,0:T(8,128)(2,1)} %wq_own.1, ...), custom_call_target="tpu_custom_call" | custom-call | flops 3221225472 | bytes 18874368 | tf_op jit(solution)/shard_map/project/pallas_call | solution.py:819
  46.3 0.9 collective-permute-done.cotl_hbm
  47.2 5.3 collective-permute-done.1.cotr_hbm
  52.5 0.8 collective-permute-start.2
  53.2 1.5 collective-permute-start.3
  54.7 1.0 copy.54.segk_ref
  55.8 0.1 copy.55
  55.9 12.3 %attn_fwd.1 = (bf16[512,1536]{1,0:T(8,128)(2,1)}, f32[12,1,512]{2,1,0:T(1,128)}) custom-call(s32[5]{0:T(128)} %stack.32.meta, bf16[512,1536]{1,0:T(8,128)(2,1)} %get-tuple-element.72.q_ref, bf16[1024,512]{1,0:T(8,128)(2,1)} %get-tuple-element.73.k_ref.v_ref, bf16[1024,512]{1,0:T(8,128)(2,1)} %get-tuple-element.73.k_ref.v_ref, s32[1024,1]{1,0:T(8,128)} %copy.54.segk_ref, ...), custom_call_target="tpu_custom_call" | custom-call | flops 2415919104 | bytes 3145728 | tf_op jit(solution)/shard_map/attn_fwd/pallas_call | solution.py:217
  68.1 12.2 %mix.1 = (f32[512,1536]{1,0:T(8,128)}, bf16[512,1536]{1,0:T(8,128)(2,1)}, f32[512,8]{1,0:T(8,128)}) custom-call(bf16[512,1536]{1,0:T(8,128)(2,1)} %get-tuple-element.76.ob_ref, bf16[512,1536]{1,0:T(8,128)(2,1)} %bitcast.41, bf16[1536,1536]{1,0:T(8,128)(2,1)} %all-gather.2.cloned.1.call-done.wo_ref, f32[16,1536]{1,0:T(8,128)} %get-tuple-element.77.small_ref, ...), custom_call_target="tpu_custom_call" | custom-call | flops 2415919104 | bytes 9437184 | tf_op jit(solution)/shard_map/mix/pallas_call | solution.py:892
  80.3 0.0 collective-permute-done.2
  80.3 11.4 %collective-permute-done.3 = bf16[512,1536]{1,0:T(8,128)(2,1)} collective-permute-done((bf16[512,1536]{1,0:T(8,128)(2,1)}, bf16[512,1536]{1,0:T(8,128)(2,1)}, u32[]{:S(2)}, u32[]{:S(2)}) %collective-permute-start.3) | collective-permute-done | bytes 1572896 | tf_op jit(solution)/shard_map/ppermute | solution.py:1312
  91.7 1.0 multiply_bitcast_fusion
  92.7 0.1 copy.56
  92.8 0.6 pad.4.meta_hbm
  93.5 2.9 add.52.cot2_hbm
  96.4 211.3 %moe.1 = (bf16[3,512,1536]{2,1,0:T(8,128)(2,1)}, f32[4,8,512]{2,1,0:T(8,128)}, bf16[512,1536]{1,0:T(8,128)(2,1)}, bf16[2,512,1536]{2,1,0:T(8,128)(2,1)}, bf16[51...) custom-call(bf16[512,1536]{1,0:T(8,128)(2,1)} %get-tuple-element.79., ...), custom_call_target="tpu_custom_call" | custom-call | flops 74490839040 | bytes 78643200 | tf_op jit(solution)/shard_map/moe/pallas_call | solution.py:673
  307.7 0.0 copy-start.8
  307.8 0.0 reduce-scatter.2.cloned.1.call-update
  307.8 1.4 slice.13.gain_ref
  309.2 0.5 broadcast_select_fusion.flags
  309.7 0.8 slice.12
  310.6 0.1 copy.58
  310.7 3.5 collective-permute-start.4
  314.2 0.1 collective-permute-start.5
  314.3 0.7 bitcast_multiply_fusion.dot_ref
  315.0 20.4 %turn.1 = (f32[512,1536]{1,0:T(8,128)}, bf16[512,1536]{1,0:T(8,128)(2,1)}, bf16[512,1536]{1,0:T(8,128)(2,1)}, f32[16,1536]{1,0:T(8,128)}) custom-call(s32[3]{0:T(128)} %broadcast_select_fusion.flags, bf16[3,512,1536]{2,1,0:T(8,128)(2,1)} %get-tuple-element.88.dn_ref, f32[512,8]{1,0:T(8,128)} %bitcast_multiply_fusion.dot_ref, ...), custom_call_target="tpu_custom_call" | custom-call | flops 2415919104 | bytes 18874368 | tf_op jit(solution)/shard_map/turn/pallas_call | solution.py:950
  335.4 17.6 %attn_bwd.1 = (bf16[512,1536]{1,0:T(8,128)(2,1)}, bf16[1024,256]{1,0:T(8,128)(2,1)}, bf16[1024,256]{1,0:T(8,128)(2,1)}) custom-call(s32[5]{0:T(128)} %stack.32.meta, bf16[512,1536]{1,0:T(8,128)(2,1)} %get-tuple-element.72.q_ref, bf16[1024,512]{1,0:T(8,128)(2,1)} %get-tuple-element.73.k_ref.v_ref, bf16[1024,512]{1,0:T(8,128)(2,1)} %get-tuple-element.73.k_ref.v_ref, ...), custom_call_target="tpu_custom_call" | custom-call | flops 6442450944 | bytes 6291456 | tf_op jit(solution)/shard_map/attn_bwd/pallas_call | solution.py:259
  353.0 157.1 %tail.1 = (bf16[768,1536]{1,0:T(8,128)(2,1)}, bf16[768,256]{1,0:T(8,128)(2,1)}, bf16[768,256]{1,0:T(8,128)(2,1)}, bf16[768,1536]{1,0:T(8,128)(2,1)}, bf16[768,12...) custom-call(bf16[512,1536]{1,0:T(8,128)(2,1)} %get-tuple-element.76.ob_ref, bf16[512,1536]{1,0:T(8,128)(2,1)} %get-tuple-element.91.da_ref, ...), custom_call_target="tpu_custom_call" | custom-call | flops 8858370048 | bytes 37748736 | tf_op jit(solution)/shard_map/tail/pallas_call | solution.py:1152
  510.1 0.0 collective-permute-done.4.y2_ref
  510.1 0.0 collective-permute-done.5.y3_ref
  510.1 0.0 reduce-scatter.2.cloned.1.call-done.shard_ref
  510.2 12.8 %finish.1 = (f32[768,1536]{1,0:T(8,128)}, f32[768,256]{1,0:T(8,128)}, f32[768,256]{1,0:T(8,128)}, f32[768,1536]{1,0:T(8,128)}, f32[768,8]{1,0:T(8,128)}, /*index...) custom-call(s32[3]{0:T(128)} %broadcast_select_fusion.flags, ...), custom_call_target="tpu_custom_call" | custom-call | bytes 18874368 | tf_op jit(solution)/shard_map/finish/pallas_call | solution.py:1215
  523.0 1.7 copy.60
  524.7 1.4 slice_reduce_fusion
  526.1 1.1 copy.62
  (27 shorter events, 0.2 us)
Async XLA Ops:
  7.2 1.4 copy-start.1
  7.2 8.8 %copy-start.3 = (s32[1,1024]{1,0:T(1,128)S(1)}, s32[1,1024]{1,0:T(1,128)}, u32[]{:S(2)}) copy-start(s32[1,1024]{1,0:T(1,128)} %param.19) | copy-start | bytes 12292
  7.2 16.6 %copy-start.6 = (bf16[768]{0:T(1024)(128)(2,1)S(1)}, bf16[768]{0:T(1024)(128)(2,1)}, u32[]{:S(2)}) copy-start(bf16[768]{0:T(1024)(128)(2,1)} %param.27) | copy-start | bytes 4612
  7.2 16.6 %copy-start.7 = (bf16[768]{0:T(1024)(128)(2,1)S(1)}, bf16[768]{0:T(1024)(128)(2,1)}, u32[]{:S(2)}) copy-start(bf16[768]{0:T(1024)(128)(2,1)} %param.28) | copy-start | bytes 4612
  7.2 16.6 %copy-start.2 = (s32[1,512,4]{1,2,0:T(4,128)S(1)}, s32[1,512,4]{1,2,0:T(4,128)}, u32[]{:S(2)}) copy-start(s32[1,512,4]{1,2,0:T(4,128)} %param.20) | copy-start | bytes 24580
  7.2 17.3 %copy-start.5 = (s32[1,1,2048]{2,1,0:T(1,128)S(1)}, s32[1,1,2048]{2,1,0:T(1,128)}, u32[]{:S(2)}) copy-start(s32[1,1,2048]{2,1,0:T(1,128)} %param.21) | copy-start | bytes 24580
  7.2 60.9 %all-gather.2.cloned.1.call-start = ((), (), s32[]{:S(2)}) async-start(), calls=%async_computation.1 | async-start | bytes 7077888 | tf_op jit(solution)/shard_map/all_gather | solution.py:1255
  8.0 502.2 %reduce-scatter.2.cloned.1.call-start = ((), (), s32[]{:S(2)}) async-start(), calls=%async_computation.2 | async-start | bytes 15925248 | tf_op jit(solution)/shard_map/reduce_scatter | solution.py:1328
  8.6 38.6 %collective-permute-start = (bf16[512,1536]{1,0:T(8,128)(2,1)S(1)}, bf16[512,1536]{1,0:T(8,128)(2,1)}, u32[]{:S(2)}, u32[]{:S(2)}) collective-permute-start(bf16[512,1536]{1,0:T(8,128)(2,1)S(1)} %bitcast.34), channel_id=1, source_target_pairs={{0,1},{1,2},{2,3},{4,5},{5,6},{6,7},{8,9},{9,10},{10,11},{12,13},{... | collective-permute-start | bytes 4718600 | tf_op jit(solution)/shard_map/ppermute | solution.py:1258
  14.6 37.8 %collective-permute-start.1 = (bf16[512,1536]{1,0:T(8,128)(2,1)S(1)}, bf16[512,1536]{1,0:T(8,128)(2,1)}, u32[]{:S(2)}, u32[]{:S(2)}) collective-permute-start(bf16[512,1536]{1,0:T(8,128)(2,1)S(1)} %bitcast.35), channel_id=1, source_target_pairs={{1,0},{2,1},{3,2},{5,4},{6,5},{7,6},{9,8},{10,9},{11,10},{13,12},{... | collective-permute-start | bytes 4718600 | tf_op jit(solution)/shard_map/ppermute | solution.py:1259
  25.7 4.6 copy-start.4
  52.5 27.8 %collective-permute-start.2 = (bf16[512,1536]{1,0:T(8,128)(2,1)}, bf16[512,1536]{1,0:T(8,128)(2,1)S(1)}, u32[]{:S(2)}, u32[]{:S(2)}) collective-permute-start(bf16[512,1536]{1,0:T(8,128)(2,1)} %collective-permute-done.cotl_hbm), channel_id=1, source_target_pairs={{1,2},{2,3},{5,6},{6,7},{9,10},{10,11},{13,14},{14,15},{17,18},{18... | collective-permute-start | bytes 4718600 | tf_op jit(solution)/shard_map/ppermute | solution.py:1311
  53.2 38.4 %collective-permute-start.3 = (bf16[512,1536]{1,0:T(8,128)(2,1)}, bf16[512,1536]{1,0:T(8,128)(2,1)}, u32[]{:S(2)}, u32[]{:S(2)}) collective-permute-start(bf16[512,1536]{1,0:T(8,128)(2,1)} %collective-permute-done.1.cotr_hbm), channel_id=1, source_target_pairs={{1,0},{2,1},{5,4},{6,5},{9,8},{10,9},{13,12},{14,13},{17,16},{18,1... | collective-permute-start | bytes 4718600 | tf_op jit(solution)/shard_map/ppermute | solution.py:1312
  307.7 1.4 copy-start.8
  310.7 199.4 %collective-permute-start.4 = (bf16[512,1536]{1,0:T(8,128)(2,1)}, bf16[512,1536]{1,0:T(8,128)(2,1)}, u32[]{:S(2)}, u32[]{:S(2)}) collective-permute-start(bf16[512,1536]{1,0:T(8,128)(2,1)} %get-tuple-element.110), channel_id=1, source_target_pairs={{0,3},{3,0},{4,7},{7,4},{8,11},{11,8},{12,15},{15,12},{16,19},{19,... | collective-permute-start | bytes 4718600 | tf_op jit(solution)/shard_map/ppermute | solution.py:1327
  314.2 195.9 %collective-permute-start.5 = (bf16[512,1536]{1,0:T(8,128)(2,1)}, bf16[512,1536]{1,0:T(8,128)(2,1)}, u32[]{:S(2)}, u32[]{:S(2)}) collective-permute-start(bf16[512,1536]{1,0:T(8,128)(2,1)} %get-tuple-element.111), channel_id=1, source_target_pairs={{0,2},{1,3},{2,0},{3,1},{4,6},{5,7},{6,4},{7,5},{8,10},{9,11},{10,... | collective-permute-start | bytes 4718600 | tf_op jit(solution)/shard_map/ppermute | solution.py:1327
  510.1 16.0 %copy-start = (bf16[512,1536]{1,0:T(8,128)(2,1)S(1)}, bf16[512,1536]{1,0:T(8,128)(2,1)}, u32[]{:S(2)}) copy-start(bf16[512,1536]{1,0:T(8,128)(2,1)} %get-tuple-element.116) | copy-start | bytes 4718596
Sparse Core Ops, SparseCore 0:
  9.6 17.1 all-gather.1
  307.9 127.0 reduce-scatter.1

commit v6 on v5

--- a/solution.py
+++ b/solution.py
@@ -309,7 +309,7 @@
 
 
 def moe_kernel(cap, tile, n,
-               x_hbm, cot_hbm, cotl_hbm, cotr_hbm, cot2_hbm, meta_hbm, gate_hbm, up_hbm, down_hbm,
+               x_hbm, cot_hbm, cotl_hbm, cotr_hbm, cotl2_hbm, cotr2_hbm, meta_hbm, gate_hbm, up_hbm, down_hbm,
                dn_out, dw_out, y_own, y_near, y_second, y_third, y_in, grads_out, xall, cotfar,
                gate_ref, up_ref, down_ref, x_ref, cot_ref, metas, xs_ref, dy_ref, hb_ref, dg_ref,
                du_ref, pdn_ref, transit, py_ref, dws, pick_ref, put_ref, ys_ref, acc_ref, stage,
@@ -344,7 +344,8 @@
     outward = jnp.where(me < 2, 0, n - 1)
     inward = n - 1 - jnp.clip(me, 1, n - 2)
     inner = jnp.where(me < 2, 1, n - 2)
-    far_copy = lambda: remote(cot2_hbm, cotfar, far_sem.at[0], far_sem.at[1], "expert", outward)
+    far_copy = lambda ref=cotl2_hbm: remote(ref, cotfar, far_sem.at[0], far_sem.at[1], "expert",
+                                            outward)
     middle_device = jnp.logical_not(edge)
 
     for d in range(2):
@@ -452,9 +453,10 @@
                 arrive(d, 0)
                 forward(d, 1)
 
-            @pl.when(middle_device)
-            def _():
-                far_copy().start()
+            for ref, when in ((cotl2_hbm, me >= 2), (cotr2_hbm, me < 2)):
+                @pl.when(middle_device & when)
+                def _():
+                    far_copy(ref).start()
 
         @pl.when(p > 0)
         def _():
@@ -490,9 +492,13 @@
         def _():
             fetch(xall.at[src], cotr_hbm)
 
-        @pl.when((src == me - 2) | (src == me + 2))
-        def _():
-            fetch(xall.at[src], cot2_hbm)
+        @pl.when(src == me - 2)
+        def _():
+            fetch(xall.at[src], cotl2_hbm)
+
+        @pl.when(src == me + 2)
+        def _():
+            fetch(xall.at[src], cotr2_hbm)
 
         @pl.when((src == me - 3) | (src == me + 3))
         def _():
@@ -662,7 +668,7 @@
             remote(dws.at[0], dw_out.at[j], dw_send.at[j], dw_recv.at[j], "expert", j).wait_recv()
 
 
-def moe(x, cot, cot_left, cot_right, cot_second, meta, gate, up, down, cap):
+def moe(x, cot, cot_left, cot_right, second_left, second_right, meta, gate, up, down, cap):
     n = meta.shape[0]
     tokens, width = x.shape
     local, _, hidden = gate.shape
@@ -679,7 +685,7 @@
             shape((local, width, 3 * hidden), BF),
             shape((n, tokens, width), BF), shape((tokens, width), BF),
         ),
-        in_specs=[anywhere] * 9,
+        in_specs=[anywhere] * 10,
         out_specs=[anywhere] * 10,
         scratch_shapes=[
             pltpu.VMEM((local, width, hidden), BF), pltpu.VMEM((local, width, hidden), BF),
@@ -707,7 +713,7 @@
             bytes_accessed=2 * (8 * n * tokens * width + 6 * local * width * hidden),
         ),
         name="moe",
-    )(x, cot, cot_left, cot_right, cot_second, meta, gate, up, down)
+    )(x, cot, cot_left, cot_right, second_left, second_right, meta, gate, up, down)
 
 
 RIGHT = [(0, 1), (1, 2), (2, 3)]
@@ -904,78 +910,101 @@
     )(ob, x, wo, small, routed)
 
 
-def turn_kernel(strip, flags, dn_ref, dot_ref, gates_ref, hidden_ref, cot_ref, wo_ref, small_ref,
-                dh_ref, da_ref, dob_ref, misc_ref, normed_ref, dlog_ref):
+def turn_kernel(strip, local, flags, dn_ref, dw_ref, kept_ref, gates_ref, hidden_ref, cot_ref,
+                wo_ref, small_ref, dh_ref, da_ref, dob_ref, misc_ref,
+                normed_ref, dlog_ref, da_all, row_ref, dot_ref):
     j = pl.program_id(0)
+    strips = da_all.shape[0] // strip
 
     @pl.when(j == 0)
     def _():
+        for d in range(dw_ref.shape[0]):
+            row_ref[d * local : (d + 1) * local, :] = dw_ref[d, 0:local, :]
+        dot_ref[...] = row_ref[...].T * kept_ref[...]
+        misc_ref[...] = jnp.zeros_like(misc_ref)
+
+    @pl.when(j < strips)
+    def _():
+        rows = pl.ds(pl.multiple_of(j * strip, strip), strip)
         gain = small_ref[1:2, :]
-
-        def one(k, total):
-            rows = pl.ds(pl.multiple_of(k * strip, strip), strip)
-            gates, dot = gates_ref[rows, :], dot_ref[rows, :]
-            dlogits = gates * (dot - jnp.sum(gates * dot, axis=1, keepdims=True))
-            dn = jnp.zeros((strip, dh_ref.shape[1]), F32)
-            for e in range(dlogits.shape[1]):
-                dn = dn + dlogits[:, e : e + 1] * small_ref[8 + e : 9 + e, :]
-            for part in range(dn_ref.shape[0]):
-                dn = dn + jnp.where(flags[part] > 0, dn_ref[part, rows, :].astype(F32), 0.0)
-            h = hidden_ref[rows, :]
-            root = inverse_root(h)
-            scaled = h * root
-            normed_ref[rows, :] = scaled * gain
-            dlog_ref[rows, :] = dlogits
-            dh = cot_ref[rows, :].astype(F32) + norm_back(h, root, gain, dn)
-            dh_ref[rows, :] = dh
-            da_ref[rows, :] = dh.astype(BF)
-            return total + fold_rows(dn * scaled, jnp.sum)
-
-        tokens, width = dh_ref.shape
-        misc_ref[8:16, :] = lax.fori_loop(0, tokens // strip, one, jnp.zeros((8, width), F32))
-
-    tile = wo_ref.shape[0]
-    cols = pl.ds(pl.multiple_of(j * tile, tile), tile)
-    dob_ref[:, cols] = mm_nt(da_ref[...], wo_ref[...]).astype(BF)
-    misc_ref[0:8, cols] = exact(dlog_ref[...], normed_ref[:, cols], ((0,), (0,)))
-
-
-def turn(flags, dn_parts, dot, gates, hidden, cot, wo, small):
+        gates, dot = gates_ref[rows, :], dot_ref[rows, :]
+        dlogits = gates * (dot - jnp.sum(gates * dot, axis=1, keepdims=True))
+        dn = jnp.zeros(dh_ref.shape, F32)
+        for e in range(dlogits.shape[1]):
+            dn = dn + dlogits[:, e : e + 1] * small_ref[8 + e : 9 + e, :]
+        for part in range(dn_ref.shape[0]):
+            dn = dn + jnp.where(flags[part] > 0, dn_ref[part].astype(F32), 0.0)
+        h = hidden_ref[...]
+        root = inverse_root(h)
+        scaled = h * root
+        normed_ref[rows, :] = scaled * gain
+        dlog_ref[rows, :] = dlogits
+        dh = cot_ref[...].astype(F32) + norm_back(h, root, gain, dn)
+        dh_ref[...] = dh
+        da = dh.astype(BF)
+        da_ref[...] = da
+        da_all[rows, :] = da
+        misc_ref[8:16, :] += fold_rows(dn * scaled, jnp.sum)
+
+    @pl.when(j >= strips)
+    def _():
+        tile = wo_ref.shape[0]
+        cols = pl.ds(pl.multiple_of((j - strips) * tile, tile), tile)
+        dob_ref[...] = mm_nt(da_all[...], wo_ref[...]).astype(BF)
+        misc_ref[0:8, cols] = exact(dlog_ref[...], normed_ref[:, cols], ((0,), (0,)))
+
+
+def turn(flags, dn_parts, dw_parts, kept, gates, hidden, cot, wo, small):
     tokens, width = cot.shape
-    tile = 256
+    tile, strip = 256, row_strip(tokens)
+    strips = tokens // strip
+    experts = gates.shape[1]
+    local = experts // dw_parts.shape[0]
     shape = jax.ShapeDtypeStruct
     once = pl.Buffered(1)
     const = lambda v: pl.BlockSpec(v.shape, lambda j, f: (0,) * v.ndim, pipeline_mode=once)
-    whole = lambda r: pl.BlockSpec((r, width), lambda j, f: (0, 0))
+    early = lambda j: jnp.minimum(j, strips - 1)
+    late = lambda j: jnp.maximum(j - strips, 0)
+    rows = pl.BlockSpec((strip, width), lambda j, f: (early(j), 0))
     return pl.pallas_call(
-        functools.partial(turn_kernel, row_strip(tokens)),
+        functools.partial(turn_kernel, strip, local),
         out_shape=(shape((tokens, width), F32), shape((tokens, width), BF),
                    shape((tokens, width), BF), shape((16, width), F32)),
         grid_spec=pltpu.PrefetchScalarGridSpec(
             num_scalar_prefetch=1,
-            grid=(width // tile,),
-            in_specs=[const(dn_parts), const(dot), const(gates), const(hidden), const(cot),
-                      pl.BlockSpec((tile, width), lambda j, f: (j, 0)), const(small)],
-            out_specs=[whole(tokens), whole(tokens), whole(tokens), whole(16)],
-            scratch_shapes=[pltpu.VMEM((tokens, width), F32),
-                            pltpu.VMEM((tokens, gates.shape[1]), F32)],
+            grid=(strips + width // tile,),
+            in_specs=[pl.BlockSpec((dn_parts.shape[0], strip, width), lambda j, f: (0, early(j), 0)),
+                      const(dw_parts), const(kept), const(gates), rows, rows,
+                      pl.BlockSpec((tile, width), lambda j, f: (late(j), 0)), const(small)],
+            out_specs=[rows, rows, pl.BlockSpec((tokens, tile), lambda j, f: (0, late(j))),
+                       pl.BlockSpec((16, width), lambda j, f: (0, 0))],
+            scratch_shapes=[pltpu.VMEM((tokens, width), F32), pltpu.VMEM((tokens, experts), F32),
+                            pltpu.VMEM((tokens, width), BF), pltpu.VMEM((experts, tokens), F32),
+                            pltpu.VMEM((tokens, experts), F32)],
         ),
         compiler_params=pltpu.CompilerParams(vmem_limit_bytes=VMEM_LIMIT),
         cost_estimate=pl.CostEstimate(
             flops=2 * tokens * width * width, transcendentals=0, bytes_accessed=8 * width * width),
         name="turn",
-    )(flags, dn_parts, dot, gates, hidden, cot, wo, small)
+    )(flags, dn_parts, dw_parts, kept, gates, hidden, cot, wo, small)
 
 
 WIDE = 512
 LINKS = 9
 
 
-def tail_kernel(ob_ref, da_ref, xa_ref, dq_ref, dkp_ref, dvp_ref, cos_ref, sin_ref, wq_ref, wk_ref,
-                wv_ref, dh_ref, x_ref, gain_ref, misc_ref,
+def tail_kernel(ob_ref, da_ref, xa_hbm, q_ref, kv_ref, do_ref, lse_ref, segk_ref, segq_ref,
+                cos_ref, sin_ref, wq_hbm, wk_hbm, wv_hbm, dh_hbm, x_hbm, gain_ref, misc_ref,
                 qg_out, kg_out, vg_out, og_out, mg_out, gt_ref,
+                dq_ref, dkp_ref, dvp_ref, bias_ref, p_ref, dp_ref, kt_ref, dk_acc, dv_acc,
                 dkv_in, dkv_ref, part, buf0, buf1, buf2, buf3, buf4, res,
-                kv_sem, send_sem, recv_sem, out_sem):
+                xa_ref, wq_ref, wk_ref, wv_ref, dh_ref, x_ref,
+                kv_sem, send_sem, recv_sem, out_sem, load_sem):
+    loads = [pltpu.make_async_copy(a, b, load_sem.at[k]) for k, (a, b) in enumerate((
+        (xa_hbm, xa_ref), (wq_hbm, wq_ref), (wk_hbm, wk_ref), (wv_hbm, wv_ref), (dh_hbm, dh_ref),
+        (x_hbm, x_ref)))]
+    for load in loads:
+        load.start()
     ctx = lax.axis_index("context")
     dp = lax.axis_index("dp")
     z = lax.axis_index("expert")
@@ -1006,17 +1035,14 @@
         exchange(ref.at[theirs], dkv_in.at[k], kv_sem.at[0, k], kv_sem.at[1, k], "c")
         for k, ref in enumerate((dkp_ref, dvp_ref))
     ]
-    for copy in kv_copies:
-        copy.start()
-
     sizes = [half // 2, half // 4, half // 8, half // 16]
     bufs = [buf1, buf2, buf3, buf4]
     columns = [WIDE] * (chunks - 1) + [128]
 
     def flows(c):
         w = columns[c] // 2 if columns[c] >= 256 else columns[c]
-        ways = [("x", "y", "n", "f"), ("y", "x", "n", "f")]
-        return [(k, k * w, w, ways[(k + c) % 2]) for k in range(columns[c] // w)]
+        ways = [("n", "x", "y", "f"), ("y", "x", "n", "f"), ("n", "y", "x", "f"), ("x", "y", "n", "f")]
+        return [(k, k * w, w, ways[(k + 2 * c) % 4]) for k in range(columns[c] // w)]
 
     def rows_at(ways, depth):
         first = 0
@@ -1038,7 +1064,7 @@
         cols = pl.ds(first, w)
         ss, rs = send_sem.at[c, k, level], recv_sem.at[c, k, level]
         if level == 0:
-            src = part.at[c % 3, pl.ds(pl.multiple_of((1 - ctx) * half, 16), half), cols]
+            src = part.at[c % 4, pl.ds(pl.multiple_of((1 - ctx) * half, 16), half), cols]
             return exchange(src, buf0.at[c, :, cols], ss, rs, "c")
         if level <= 4:
             way, size = ways[level - 1], sizes[level - 1]
@@ -1055,15 +1081,18 @@
             left, right, first = ((ob_ref, da_ref, c * WIDE) if c < 3 else
                                   (xa_ref, dq_ref, (c - 3) * WIDE) if c < 6 else
                                   (xa_ref, dkv_ref, 0))
+            if c == 3:
+                loads[0].wait()
+            tall = width // 2
             def one(j, _):
-                rows = pl.ds(pl.multiple_of(j * 256, 256), 256)
-                part[c % 3, rows, :] = mm_tn(left[:, rows], right[:, first : first + WIDE]).astype(BF)
+                rows = pl.ds(pl.multiple_of(j * tall, tall), tall)
+                part[c % 4, rows, :] = mm_tn(left[:, rows], right[:, first : first + WIDE]).astype(BF)
                 return 0
-            lax.fori_loop(0, width // 256, one, 0)
+            lax.fori_loop(0, width // tall, one, 0)
         else:
-            part[c % 3, :, 0:128] = jnp.zeros((width, 128), BF)
-            part[c % 3, :, 0:16] = misc_rows.T.astype(BF)
-            part[c % 3, :, 16:24] = gain_rows.T.astype(BF)
+            part[c % 4, :, 0:128] = jnp.zeros((width, 128), BF)
+            part[c % 4, :, 0:16] = misc_rows.T.astype(BF)
+            part[c % 4, :, 16:24] = gain_rows.T.astype(BF)
 
     def finish(c):
         for copy in out_copy(c):
@@ -1089,7 +1118,7 @@
             if level > 0:
                 link(c, flow, level - 1).wait()
             if level == 1:
-                plus(buf0.at[c], 0, cols, part.at[c % 3], ctx * half, half)
+                plus(buf0.at[c], 0, cols, part.at[c % 4], ctx * half, half)
             elif 1 < level <= 4:
                 before = buf0 if level == 2 else bufs[level - 3]
                 plus(bufs[level - 2].at[c], 0, cols, before.at[c],
@@ -1104,14 +1133,74 @@
         if level == LINKS:
             finish(c)
 
+    length = kv_ref.shape[0]
+    tq = tokens // 2
+    kb = tq
+    reach = length // 2
+    make_bias(ctx, tokens, segk_ref, segq_ref, bias_ref)
+
+    def attend(index):
+        step, piece = index // 2, index % 2
+        group, place = step * HEADS_AT_ONCE // GROUP, step * HEADS_AT_ONCE % GROUP
+        k_at = slice(group * HEAD_SIZE, (group + 1) * HEAD_SIZE)
+        v_at = slice(kv_width + group * HEAD_SIZE, kv_width + (group + 1) * HEAD_SIZE)
+        if place == 0 and piece == 0:
+            kt_ref[...] = kv_ref[:, k_at].astype(F32).T.astype(BF)
+            dk_acc[...] = jnp.zeros_like(dk_acc)
+            dv_acc[...] = jnp.zeros_like(dv_acc)
+        cols = pl.ds(piece * tq, tq)
+        high = ctx * 2 + piece + 1
+        low = jnp.maximum(high - 1 - reach // kb, 0)
+        heads = [step * HEADS_AT_ONCE + h for h in range(HEADS_AT_ONCE)]
+        at = [slice(h * HEAD_SIZE, (h + 1) * HEAD_SIZE) for h in heads]
+
+        def score(i, deltas):
+            rows = pl.ds(pl.multiple_of(i * kb, kb), kb)
+            key, value, bias = kv_ref[rows, k_at], kv_ref[rows, v_at], bias_ref[rows, cols]
+            out = []
+            for h in range(HEADS_AT_ONCE):
+                s = mm_nt(key, q_ref[cols, at[h]]) * SCALE + bias
+                p = jnp.exp(s - lse_ref[heads[h], :, cols])
+                dp = mm_nt(value, do_ref[cols, at[h]])
+                p_ref[h, rows, :] = p
+                dp_ref[h, rows, :] = dp
+                out.append(deltas[h] + fold_rows(p * dp, jnp.sum))
+            return tuple(out)
+
+        deltas = lax.fori_loop(low, high, score, tuple(jnp.zeros((8, tq), F32) for _ in heads))
+        deltas = [jnp.sum(d, axis=0, keepdims=True) for d in deltas]
+
+        def grads(i, dqs):
+            rows = pl.ds(pl.multiple_of(i * kb, kb), kb)
+            kt = kt_ref[:, rows]
+            out, dk, dv = [], dk_acc[rows, :], dv_acc[rows, :]
+            for h in range(HEADS_AT_ONCE):
+                p = p_ref[h, rows, :]
+                ds = (p * (dp_ref[h, rows, :] - deltas[h])).astype(BF)
+                dv = dv + mm(p.astype(BF), do_ref[cols, at[h]])
+                dk = dk + mm(ds, q_ref[cols, at[h]])
+                out.append(dqs[h] + mm(kt, ds))
+            dk_acc[rows, :] = dk
+            dv_acc[rows, :] = dv
+            return tuple(out)
+
+        dqs = lax.fori_loop(low, high, grads,
+                            tuple(jnp.zeros((HEAD_SIZE, tq), F32) for _ in heads))
+        for h in range(HEADS_AT_ONCE):
+            dq = dqs[h].T * SCALE
+            turned = pltpu.roll(dq, HEAD_SIZE // 2, 1)
+            dq_ref[cols, at[h]] = (dq * cos_ref[cols, :] - turned * sin_ref[cols, :]).astype(BF)
+        if place == GROUP - HEADS_AT_ONCE and piece == 1:
+            dkp_ref[:, k_at] = (dk_acc[...] * SCALE).astype(BF)
+            dvp_ref[:, k_at] = dv_acc[...].astype(BF)
+
     gain_rows = None
     misc_rows = misc_ref[...]
-    begin = [0, 0, 0, 1, 1, 1, 3, 3]
-    for t in range(max(begin) + LINKS + 1):
-        for c in range(chunks):
-            if 0 <= t - begin[c] <= LINKS:
-                do(c, t - begin[c])
-        if t == 1:
+    steps = 2 * QUERY_HEADS // HEADS_AT_ONCE
+    begin = [0, 0, 0, 3, 3, 3, 3, 5]
+    paces = begin[3]
+    for t in range(begin[-1] + LINKS + 1):
+        if t == begin[6]:
             for copy in kv_copies:
                 copy.wait()
             for h in range(kv_width // HEAD_SIZE):
@@ -1121,18 +1210,42 @@
                 dkv_ref[:, at] = (dk * cos_ref[...] - turned * sin_ref[...]).astype(BF)
             dv = dvp_ref[ours, :].astype(F32) + dkv_in[1].astype(F32)
             dkv_ref[:, kv_width : 2 * kv_width] = dv.astype(BF)
-        if t == 2:
-            step = 64
+        for c in range(chunks):
+            if 0 <= t - begin[c] <= LINKS:
+                do(c, t - begin[c])
+        if t < paces:
+            for k in (range(2), range(2, 6), range(6, steps))[t]:
+                attend(k)
+        if t == paces - 1:
+            for copy in kv_copies:
+                copy.start()
+        if t == begin[7] - 1:
+            for load in loads[1:]:
+                load.wait()
+
+            def column(j, _):
+                cols = pl.ds(pl.multiple_of(j * tq, tq), tq)
+                tile = mm_nt(dq_ref[...], wq_ref[cols, :])
+                tile = tile + mm_nt(dkv_ref[:, 0:kv_width], wk_ref[cols, :])
+                tile = tile + mm_nt(dkv_ref[:, kv_width : 2 * kv_width], wv_ref[cols, :])
+                at = pl.ds(pl.multiple_of(lax.rem(j, 2) * tokens, 16), tokens)
+                p_ref[lax.div(j, 2), at, :] = tile
+                return 0
+
+            lax.fori_loop(0, width // tq, column, 0)
+            step = 128
+
             def strip(k, total):
                 rows = pl.ds(pl.multiple_of(k * step, step), step)
-                dxa = mm_nt(dq_ref[rows, :], wq_ref[...])
-                dxa = dxa + mm_nt(dkv_ref[rows, 0:kv_width], wk_ref[...])
-                dxa = dxa + mm_nt(dkv_ref[rows, kv_width : 2 * kv_width], wv_ref[...])
+                dxa = jnp.concatenate([
+                    p_ref[j // 2, pl.ds(pl.multiple_of(j % 2 * tokens + k * step, step), step), :]
+                    for j in range(width // tq)], axis=1)
                 v = x_ref[rows, :].astype(F32)
                 root = inverse_root(v)
-                back = dh_ref[rows, :] + norm_back(v, root, gain_ref[...], dxa)
+                back = dh_ref[rows, :] + norm_back(v, root, gain_ref[0:1, :], dxa)
                 gt_ref[rows, :] = back.astype(BF)
                 return total + fold_rows(dxa * v * root, jnp.sum)
+
             total = lax.fori_loop(0, tokens // step, strip, jnp.zeros((8, width), F32))
             gain_rows = jnp.broadcast_to(jnp.sum(total, axis=0, keepdims=True), (8, width))
     for c in range(chunks):
@@ -1140,9 +1253,10 @@
             copy.wait()
 
 
-def tail(ob, da, xa, dq, dk_part, dv_part, cos, sin, wq, wk, wv, dh, x, gain, misc):
+def tail(ob, da, xa, q, kv, do, lse, segk, segq, cos, sin, wq, wk, wv, dh, x, gain, misc):
     tokens, width = xa.shape
-    kv_width = dk_part.shape[1]
+    length, kv_width = kv.shape[0], kv.shape[1] // 2
+    tq = tokens // 2
     half = width // 2
     vmem = pl.BlockSpec(memory_space=pltpu.VMEM)
     anywhere = pl.BlockSpec(memory_space=pl.ANY)
@@ -1155,15 +1269,24 @@
             shape((half, width), BF), shape((half, kv_width), BF), shape((half, kv_width), BF),
             shape((half, width), BF), shape((half, 128), BF), shape((tokens, width), BF),
         ),
-        in_specs=[vmem] * 15,
+        in_specs=[vmem, vmem, anywhere] + [vmem] * 8 + [anywhere] * 5 + [vmem] * 2,
         out_specs=[anywhere] * 5 + [vmem],
         scratch_shapes=[
+            pltpu.VMEM((tokens, width), BF), pltpu.VMEM((length, kv_width), BF),
+            pltpu.VMEM((length, kv_width), BF), pltpu.VMEM((length, tokens), F32),
+            pltpu.VMEM((HEADS_AT_ONCE, length, tq), F32),
+            pltpu.VMEM((HEADS_AT_ONCE, length, tq), F32),
+            pltpu.VMEM((HEAD_SIZE, length), BF), pltpu.VMEM((length, HEAD_SIZE), F32),
+            pltpu.VMEM((length, HEAD_SIZE), F32),
             pltpu.VMEM((2, tokens, kv_width), BF), pltpu.VMEM((tokens, 2 * kv_width), BF),
-            pltpu.VMEM((3, width, WIDE), BF),
+            pltpu.VMEM((4, width, WIDE), BF),
             pltpu.VMEM((chunks, half, WIDE), BF), pltpu.VMEM((chunks, half // 2, WIDE), BF),
             pltpu.VMEM((chunks, half // 4, WIDE), BF), pltpu.VMEM((chunks, half // 8, WIDE), BF),
             pltpu.VMEM((chunks, half // 16, WIDE), BF), pltpu.VMEM((chunks, half, WIDE), BF),
-            dma((2, 2)), dma((chunks, 2, LINKS)), dma((chunks, 2, LINKS)), dma((chunks, 2)),
+            pltpu.VMEM((tokens, width), BF), pltpu.VMEM((width, width), BF),
+            pltpu.VMEM((width, kv_width), BF), pltpu.VMEM((width, kv_width), BF),
+            pltpu.VMEM((tokens, width), F32), pltpu.VMEM((tokens, width), BF),
+            dma((2, 2)), dma((chunks, 2, LINKS)), dma((chunks, 2, LINKS)), dma((chunks, 2)), dma((6,)),
         ],
         compiler_params=pltpu.CompilerParams(
             vmem_limit_bytes=MOE_VMEM, collective_id=2, has_side_effects=True
@@ -1173,12 +1296,12 @@
             transcendentals=0, bytes_accessed=16 * width * width,
         ),
         name="tail",
-    )(ob, da, xa, dq, dk_part, dv_part, cos, sin, wq, wk, wv, dh, x, gain, misc)
+    )(ob, da, xa, q, kv, do, lse, segk, segq, cos, sin, wq, wk, wv, dh, x, gain, misc)
 
 
 def finish_kernel(flags, qg_ref, kg_ref, vg_ref, og_ref, misc_ref, y0_ref, y1_ref, y2_ref, y3_ref,
                   hidden_ref, shard_ref,
-                  q_out, k_out, v_out, o_out, router_out, gains_out, layer_out,
+                  q_out, k_out, v_out, o_out, router_out, first_out, second_out, layer_out,
                   gate_out, up_out, down_out):
     for src, dst in ((qg_ref, q_out), (kg_ref, k_out), (vg_ref, v_out), (og_ref, o_out)):
         dst[...] = src[...].astype(F32)
@@ -1195,10 +1318,10 @@
     @pl.when(pl.program_id(0) == 0)
     def _():
         misc = misc_ref[...].astype(F32)
-        router_out[...] = misc[:, 0 : router_out.shape[1]]
         rows = misc.T
-        gains_out[0:1, :] = rows[16:17, :]
-        gains_out[1:2, :] = jnp.sum(rows[8:16, :], axis=0, keepdims=True)
+        router_out[...] = rows[0 : router_out.shape[0], :]
+        first_out[...] = rows[16:17, :]
+        second_out[...] = jnp.sum(rows[8:16, :], axis=0, keepdims=True)
 
 
 def finish(flags, qg, kg, vg, og, misc, y_own, y_in, y_far, hidden, shard, experts):
@@ -1216,7 +1339,8 @@
         finish_kernel,
         out_shape=(
             shape((half, width), F32), shape((half, kv_width), F32), shape((half, kv_width), F32),
-            shape((half, width), F32), shape((half, experts), F32), shape((2, half), F32),
+            shape((half, width), F32), shape((experts, half), F32), shape((1, half), F32),
+            shape((1, half), F32),
             shape((tokens, width), BF), shape((local, rows, ff), F32),
             shape((local, rows, ff), F32), shape((local, rows, ff), F32),
         ),
@@ -1231,7 +1355,7 @@
             ],
             out_specs=[
                 cut(half, width), cut(half, kv_width), cut(half, kv_width), cut(half, width),
-                const(half, experts), const(2, half), cut(tokens, width), grads(ff), grads(ff),
+                const(experts, half), const(1, half), const(1, half), cut(tokens, width), grads(ff), grads(ff),
                 grads(ff),
             ],
         ),
@@ -1313,41 +1437,40 @@
     mixed, lse = attention_forward(q, kv, spans, segk, segq)
 
     hidden, expert_input, gates = mix(mixed, x, output_full, small, routed_float)
-    second_left, second_right, gates = lax.optimization_barrier((second_left, second_right, gates))
-    cot_second = second_left + second_right
+    expert_index = lax.axis_index("expert")
+    between = (expert_index > 0) & (expert_index < expert_size - 1)
+    flags = jnp.stack([expert_size > 0, between, expert_size > 0]).astype(jnp.int32)
+    second_left, second_right, expert_input, flags = lax.optimization_barrier(
+        (second_left, second_right, expert_input, flags))
     routing = jnp.stack([slots, (gates * kept_float).T], axis=0)
     routing = routing.reshape(2, expert_size, local, rows).transpose(1, 0, 2, 3)
     routing = routing.reshape(expert_size, 2 * local, rows)
     routing = jnp.pad(routing, ((0, 0), (0, 8 - 2 * local), (0, 0)))
     dn_parts, dw_parts, y_own, _, y_second, y_third, y_in, grads_low, _, _ = moe(
-        expert_input, upstream, cot_left, cot_right, cot_second, routing, gate_weight, up_weight,
+        expert_input, upstream, cot_left, cot_right, second_left, second_right, routing, gate_weight, up_weight,
         down_weight, cap,
     )
-    gate_dot = dw_parts[:, :local].reshape(expert_count, rows).T * kept_float
     y_far = (lax.ppermute(y_third, "expert", FAR), lax.ppermute(y_second, "expert", ACROSS))
     grads_shard = lax.psum_scatter(
         grads_low, ("dp", "context"), scatter_dimension=1, tiled=True
     )
 
-    expert_index = lax.axis_index("expert")
-    between = (expert_index > 0) & (expert_index < expert_size - 1)
-    flags = jnp.where(between, jnp.array([1, 1, 1], jnp.int32), jnp.array([1, 0, 1], jnp.int32))
     hidden_total, attn_grad_low, mixed_grad_low, misc = turn(
-        flags, dn_parts, gate_dot, gates, hidden, upstream, output_full, small
-    )
-    dq_low, dk_part, dv_part = attention_backward(
-        q, kv, mixed_grad_low, lse, cos_full, sin_full, spans, segk, segq
+        flags, dn_parts, dw_parts, kept_float, gates, hidden, upstream, output_full, small
     )
     if (lax.axis_size("dp"), context_size, expert_size) == (4, 2, 4):
         *sums, grad_tokens = tail(
-            mixed, attn_grad_low, attn_input, dq_low, dk_part, dv_part, cos_full, sin_full,
-            query_full, key_full, value_full, hidden_total, x, small[0:1], misc,
+            mixed, attn_grad_low, attn_input, q, kv, mixed_grad_low, lse, segk, segq,
+            cos_full, sin_full, query_full, key_full, value_full, hidden_total, x, small, misc,
         )
         late, grad_tokens = lax.optimization_barrier((hidden, grad_tokens))
-        (query_grad, key_grad, value_grad, output_grad, router_grad, gains, layer_out,
+        (query_grad, key_grad, value_grad, output_grad, router_grad, first, second, layer_out,
          *expert_sums) = finish(flags, *sums, y_own, y_in, y_far, late, grads_shard, expert_count)
-        sums = (query_grad, key_grad, value_grad, output_grad, router_grad, gains[0], gains[1])
+        sums = (query_grad, key_grad, value_grad, output_grad, router_grad.T, first[0], second[0])
     else:
+        dq_low, dk_part, dv_part = attention_backward(
+            q, kv, mixed_grad_low, lse, cos_full, sin_full, spans, segk, segq
+        )
         dkv = lax.psum_scatter(
             jnp.concatenate([dk_part, dv_part], axis=1), "context", scatter_dimension=0, tiled=True
         )

time: 535 us -> 524 us (0.979)
  local copies, waits for them, and re-layouts: 12.5 us -> 6.92 us
    pallas_call x2 -> x1, Pallas kernels: 38 us -> 17.9 us  [turn(): pl.pallas_call(functools.partial(turn_kernel, strip, local), out_shape=(s...]
    pallas_call x1, Pallas kernels: 157 us -> 173 us  [tail(): pl.pallas_call(tail_kernel, out_shape=(shape((half, width), BF), shape((h...]
  transfers between devices with their start and end apart: 8 -> 8, of which waited for: 3 -> 3; matrix products, arithmetic and copies ran while one was open for 3% -> 2% of each run, Pallas kernels for 44% -> 44%
where the time goes in v6:
time: 524 us; the launch traced here: 523 us
  Pallas kernels  456 us (87%)
  between operations  19.7 us (4%)
  waiting for transfers between devices  16.1 us (3%)
  starting transfers between devices  13.3 us (3%)
  other arithmetic  11.4 us (2%)
  local copies, waits for them, and re-layouts  6.92 us (1%)
    pallas_call x1, Pallas kernels, moe(): pl.pallas_call(functools.partial(moe_kernel, cap, tile, n), out_shape=(sh...  213 us
    pallas_call x1, Pallas kernels, tail(): pl.pallas_call(tail_kernel, out_shape=(shape((half, width), BF), shape((h...  173 us
    pallas_call x1, Pallas kernels, turn(): pl.pallas_call(functools.partial(turn_kernel, strip, local), out_shape=(s...  17.9 us
    pallas_call x1, Pallas kernels, project(): pl.pallas_call(project_kernel, out_shape=(shape((tokens, width), BF), sha...  14.5 us
    ppermute x1, waiting for transfers between devices, body(): second_right = lax.ppermute(cot_right, 'expert', LEFT_ON)  13.2 us
    pallas_call x1, Pallas kernels, finish(): pl.pallas_call(finish_kernel, out_shape=(shape((half, width), F32), shape...  12.7 us
    pallas_call x1, Pallas kernels, attention_forward(): pl.pallas_call(functools.partial(attn_fwd_kernel, kb, tq), out_shape=(jax...  12.2 us
    pallas_call x1, Pallas kernels, mix(): pl.pallas_call(functools.partial(mix_kernel, row_strip(tokens)), out_shap...  12.2 us
  transfers between devices with their start and end apart: 8, of which 3 were waited for; matrix products, arithmetic and copies ran while one was open for 2% of the time, Pallas kernels for 44%

profile of v6, /device:TPU:0, one launch (start us, length us, event | category | flops | bytes accessed | tf_op | source)
XLA Modules:
  0.0 522.9 jit_solution(13750394175311095757)
XLA Ops:
  7.2 0.0 copy-start.2
  7.2 0.0 copy-start.4
  7.2 0.0 copy-start.7
  7.2 0.0 copy-start.8
  7.2 0.0 copy-start.3
  7.2 0.0 all-gather.2.cloned.1.call-start
  7.3 0.7 all-gather.2.cloned.1.call-update
  8.0 0.0 reduce-scatter.2.cloned.1.call-start
  8.0 0.6 copy-done.2
  8.6 1.3 collective-permute-start.1
  9.9 6.7 %collective-permute-start = (bf16[512,1536]{1,0:T(8,128)(2,1)S(1)}, bf16[512,1536]{1,0:T(8,128)(2,1)}, u32[]{:S(2)}, u32[]{:S(2)}) collective-permute-start(bf16[512,1536]{1,0:T(8,128)(2,1)S(1)} %bitcast.35), channel_id=1, source_target_pairs={{0,1},{1,2},{2,3},{4,5},{5,6},{6,7},{8,9},{9,10},{10,11},{12,13},{... | collective-permute-start | bytes 4718600 | tf_op jit(solution)/shard_map/ppermute | solution.py:1382
  16.6 0.0 copy-done.4
  16.6 0.6 constant_dynamic-slice_fusion.2
  17.2 1.9 fusion.4
  24.4 0.0 copy-done.7
  24.5 0.2 copy.39
  24.6 0.5 broadcast.35
  25.1 0.7 reduce.7
  25.8 0.3 broadcast_in_dim.46
  26.1 0.1 copy.40
  26.2 0.1 copy.41
  26.4 0.0 copy-start.5
  26.4 0.1 copy.42
  26.5 1.0 convert_reduce_fusion
  27.5 0.1 copy.44
  27.6 0.1 pad.16.clone
  27.7 0.6 stack.38.meta
  28.3 0.6 constant_dynamic-slice_fusion.segq_ref
  28.9 1.0 fusion.1
  29.9 1.0 pad_maximum_fusion
  30.9 0.0 copy-done.5
  30.9 0.7 maximum_convert_fusion.small_own
  31.6 0.1 select_convert_fusion
  31.7 0.8 fusion.5
  32.4 14.5 %project.1 = (bf16[512,1536]{1,0:T(8,128)(2,1)}, bf16[512,1536]{1,0:T(8,128)(2,1)}, bf16[1024,512]{1,0:T(8,128)(2,1)}, bf16[1536,1536]{1,0:T(8,128)(2,1)}, bf16[...) custom-call(bf16[512,1536]{1,0:T(8,128)(2,1)} %bitcast.40, bf16[768,1536]{1,0:T(8,128)(2,1)} %wq_own.1, ...), custom_call_target="tpu_custom_call" | custom-call | flops 3221225472 | bytes 18874368 | tf_op jit(solution)/shard_map/project/pallas_call | solution.py:825
  46.9 1.1 collective-permute-done.1.cotr_hbm
  48.0 1.1 collective-permute-done.cotl_hbm
  49.1 0.7 collective-permute-start.2
  49.8 1.5 collective-permute-start.3
  51.3 0.6 add_convert_fusion.1.flags
  51.9 0.1 copy.49
  52.0 1.0 copy.48.segk_ref
  53.1 12.2 %attn_fwd.1 = (bf16[512,1536]{1,0:T(8,128)(2,1)}, f32[12,1,512]{2,1,0:T(1,128)}) custom-call(s32[5]{0:T(128)} %stack.38.meta, bf16[512,1536]{1,0:T(8,128)(2,1)} %get-tuple-element.73.q_ref, bf16[1024,512]{1,0:T(8,128)(2,1)} %get-tuple-element.74.k_ref.v_ref.kv_ref, bf16[1024,512]{1,0:T(8,128)(2,1)} %get-tuple-element.74.k_ref.v_ref.kv_ref, ...), custom_call_target="tpu_custom_call" | custom-call | flops 2415919104 | bytes 3145728 | tf_op jit(solution)/shard_map/attn_fwd/pallas_call | solution.py:217
  65.3 12.2 %mix.1 = (f32[512,1536]{1,0:T(8,128)}, bf16[512,1536]{1,0:T(8,128)(2,1)}, f32[512,8]{1,0:T(8,128)}) custom-call(bf16[512,1536]{1,0:T(8,128)(2,1)} %get-tuple-element.77.ob_ref, bf16[512,1536]{1,0:T(8,128)(2,1)} %bitcast.41, bf16[1536,1536]{1,0:T(8,128)(2,1)} %all-gather.2.cloned.1.call-done.wo_ref, f32[16,1536]{1,0:T(8,128)} %get-tuple-element.78.small_ref.gain_ref, ...), custom_call_target="tpu_custom_call" | custom-call | flops 2415919104 | bytes 9437184 | tf_op jit(solution)/shard_map/mix/pallas_call | solution.py:898
  77.5 0.0 collective-permute-done.2.cotl2_hbm
  77.5 0.0 copy-start.9
  77.5 13.2 %collective-permute-done.3.cotr2_hbm = bf16[512,1536]{1,0:T(8,128)(2,1)} collective-permute-done((bf16[512,1536]{1,0:T(8,128)(2,1)}, bf16[512,1536]{1,0:T(8,128)(2,1)}, u32[]{:S(2)}, u32[]{:S(2)}) %collective-permute-start.3) | collective-permute-done | bytes 1572896 | tf_op jit(solution)/shard_map/ppermute | solution.py:1436
  90.7 1.0 multiply_bitcast_fusion
  91.7 0.1 copy.50
  91.9 0.6 pad.4.meta_hbm
  92.5 212.7 %moe.1 = (bf16[3,512,1536]{2,1,0:T(8,128)(2,1)}, f32[4,8,512]{2,1,0:T(8,128)}, bf16[512,1536]{1,0:T(8,128)(2,1)}, bf16[2,512,1536]{2,1,0:T(8,128)(2,1)}, bf16[51...) custom-call(bf16[512,1536]{1,0:T(8,128)(2,1)} %get-tuple-element.82., ...), custom_call_target="tpu_custom_call" | custom-call | flops 74490839040 | bytes 78643200 | tf_op jit(solution)/shard_map/moe/pallas_call | solution.py:679
  305.2 0.0 reduce-scatter.2.cloned.1.call-update
  305.3 2.9 collective-permute-start.4
  308.2 0.1 collective-permute-start.5
  308.3 17.9 %turn.1 = (f32[512,1536]{1,0:T(8,128)}, bf16[512,1536]{1,0:T(8,128)(2,1)}, bf16[512,1536]{1,0:T(8,128)(2,1)}, f32[16,1536]{1,0:T(8,128)}) custom-call(s32[3]{0:T(128)} %add_convert_fusion.1.flags, bf16[3,512,1536]{2,1,0:T(8,128)(2,1)} %get-tuple-element.88.dn_ref, f32[4,8,512]{2,1,0:T(8,128)} %get-tuple-element.89.dw_ref, f32[512,8]{1,0:T(8,128)} %copy-done, ...), custom_call_target="tpu_custom_call" | custom-call | flops 2415919104 | bytes 18874368 | tf_op jit(solution)/shard_map/turn/pallas_call | solution.py:969
  326.2 173.3 %tail.1 = (bf16[768,1536]{1,0:T(8,128)(2,1)}, bf16[768,256]{1,0:T(8,128)(2,1)}, bf16[768,256]{1,0:T(8,128)(2,1)}, bf16[768,1536]{1,0:T(8,128)(2,1)}, bf16[768,12...) custom-call(bf16[512,1536]{1,0:T(8,128)(2,1)} %get-tuple-element.77.ob_ref, bf16[512,1536]{1,0:T(8,128)(2,1)} %get-tuple-element.91.da_ref, ...), custom_call_target="tpu_custom_call" | custom-call | flops 8858370048 | bytes 37748736 | tf_op jit(solution)/shard_map/tail/pallas_call | solution.py:1266
  499.5 0.0 collective-permute-done.4.y2_ref
  499.6 0.0 collective-permute-done.5.y3_ref
  499.6 0.0 reduce-scatter.2.cloned.1.call-done.shard_ref
  499.6 12.7 %finish.1 = (f32[768,1536]{1,0:T(8,128)}, f32[768,256]{1,0:T(8,128)}, f32[768,256]{1,0:T(8,128)}, f32[768,1536]{1,0:T(8,128)}, f32[8,768]{1,0:T(8,128)}, /*index...) custom-call(s32[3]{0:T(128)} %add_convert_fusion.1.flags, ...), custom_call_target="tpu_custom_call" | custom-call | bytes 18874368 | tf_op jit(solution)/shard_map/finish/pallas_call | solution.py:1338
  512.3 1.3 reduce.3
  513.6 1.3 reduce.4
  514.9 0.0 copy-done.1
  514.9 1.1 copy.54
  (22 shorter events, 0.2 us)
Async XLA Ops:
  7.2 1.4 copy-start.2
  7.2 9.4 %copy-start.4 = (s32[1,1024]{1,0:T(1,128)S(1)}, s32[1,1024]{1,0:T(1,128)}, u32[]{:S(2)}) copy-start(s32[1,1024]{1,0:T(1,128)} %param.17) | copy-start | bytes 12292
  7.2 17.2 %copy-start.7 = (bf16[768]{0:T(1024)(128)(2,1)S(1)}, bf16[768]{0:T(1024)(128)(2,1)}, u32[]{:S(2)}) copy-start(bf16[768]{0:T(1024)(128)(2,1)} %param.25) | copy-start | bytes 4612
  7.2 17.2 %copy-start.8 = (bf16[768]{0:T(1024)(128)(2,1)S(1)}, bf16[768]{0:T(1024)(128)(2,1)}, u32[]{:S(2)}) copy-start(bf16[768]{0:T(1024)(128)(2,1)} %param.26) | copy-start | bytes 4612
  7.2 17.2 %copy-start.3 = (s32[1,512,4]{1,2,0:T(4,128)S(1)}, s32[1,512,4]{1,2,0:T(4,128)}, u32[]{:S(2)}) copy-start(s32[1,512,4]{1,2,0:T(4,128)} %param.18) | copy-start | bytes 24580
  7.2 17.9 %copy-start.6 = (s32[1,1,2048]{2,1,0:T(1,128)S(1)}, s32[1,1,2048]{2,1,0:T(1,128)}, u32[]{:S(2)}) copy-start(s32[1,1,2048]{2,1,0:T(1,128)} %param.19) | copy-start | bytes 24580
  7.2 58.1 %all-gather.2.cloned.1.call-start = ((), (), s32[]{:S(2)}) async-start(), calls=%async_computation.1 | async-start | bytes 7077888 | tf_op jit(solution)/shard_map/all_gather | solution.py:1379
  8.0 491.6 %reduce-scatter.2.cloned.1.call-start = ((), (), s32[]{:S(2)}) async-start(), calls=%async_computation.2 | async-start | bytes 15925248 | tf_op jit(solution)/shard_map/reduce_scatter | solution.py:1454
  8.6 39.4 %collective-permute-start.1 = (bf16[512,1536]{1,0:T(8,128)(2,1)S(1)}, bf16[512,1536]{1,0:T(8,128)(2,1)}, u32[]{:S(2)}, u32[]{:S(2)}) collective-permute-start(bf16[512,1536]{1,0:T(8,128)(2,1)S(1)} %bitcast.34), channel_id=1, source_target_pairs={{1,0},{2,1},{3,2},{5,4},{6,5},{7,6},{9,8},{10,9},{11,10},{13,12},{... | collective-permute-start | bytes 4718600 | tf_op jit(solution)/shard_map/ppermute | solution.py:1383
  9.9 39.2 %collective-permute-start = (bf16[512,1536]{1,0:T(8,128)(2,1)S(1)}, bf16[512,1536]{1,0:T(8,128)(2,1)}, u32[]{:S(2)}, u32[]{:S(2)}) collective-permute-start(bf16[512,1536]{1,0:T(8,128)(2,1)S(1)} %bitcast.35), channel_id=1, source_target_pairs={{0,1},{1,2},{2,3},{4,5},{5,6},{6,7},{8,9},{9,10},{10,11},{12,13},{... | collective-permute-start | bytes 4718600 | tf_op jit(solution)/shard_map/ppermute | solution.py:1382
  26.4 4.6 copy-start.5
  32.4 58.3 %copy-start = (f32[512,8]{1,0:T(8,128)}, f32[512,8]{1,0:T(8,128)S(1)}, u32[]{:S(2)}) copy-start(f32[512,8]{1,0:T(8,128)S(1)} %get-tuple-element.87.kept_ref) | copy-start | bytes 49156
  49.1 28.4 %collective-permute-start.2 = (bf16[512,1536]{1,0:T(8,128)(2,1)}, bf16[512,1536]{1,0:T(8,128)(2,1)S(1)}, u32[]{:S(2)}, u32[]{:S(2)}) collective-permute-start(bf16[512,1536]{1,0:T(8,128)(2,1)} %collective-permute-done.cotl_hbm), channel_id=1, source_target_pairs={{1,2},{2,3},{5,6},{6,7},{9,10},{10,11},{13,14},{14,15},{17,18},{18... | collective-permute-start | bytes 4718600 | tf_op jit(solution)/shard_map/ppermute | solution.py:1435
  49.8 40.9 %collective-permute-start.3 = (bf16[512,1536]{1,0:T(8,128)(2,1)}, bf16[512,1536]{1,0:T(8,128)(2,1)}, u32[]{:S(2)}, u32[]{:S(2)}) collective-permute-start(bf16[512,1536]{1,0:T(8,128)(2,1)} %collective-permute-done.1.cotr_hbm), channel_id=1, source_target_pairs={{1,0},{2,1},{5,4},{6,5},{9,8},{10,9},{13,12},{14,13},{17,16},{18,1... | collective-permute-start | bytes 4718600 | tf_op jit(solution)/shard_map/ppermute | solution.py:1436
  77.5 13.2 %copy-start.9 = (bf16[512,1536]{1,0:T(8,128)(2,1)}, bf16[512,1536]{1,0:T(8,128)(2,1)S(1)}, u32[]{:S(2)}) copy-start(bf16[512,1536]{1,0:T(8,128)(2,1)S(1)} %collective-permute-done.2.cotl2_hbm) | copy-start | bytes 4718596
  305.3 194.3 %collective-permute-start.4 = (bf16[512,1536]{1,0:T(8,128)(2,1)}, bf16[512,1536]{1,0:T(8,128)(2,1)}, u32[]{:S(2)}, u32[]{:S(2)}) collective-permute-start(bf16[512,1536]{1,0:T(8,128)(2,1)} %get-tuple-element.107), channel_id=1, source_target_pairs={{0,3},{3,0},{4,7},{7,4},{8,11},{11,8},{12,15},{15,12},{16,19},{19,... | collective-permute-start | bytes 4718600 | tf_op jit(solution)/shard_map/ppermute | solution.py:1453
  308.2 191.4 %collective-permute-start.5 = (bf16[512,1536]{1,0:T(8,128)(2,1)}, bf16[512,1536]{1,0:T(8,128)(2,1)}, u32[]{:S(2)}, u32[]{:S(2)}) collective-permute-start(bf16[512,1536]{1,0:T(8,128)(2,1)} %get-tuple-element.108), channel_id=1, source_target_pairs={{0,2},{1,3},{2,0},{3,1},{4,6},{5,7},{6,4},{7,5},{8,10},{9,11},{10,... | collective-permute-start | bytes 4718600 | tf_op jit(solution)/shard_map/ppermute | solution.py:1453
  499.6 15.3 %copy-start.1 = (bf16[512,1536]{1,0:T(8,128)(2,1)S(1)}, bf16[512,1536]{1,0:T(8,128)(2,1)}, u32[]{:S(2)}) copy-start(bf16[512,1536]{1,0:T(8,128)(2,1)} %get-tuple-element.113) | copy-start | bytes 4718596
Sparse Core Ops, SparseCore 0:
  9.6 17.1 all-gather.1
  305.4 111.0 reduce-scatter.1

commit v7 on v6

--- a/solution.py
+++ b/solution.py
@@ -1139,64 +1139,68 @@
     reach = length // 2
     make_bias(ctx, tokens, segk_ref, segq_ref, bias_ref)
 
-    def attend(index):
-        step, piece = index // 2, index % 2
+    def attend(step):
         group, place = step * HEADS_AT_ONCE // GROUP, step * HEADS_AT_ONCE % GROUP
         k_at = slice(group * HEAD_SIZE, (group + 1) * HEAD_SIZE)
         v_at = slice(kv_width + group * HEAD_SIZE, kv_width + (group + 1) * HEAD_SIZE)
-        if place == 0 and piece == 0:
+        heads = [step * HEADS_AT_ONCE + h for h in range(HEADS_AT_ONCE)]
+        at = [slice(h * HEAD_SIZE, (h + 1) * HEAD_SIZE) for h in heads]
+        if place == 0:
             kt_ref[...] = kv_ref[:, k_at].astype(F32).T.astype(BF)
             dk_acc[...] = jnp.zeros_like(dk_acc)
             dv_acc[...] = jnp.zeros_like(dv_acc)
-        cols = pl.ds(piece * tq, tq)
-        high = ctx * 2 + piece + 1
-        low = jnp.maximum(high - 1 - reach // kb, 0)
-        heads = [step * HEADS_AT_ONCE + h for h in range(HEADS_AT_ONCE)]
-        at = [slice(h * HEAD_SIZE, (h + 1) * HEAD_SIZE) for h in heads]
-
-        def score(i, deltas):
-            rows = pl.ds(pl.multiple_of(i * kb, kb), kb)
-            key, value, bias = kv_ref[rows, k_at], kv_ref[rows, v_at], bias_ref[rows, cols]
-            out = []
+
+        def half_of_queries(piece, _):
+            cols = pl.ds(pl.multiple_of(piece * tq, tq), tq)
+            high = ctx * 2 + piece + 1
+            low = jnp.maximum(high - 1 - reach // kb, 0)
+
+            def score(i, deltas):
+                rows = pl.ds(pl.multiple_of(i * kb, kb), kb)
+                key, value, bias = kv_ref[rows, k_at], kv_ref[rows, v_at], bias_ref[rows, cols]
+                out = []
+                for h in range(HEADS_AT_ONCE):
+                    s = mm_nt(key, q_ref[cols, at[h]]) * SCALE + bias
+                    p = jnp.exp(s - lse_ref[heads[h], :, cols])
+                    dp = mm_nt(value, do_ref[cols, at[h]])
+                    p_ref[h, rows, :] = p
+                    dp_ref[h, rows, :] = dp
+                    out.append(deltas[h] + fold_rows(p * dp, jnp.sum))
+                return tuple(out)
+
+            deltas = lax.fori_loop(low, high, score, tuple(jnp.zeros((8, tq), F32) for _ in heads))
+            deltas = [jnp.sum(d, axis=0, keepdims=True) for d in deltas]
+
+            def grads(i, dqs):
+                rows = pl.ds(pl.multiple_of(i * kb, kb), kb)
+                kt = kt_ref[:, rows]
+                out, dk, dv = [], dk_acc[rows, :], dv_acc[rows, :]
+                for h in range(HEADS_AT_ONCE):
+                    p = p_ref[h, rows, :]
+                    ds = (p * (dp_ref[h, rows, :] - deltas[h])).astype(BF)
+                    dv = dv + mm(p.astype(BF), do_ref[cols, at[h]])
+                    dk = dk + mm(ds, q_ref[cols, at[h]])
+                    out.append(dqs[h] + mm(kt, ds))
+                dk_acc[rows, :] = dk
+                dv_acc[rows, :] = dv
+                return tuple(out)
+
+            dqs = lax.fori_loop(low, high, grads,
+                                tuple(jnp.zeros((HEAD_SIZE, tq), F32) for _ in heads))
             for h in range(HEADS_AT_ONCE):
-                s = mm_nt(key, q_ref[cols, at[h]]) * SCALE + bias
-                p = jnp.exp(s - lse_ref[heads[h], :, cols])
-                dp = mm_nt(value, do_ref[cols, at[h]])
-                p_ref[h, rows, :] = p
-                dp_ref[h, rows, :] = dp
-                out.append(deltas[h] + fold_rows(p * dp, jnp.sum))
-            return tuple(out)
-
-        deltas = lax.fori_loop(low, high, score, tuple(jnp.zeros((8, tq), F32) for _ in heads))
-        deltas = [jnp.sum(d, axis=0, keepdims=True) for d in deltas]
-
-        def grads(i, dqs):
-            rows = pl.ds(pl.multiple_of(i * kb, kb), kb)
-            kt = kt_ref[:, rows]
-            out, dk, dv = [], dk_acc[rows, :], dv_acc[rows, :]
-            for h in range(HEADS_AT_ONCE):
-                p = p_ref[h, rows, :]
-                ds = (p * (dp_ref[h, rows, :] - deltas[h])).astype(BF)
-                dv = dv + mm(p.astype(BF), do_ref[cols, at[h]])
-                dk = dk + mm(ds, q_ref[cols, at[h]])
-                out.append(dqs[h] + mm(kt, ds))
-            dk_acc[rows, :] = dk
-            dv_acc[rows, :] = dv
-            return tuple(out)
-
-        dqs = lax.fori_loop(low, high, grads,
-                            tuple(jnp.zeros((HEAD_SIZE, tq), F32) for _ in heads))
-        for h in range(HEADS_AT_ONCE):
-            dq = dqs[h].T * SCALE
-            turned = pltpu.roll(dq, HEAD_SIZE // 2, 1)
-            dq_ref[cols, at[h]] = (dq * cos_ref[cols, :] - turned * sin_ref[cols, :]).astype(BF)
-        if place == GROUP - HEADS_AT_ONCE and piece == 1:
+                dq = dqs[h].T * SCALE
+                turned = pltpu.roll(dq, HEAD_SIZE // 2, 1)
+                dq_ref[cols, at[h]] = (dq * cos_ref[cols, :] - turned * sin_ref[cols, :]).astype(BF)
+            return 0
+
+        lax.fori_loop(0, 2, half_of_queries, 0)
+        if place == GROUP - HEADS_AT_ONCE:
             dkp_ref[:, k_at] = (dk_acc[...] * SCALE).astype(BF)
             dvp_ref[:, k_at] = dv_acc[...].astype(BF)
 
     gain_rows = None
     misc_rows = misc_ref[...]
-    steps = 2 * QUERY_HEADS // HEADS_AT_ONCE
+    steps = QUERY_HEADS // HEADS_AT_ONCE
     begin = [0, 0, 0, 3, 3, 3, 3, 5]
     paces = begin[3]
     for t in range(begin[-1] + LINKS + 1):
@@ -1214,7 +1218,7 @@
             if 0 <= t - begin[c] <= LINKS:
                 do(c, t - begin[c])
         if t < paces:
-            for k in (range(2), range(2, 6), range(6, steps))[t]:
+            for k in (range(1), range(1, 3), range(3, steps))[t]:
                 attend(k)
         if t == paces - 1:
             for copy in kv_copies:
@@ -1299,17 +1303,14 @@
     )(ob, da, xa, q, kv, do, lse, segk, segq, cos, sin, wq, wk, wv, dh, x, gain, misc)
 
 
-def finish_kernel(flags, qg_ref, kg_ref, vg_ref, og_ref, misc_ref, y0_ref, y1_ref, y2_ref, y3_ref,
-                  hidden_ref, shard_ref,
+def finish_kernel(qg_ref, kg_ref, vg_ref, og_ref, misc_ref, y2_ref, y3_ref, hidden_ref, shard_ref,
                   q_out, k_out, v_out, o_out, router_out, first_out, second_out, layer_out,
                   gate_out, up_out, down_out):
     for src, dst in ((qg_ref, q_out), (kg_ref, k_out), (vg_ref, v_out), (og_ref, o_out)):
         dst[...] = src[...].astype(F32)
     out = hidden_ref[...]
-    for ref in (y0_ref, y2_ref, y3_ref):
+    for ref in (y2_ref, y3_ref):
         out = out + ref[...].astype(F32)
-    out = out + y1_ref[0].astype(F32)
-    out = out + jnp.where(flags[1] > 0, y1_ref[1].astype(F32), 0.0)
     layer_out[...] = out.astype(BF)
     hidden = gate_out.shape[2]
     for k, dst in enumerate((gate_out, up_out, down_out)):
@@ -1324,7 +1325,7 @@
         second_out[...] = jnp.sum(rows[8:16, :], axis=0, keepdims=True)
 
 
-def finish(flags, qg, kg, vg, og, misc, y_own, y_in, y_far, hidden, shard, experts):
+def finish(qg, kg, vg, og, misc, y_far, hidden, shard, experts):
     half, width = qg.shape
     kv_width = kg.shape[1]
     tokens = hidden.shape[0]
@@ -1332,9 +1333,9 @@
     ff = three // 3
     grid = 4
     shape = jax.ShapeDtypeStruct
-    cut = lambda r, d: pl.BlockSpec((r // grid, d), lambda i, f: (i, 0))
-    const = lambda r, d: pl.BlockSpec((r, d), lambda i, f: (0, 0))
-    grads = lambda d: pl.BlockSpec((local, rows // grid, d), lambda i, f: (0, i, 0))
+    cut = lambda r, d: pl.BlockSpec((r // grid, d), lambda i: (i, 0))
+    const = lambda r, d: pl.BlockSpec((r, d), lambda i: (0, 0))
+    grads = lambda d: pl.BlockSpec((local, rows // grid, d), lambda i: (0, i, 0))
     return pl.pallas_call(
         finish_kernel,
         out_shape=(
@@ -1344,13 +1345,10 @@
             shape((tokens, width), BF), shape((local, rows, ff), F32),
             shape((local, rows, ff), F32), shape((local, rows, ff), F32),
         ),
-        grid_spec=pltpu.PrefetchScalarGridSpec(
-            num_scalar_prefetch=1,
             grid=(grid,),
             in_specs=[
                 cut(half, width), cut(half, kv_width), cut(half, kv_width), cut(half, width),
-                const(half, 128), cut(tokens, width),
-                pl.BlockSpec((2, tokens // grid, width), lambda i, f: (0, i, 0)),
+                const(half, 128),
                 cut(tokens, width), cut(tokens, width), cut(tokens, width), grads(three),
             ],
             out_specs=[
@@ -1358,11 +1356,10 @@
                 const(experts, half), const(1, half), const(1, half), cut(tokens, width), grads(ff), grads(ff),
                 grads(ff),
             ],
-        ),
         compiler_params=pltpu.CompilerParams(vmem_limit_bytes=VMEM_LIMIT),
         cost_estimate=pl.CostEstimate(flops=0, transcendentals=0, bytes_accessed=16 * half * width),
         name="finish",
-    )(flags, qg, kg, vg, og, misc, y_own, y_in, *y_far, hidden, shard)
+    )(qg, kg, vg, og, misc, *y_far, hidden, shard)
 
 
 def body(
@@ -1459,13 +1456,16 @@
         flags, dn_parts, dw_parts, kept_float, gates, hidden, upstream, output_full, small
     )
     if (lax.axis_size("dp"), context_size, expert_size) == (4, 2, 4):
+        near = hidden + y_own.astype(F32) + y_in[0].astype(F32)
+        near = near + jnp.where(between, y_in[1].astype(F32), 0.0)
+        near, mixed_grad_low = lax.optimization_barrier((near, mixed_grad_low))
         *sums, grad_tokens = tail(
             mixed, attn_grad_low, attn_input, q, kv, mixed_grad_low, lse, segk, segq,
             cos_full, sin_full, query_full, key_full, value_full, hidden_total, x, small, misc,
         )
-        late, grad_tokens = lax.optimization_barrier((hidden, grad_tokens))
+        late, grad_tokens = lax.optimization_barrier((near, grad_tokens))
         (query_grad, key_grad, value_grad, output_grad, router_grad, first, second, layer_out,
-         *expert_sums) = finish(flags, *sums, y_own, y_in, y_far, late, grads_shard, expert_count)
+         *expert_sums) = finish(*sums, y_far, late, grads_shard, expert_count)
         sums = (query_grad, key_grad, value_grad, output_grad, router_grad.T, first[0], second[0])
     else:
         dq_low, dk_part, dv_part = attention_backward(

time: 524 us -> 521 us (level)
  Pallas kernels: 456 us -> 448 us
    pallas_call x1, Pallas kernels: 173 us -> 167 us  [tail(): pl.pallas_call(tail_kernel, out_shape=(shape((half, width), BF), shape((h...]
  transfers between devices with their start and end apart: 8 -> 8, of which waited for: 3 -> 3; matrix products, arithmetic and copies ran while one was open for 2% -> 3% of each run, Pallas kernels for 44% -> 43%
where the time goes in v7:
time: 521 us
  Pallas kernels  448 us (86%)
  between operations  19.7 us (4%)
  other arithmetic  16.2 us (3%)
  waiting for transfers between devices  16 us (3%)
  starting transfers between devices  13.3 us (3%)
  local copies, waits for them, and re-layouts  6.91 us (1%)
    pallas_call x1, Pallas kernels, moe(): pl.pallas_call(functools.partial(moe_kernel, cap, tile, n), out_shape=(sh...  213 us
    pallas_call x1, Pallas kernels, tail(): pl.pallas_call(tail_kernel, out_shape=(shape((half, width), BF), shape((h...  167 us
    pallas_call x1, Pallas kernels, turn(): pl.pallas_call(functools.partial(turn_kernel, strip, local), out_shape=(s...  18.9 us
    pallas_call x1, Pallas kernels, project(): pl.pallas_call(project_kernel, out_shape=(shape((tokens, width), BF), sha...  14.5 us
    ppermute x1, waiting for transfers between devices, body(): second_right = lax.ppermute(cot_right, 'expert', LEFT_ON)  13.2 us
    pallas_call x1, Pallas kernels, attention_forward(): pl.pallas_call(functools.partial(attn_fwd_kernel, kb, tq), out_shape=(jax...  12.2 us
    pallas_call x1, Pallas kernels, mix(): pl.pallas_call(functools.partial(mix_kernel, row_strip(tokens)), out_shap...  12.2 us
    pallas_call x1, Pallas kernels, finish(): pl.pallas_call(finish_kernel, out_shape=(shape((half, width), F32), shape...  10.6 us
  transfers between devices with their start and end apart: 8, of which 3 were waited for; matrix products, arithmetic and copies ran while one was open for 3% of the time, Pallas kernels for 43%

profile of v7, /device:TPU:0, one launch (start us, length us, event | category | flops | bytes accessed | tf_op | source)
XLA Modules:
  0.0 520.5 jit_solution(16822031506670363704)
XLA Ops:
  7.2 0.0 copy-start.3
  7.2 0.0 copy-start.5
  7.2 0.0 copy-start.8
  7.2 0.0 copy-start.9
  7.2 0.0 copy-start.4
  7.2 0.0 all-gather.2.cloned.1.call-start
  7.3 0.7 all-gather.2.cloned.1.call-update
  8.0 0.0 reduce-scatter.2.cloned.1.call-start
  8.0 0.6 copy-done.3
  8.6 1.3 collective-permute-start.1
  9.9 6.7 %collective-permute-start = (bf16[512,1536]{1,0:T(8,128)(2,1)S(1)}, bf16[512,1536]{1,0:T(8,128)(2,1)}, u32[]{:S(2)}, u32[]{:S(2)}) collective-permute-start(bf16[512,1536]{1,0:T(8,128)(2,1)S(1)} %bitcast.40), channel_id=1, source_target_pairs={{0,1},{1,2},{2,3},{4,5},{5,6},{6,7},{8,9},{9,10},{10,11},{12,13},{... | collective-permute-start | bytes 4718600 | tf_op jit(solution)/shard_map/ppermute | solution.py:1379
  16.6 0.0 copy-done.5
  16.6 0.6 constant_dynamic-slice_fusion.2
  17.2 1.9 fusion.5
  24.4 0.0 copy-done.8
  24.5 0.2 copy.39
  24.7 0.5 broadcast.39
  25.2 0.7 reduce.7
  25.8 0.3 broadcast_in_dim.50
  26.1 0.1 copy.40
  26.2 0.1 copy.41
  26.4 0.1 copy.42
  26.5 1.0 convert_reduce_fusion
  27.5 0.1 copy.44
  27.7 0.1 pad.16.clone
  27.7 0.6 stack.38.meta
  28.3 0.6 constant_dynamic-slice_fusion.segq_ref
  28.9 1.0 fusion.2
  29.9 1.0 pad_maximum_fusion
  30.9 0.0 copy-done.6
  30.9 0.7 maximum_convert_fusion.small_own
  31.6 0.1 select_convert_fusion
  31.7 0.8 fusion.6
  32.5 14.5 %project.1 = (bf16[512,1536]{1,0:T(8,128)(2,1)}, bf16[512,1536]{1,0:T(8,128)(2,1)}, bf16[1024,512]{1,0:T(8,128)(2,1)}, bf16[1536,1536]{1,0:T(8,128)(2,1)}, bf16[...) custom-call(bf16[512,1536]{1,0:T(8,128)(2,1)} %bitcast.45, bf16[768,1536]{1,0:T(8,128)(2,1)} %wq_own.1, ...), custom_call_target="tpu_custom_call" | custom-call | flops 3221225472 | bytes 18874368 | tf_op jit(solution)/shard_map/project/pallas_call | solution.py:825
  46.9 1.1 collective-permute-done.1.cotr_hbm
  48.0 1.1 collective-permute-done.cotl_hbm
  49.1 0.7 collective-permute-start.2
  49.8 1.5 collective-permute-start.3
  51.3 0.6 add_convert_fusion.1.flags
  51.9 0.1 copy.49
  52.1 1.0 copy.48.segk_ref
  53.1 12.2 %attn_fwd.1 = (bf16[512,1536]{1,0:T(8,128)(2,1)}, f32[12,1,512]{2,1,0:T(1,128)}) custom-call(s32[5]{0:T(128)} %stack.38.meta, bf16[512,1536]{1,0:T(8,128)(2,1)} %get-tuple-element.73.q_ref, bf16[1024,512]{1,0:T(8,128)(2,1)} %get-tuple-element.74.k_ref.v_ref.kv_ref, bf16[1024,512]{1,0:T(8,128)(2,1)} %get-tuple-element.74.k_ref.v_ref.kv_ref, ...), custom_call_target="tpu_custom_call" | custom-call | flops 2415919104 | bytes 3145728 | tf_op jit(solution)/shard_map/attn_fwd/pallas_call | solution.py:217
  65.3 12.2 %mix.1 = (f32[512,1536]{1,0:T(8,128)}, bf16[512,1536]{1,0:T(8,128)(2,1)}, f32[512,8]{1,0:T(8,128)}) custom-call(bf16[512,1536]{1,0:T(8,128)(2,1)} %get-tuple-element.77.ob_ref, bf16[512,1536]{1,0:T(8,128)(2,1)} %bitcast.46, bf16[1536,1536]{1,0:T(8,128)(2,1)} %all-gather.2.cloned.1.call-done.wo_ref, f32[16,1536]{1,0:T(8,128)} %get-tuple-element.80.small_ref.gain_ref, ...), custom_call_target="tpu_custom_call" | custom-call | flops 2415919104 | bytes 9437184 | tf_op jit(solution)/shard_map/mix/pallas_call | solution.py:898
  77.5 0.0 collective-permute-done.2.cotl2_hbm
  77.5 13.2 %collective-permute-done.3.cotr2_hbm = bf16[512,1536]{1,0:T(8,128)(2,1)} collective-permute-done((bf16[512,1536]{1,0:T(8,128)(2,1)}, bf16[512,1536]{1,0:T(8,128)(2,1)}, u32[]{:S(2)}, u32[]{:S(2)}) %collective-permute-start.3) | collective-permute-done | bytes 1572896 | tf_op jit(solution)/shard_map/ppermute | solution.py:1433
  90.7 0.0 copy-done.1
  90.7 1.0 multiply_bitcast_fusion
  91.7 0.1 copy.50
  91.9 0.6 pad.4.meta_hbm
  92.5 212.7 %moe.1 = (bf16[3,512,1536]{2,1,0:T(8,128)(2,1)}, f32[4,8,512]{2,1,0:T(8,128)}, bf16[512,1536]{1,0:T(8,128)(2,1)}, bf16[2,512,1536]{2,1,0:T(8,128)(2,1)}, bf16[51...) custom-call(bf16[512,1536]{1,0:T(8,128)(2,1)} %get-tuple-element.84., ...), custom_call_target="tpu_custom_call" | custom-call | flops 74490839040 | bytes 78643200 | tf_op jit(solution)/shard_map/moe/pallas_call | solution.py:679
  305.2 0.0 reduce-scatter.2.cloned.1.call-update
  305.2 2.9 collective-permute-start.4
  308.2 0.1 collective-permute-start.5
  308.3 0.0 copy-start
  308.3 18.9 %turn.1 = (f32[512,1536]{1,0:T(8,128)}, bf16[512,1536]{1,0:T(8,128)(2,1)}, bf16[512,1536]{1,0:T(8,128)(2,1)}, f32[16,1536]{1,0:T(8,128)}) custom-call(s32[3]{0:T(128)} %add_convert_fusion.1.flags, bf16[3,512,1536]{2,1,0:T(8,128)(2,1)} %get-tuple-element.90.dn_ref, f32[4,8,512]{2,1,0:T(8,128)} %get-tuple-element.91.dw_ref, f32[512,8]{1,0:T(8,128)} %copy-done.1, ...), custom_call_target="tpu_custom_call" | custom-call | flops 2415919104 | bytes 18874368 | tf_op jit(solution)/shard_map/turn/pallas_call | solution.py:969
  327.2 4.8 fusion.hidden_ref
  332.0 167.2 %tail.1 = (bf16[768,1536]{1,0:T(8,128)(2,1)}, bf16[768,256]{1,0:T(8,128)(2,1)}, bf16[768,256]{1,0:T(8,128)(2,1)}, bf16[768,1536]{1,0:T(8,128)(2,1)}, bf16[768,12...) custom-call(bf16[512,1536]{1,0:T(8,128)(2,1)} %get-tuple-element.77.ob_ref, bf16[512,1536]{1,0:T(8,128)(2,1)} %get-tuple-element.93.da_ref, ...), custom_call_target="tpu_custom_call" | custom-call | flops 8858370048 | bytes 37748736 | tf_op jit(solution)/shard_map/tail/pallas_call | solution.py:1270
  499.2 0.0 collective-permute-done.4.y2_ref
  499.2 0.0 collective-permute-done.5.y3_ref
  499.3 0.0 reduce-scatter.2.cloned.1.call-done.shard_ref
  499.3 10.6 %finish.1 = (f32[768,1536]{1,0:T(8,128)}, f32[768,256]{1,0:T(8,128)}, f32[768,256]{1,0:T(8,128)}, f32[768,1536]{1,0:T(8,128)}, f32[8,768]{1,0:T(8,128)}, /*index...) custom-call(bf16[768,1536]{1,0:T(8,128)(2,1)} %get-tuple-element.105, ...), custom_call_target="tpu_custom_call" | custom-call | bytes 18874368 | tf_op jit(solution)/shard_map/finish/pallas_call | solution.py:1339
  509.9 1.3 reduce.3
  511.2 1.3 reduce.4
  512.5 1.1 copy.54
  (25 shorter events, 0.2 us)
Async XLA Ops:
  7.2 1.4 copy-start.3
  7.2 9.4 %copy-start.5 = (s32[1,1024]{1,0:T(1,128)S(1)}, s32[1,1024]{1,0:T(1,128)}, u32[]{:S(2)}) copy-start(s32[1,1024]{1,0:T(1,128)} %param.17) | copy-start | bytes 12292
  7.2 17.2 %copy-start.8 = (bf16[768]{0:T(1024)(128)(2,1)S(1)}, bf16[768]{0:T(1024)(128)(2,1)}, u32[]{:S(2)}) copy-start(bf16[768]{0:T(1024)(128)(2,1)} %param.25) | copy-start | bytes 4612
  7.2 17.2 %copy-start.9 = (bf16[768]{0:T(1024)(128)(2,1)S(1)}, bf16[768]{0:T(1024)(128)(2,1)}, u32[]{:S(2)}) copy-start(bf16[768]{0:T(1024)(128)(2,1)} %param.26) | copy-start | bytes 4612
  7.2 17.2 %copy-start.4 = (s32[1,512,4]{1,2,0:T(4,128)S(1)}, s32[1,512,4]{1,2,0:T(4,128)}, u32[]{:S(2)}) copy-start(s32[1,512,4]{1,2,0:T(4,128)} %param.18) | copy-start | bytes 24580
  7.2 17.9 %copy-start.7 = (s32[1,1,2048]{2,1,0:T(1,128)S(1)}, s32[1,1,2048]{2,1,0:T(1,128)}, u32[]{:S(2)}) copy-start(s32[1,1,2048]{2,1,0:T(1,128)} %param.19) | copy-start | bytes 24580
  7.2 58.1 %all-gather.2.cloned.1.call-start = ((), (), s32[]{:S(2)}) async-start(), calls=%async_computation.1 | async-start | bytes 7077888 | tf_op jit(solution)/shard_map/all_gather | solution.py:1376
  8.0 23.0 %copy-start.6 = (bf16[768,8]{0,1:T(8,128)(2,1)S(1)}, bf16[768,8]{0,1:T(8,128)(2,1)}, u32[]{:S(2)}) copy-start(bf16[768,8]{0,1:T(8,128)(2,1)} %param.24) | copy-start | bytes 36868
  8.0 491.3 %reduce-scatter.2.cloned.1.call-start = ((), (), s32[]{:S(2)}) async-start(), calls=%async_computation.2 | async-start | bytes 15925248 | tf_op jit(solution)/shard_map/reduce_scatter | solution.py:1451
  8.6 39.4 %collective-permute-start.1 = (bf16[512,1536]{1,0:T(8,128)(2,1)S(1)}, bf16[512,1536]{1,0:T(8,128)(2,1)}, u32[]{:S(2)}, u32[]{:S(2)}) collective-permute-start(bf16[512,1536]{1,0:T(8,128)(2,1)S(1)} %bitcast.39), channel_id=1, source_target_pairs={{1,0},{2,1},{3,2},{5,4},{6,5},{7,6},{9,8},{10,9},{11,10},{13,12},{... | collective-permute-start | bytes 4718600 | tf_op jit(solution)/shard_map/ppermute | solution.py:1380
  9.9 39.2 %collective-permute-start = (bf16[512,1536]{1,0:T(8,128)(2,1)S(1)}, bf16[512,1536]{1,0:T(8,128)(2,1)}, u32[]{:S(2)}, u32[]{:S(2)}) collective-permute-start(bf16[512,1536]{1,0:T(8,128)(2,1)S(1)} %bitcast.40), channel_id=1, source_target_pairs={{0,1},{1,2},{2,3},{4,5},{5,6},{6,7},{8,9},{9,10},{10,11},{12,13},{... | collective-permute-start | bytes 4718600 | tf_op jit(solution)/shard_map/ppermute | solution.py:1379
  32.5 58.2 %copy-start.1 = (f32[512,8]{1,0:T(8,128)}, f32[512,8]{1,0:T(8,128)S(1)}, u32[]{:S(2)}) copy-start(f32[512,8]{1,0:T(8,128)S(1)} %get-tuple-element.89.kept_ref) | copy-start | bytes 49156
  49.1 28.4 %collective-permute-start.2 = (bf16[512,1536]{1,0:T(8,128)(2,1)}, bf16[512,1536]{1,0:T(8,128)(2,1)S(1)}, u32[]{:S(2)}, u32[]{:S(2)}) collective-permute-start(bf16[512,1536]{1,0:T(8,128)(2,1)} %collective-permute-done.cotl_hbm), channel_id=1, source_target_pairs={{1,2},{2,3},{5,6},{6,7},{9,10},{10,11},{13,14},{14,15},{17,18},{18... | collective-permute-start | bytes 4718600 | tf_op jit(solution)/shard_map/ppermute | solution.py:1432
  49.8 40.8 %collective-permute-start.3 = (bf16[512,1536]{1,0:T(8,128)(2,1)}, bf16[512,1536]{1,0:T(8,128)(2,1)}, u32[]{:S(2)}, u32[]{:S(2)}) collective-permute-start(bf16[512,1536]{1,0:T(8,128)(2,1)} %collective-permute-done.1.cotr_hbm), channel_id=1, source_target_pairs={{1,0},{2,1},{5,4},{6,5},{9,8},{10,9},{13,12},{14,13},{17,16},{18,1... | collective-permute-start | bytes 4718600 | tf_op jit(solution)/shard_map/ppermute | solution.py:1433
  77.5 13.2 %copy-start.10 = (bf16[512,1536]{1,0:T(8,128)(2,1)}, bf16[512,1536]{1,0:T(8,128)(2,1)S(1)}, u32[]{:S(2)}) copy-start(bf16[512,1536]{1,0:T(8,128)(2,1)S(1)} %collective-permute-done.2.cotl2_hbm) | copy-start | bytes 4718596
  305.2 194.0 %collective-permute-start.4 = (bf16[512,1536]{1,0:T(8,128)(2,1)}, bf16[512,1536]{1,0:T(8,128)(2,1)}, u32[]{:S(2)}, u32[]{:S(2)}) collective-permute-start(bf16[512,1536]{1,0:T(8,128)(2,1)} %get-tuple-element.110), channel_id=1, source_target_pairs={{0,3},{3,0},{4,7},{7,4},{8,11},{11,8},{12,15},{15,12},{16,19},{19,... | collective-permute-start | bytes 4718600 | tf_op jit(solution)/shard_map/ppermute | solution.py:1450
  308.2 191.1 %collective-permute-start.5 = (bf16[512,1536]{1,0:T(8,128)(2,1)}, bf16[512,1536]{1,0:T(8,128)(2,1)}, u32[]{:S(2)}, u32[]{:S(2)}) collective-permute-start(bf16[512,1536]{1,0:T(8,128)(2,1)} %get-tuple-element.111), channel_id=1, source_target_pairs={{0,2},{1,3},{2,0},{3,1},{4,6},{5,7},{6,4},{7,5},{8,10},{9,11},{10,... | collective-permute-start | bytes 4718600 | tf_op jit(solution)/shard_map/ppermute | solution.py:1450
  308.3 19.0 %copy-start = (f32[512,1536]{1,0:T(8,128)S(1)}, f32[512,1536]{1,0:T(8,128)}, u32[]{:S(2)}) copy-start(f32[512,1536]{1,0:T(8,128)} %get-tuple-element.92.hidden_ref) | copy-start | bytes 9437188
  499.3 13.2 %copy-start.2 = (bf16[512,1536]{1,0:T(8,128)(2,1)S(1)}, bf16[512,1536]{1,0:T(8,128)(2,1)}, u32[]{:S(2)}) copy-start(bf16[512,1536]{1,0:T(8,128)(2,1)} %get-tuple-element.117) | copy-start | bytes 4718596
Sparse Core Ops, SparseCore 0:
  9.6 17.1 all-gather.1
  305.4 111.0 reduce-scatter.1
